TPU v7x, 32 devices: a whole 2x2x4 slice. The times are simulated.
32 devices in a mesh: kvh: 2 (over x), ctx: 16 (over z, y, core).
Axes of the slice: x: 2, y: 2, z: 4, core: 2. Of those that a mesh axis runs over, the one named last changes fastest.
Arguments:
- queries: bfloat16 [512, 32, 128], P('ctx', 'kvh'), parts along dimension 1, may hold values from -6 to 6
- cache_keys: bfloat16 [16384, 256], P('ctx', 'kvh'), parts along dimension 1, may hold values from -6 to 6
- cache_values: bfloat16 [16384, 256], P('ctx', 'kvh'), parts along dimension 1, may hold values from -6 to 6
- span_offset: int32 [1], replicated, may hold values from 0 to 8191
- positions: int32 [512], replicated, may hold values from 0 to 8191
Outputs:
- attended: bfloat16 [512, 32, 128], P('ctx', 'kvh'), parts along dimension 1
There are 2 independent parts, one for each index of `kvh`. A program takes and returns all parts, laid end to end along the dimension named above; an argument that names none is the same for every part. Nothing has to cross between parts.
All inputs are finite; a program needn't handle non-finite values.
Results may differ from a plain program's by a relative error of at most 0.0029.
Values may be sent and summed in bfloat16 or wider, within the bound.
No kernel may reach another device: no remote copies, remote signals or barrier semaphores. Data moves between devices by JAX's collectives and lax.ppermute only.
A program may use at most 64 MiB of HBM per device.

v0:
```python
import functools

import jax
import jax.numpy as jnp
from jax import lax
from jax.experimental import pallas as pl
from jax.experimental.pallas import tpu as pltpu
from jax.sharding import PartitionSpec as P


masked_floor = -1e30
log2_e = 1.4426950408889634
inner = 4
extra_rows = 16
tail_rows = 8
code_span = 240.0
code_low = -120.0


def attend_tiles(scale, query, keys, values, limits, states, scores_ref, weights_ref, values_ref):
    rows, width = query.shape
    shard_keys = keys[0].shape[0]
    tile = scores_ref.shape[2]
    chunk = min(512, shard_keys)
    chunks = shard_keys // chunk
    scaled = query.astype(jnp.float32) * scale
    high = scaled.astype(jnp.bfloat16)
    low = (scaled - high.astype(jnp.float32)).astype(jnp.bfloat16)
    query_pair = jnp.concatenate([high, low], axis=1)
    for b, value in enumerate(values):
        values_ref[b, :width, :] = value[...].T
        values_ref[b, width:, :] = jnp.ones((extra_rows, shard_keys), jnp.bfloat16)
    sublane = lax.broadcasted_iota(jnp.int32, (8, tile), 0)
    tiles = [(b, h) for b in range(len(keys)) for h in range(rows // tile)]
    count = len(tiles)
    running, tops = [None] * count, [None] * count
    states = list(states)
    for step in range(count + 2):
        for c in range(chunks):
            span = slice(c * chunk, (c + 1) * chunk)
            if step < count:
                b, h = tiles[step]
                lanes = slice(h * tile, (h + 1) * tile)
                key = keys[b][span, :]
                scores = lax.dot_general(
                    jnp.concatenate([key, key], axis=1),
                    query_pair[lanes],
                    (((1,), (1,)), ((), ())),
                    preferred_element_type=jnp.float32,
                ).reshape(chunk // 8, 8, tile)
                position = lax.broadcasted_iota(jnp.int32, scores.shape, 0) * 8 + c * chunk
                scores = jnp.where(position <= (limits[b][:, lanes] - sublane)[None], scores, masked_floor)
                peak = jnp.max(scores, axis=0)
                running[step] = peak if c == 0 else jnp.maximum(running[step], peak)
                scores_ref[step % 2, span, :] = scores.reshape(chunk, tile)
            if 1 <= step <= count:
                t = step - 1
                if c == 0:
                    tops[t] = jnp.max(running[t], axis=0, keepdims=True)
                weights_ref[t % 2, span, :] = jnp.exp2(scores_ref[t % 2, span, :] - tops[t]).astype(jnp.bfloat16)
            if step >= 2 and c == min(1, chunks - 1):
                b, h = tiles[step - 2]
                shard_max = tops[step - 2]
                sums = lax.dot_general(
                    values_ref[b],
                    weights_ref[step % 2],
                    (((1,), (0,)), ((), ())),
                    preferred_element_type=jnp.float32,
                )
                num, den = sums[:width], sums[width : width + 1]
                if states[h] is None:
                    states[h] = (shard_max, den, num)
                else:
                    top, run_den, run_num = states[h]
                    new_top = jnp.maximum(top, shard_max)
                    keep, fresh = jnp.exp2(top - new_top), jnp.exp2(shard_max - new_top)
                    states[h] = (new_top, run_den * keep + den * fresh, run_num * keep + num * fresh)
    return states


def encode(values, level):
    _, lanes = values.shape
    size = jnp.abs(values)
    peak = jnp.maximum(jnp.max(size, axis=0, keepdims=True), 1e-30).astype(jnp.bfloat16).astype(jnp.float32)
    code = jnp.exp2(size * (code_span / peak) + code_low)
    code = jnp.where(values < 0, -code, code)
    high = level.astype(jnp.bfloat16).astype(jnp.float32)
    rest = level - high
    middle = rest.astype(jnp.bfloat16).astype(jnp.float32)
    row = lax.broadcasted_iota(jnp.int32, (tail_rows, lanes), 0)
    tail = jnp.where(row == 0, high, jnp.where(row == 1, middle, jnp.where(row == 2, rest - middle, peak)))
    return code.astype(jnp.bfloat16), tail.astype(jnp.bfloat16)


def decode(codes, tail):
    codes, tail = codes.astype(jnp.float32), tail.astype(jnp.float32)
    level = tail[0:1] + tail[1:2] + tail[2:3]
    size = (jnp.log2(jnp.abs(codes)) - code_low) * (tail[3:4] * (1.0 / code_span))
    return jnp.where(codes < 0, -size, size), level


def spread_limits(me, own_tokens, head_count, offsets_ref, span_ref, limits_ref):
    count, lanes = limits_ref.shape
    width = offsets_ref.shape[1]
    per_row = width // own_tokens
    parts = []
    for k in range(count):
        device = me ^ (k * inner)
        row = offsets_ref[pl.ds(device // per_row, 1), :]
        row = pltpu.roll(row, (width - (device % per_row) * own_tokens) % width, 1)
        parts += [row >> 8, row & 255]
    parts = jnp.concatenate(parts, axis=0).astype(jnp.float32).astype(jnp.bfloat16)
    token = lax.broadcasted_iota(jnp.int32, (width, lanes), 0)
    lane = lax.broadcasted_iota(jnp.int32, (width, lanes), 1)
    first = token * head_count
    spread = jnp.where((lane >= first) & (lane < first + head_count), 1.0, 0.0).astype(jnp.bfloat16)
    wide = lax.dot_general(parts, spread, (((1,), (0,)), ((), ())), preferred_element_type=jnp.float32)
    wide = wide.astype(jnp.int32)
    for k in range(count):
        limits_ref[k : k + 1, :] = wide[2 * k : 2 * k + 1] * 256 + wide[2 * k + 1 : 2 * k + 2] + span_ref[...]


def attend_kernel(scale, index, blocks, has_state, form, own_rows, setup, *refs):
    me = lax.axis_index("ctx")
    refs = list(refs)
    if setup:
        offsets_ref, span_ref, q_hbm, k_hbm, v_hbm = refs[:5]
        arrived, q_ref = refs.pop(), refs.pop()
        scratch = [refs.pop() for _ in range(3)][::-1]
        v_ref, k_ref, limits_ref = refs.pop(), refs.pop(), refs.pop()
        pairs = ((q_hbm, q_ref), (k_hbm, k_ref), (v_hbm, v_ref))
        copies = [pltpu.make_async_copy(*pair, arrived.at[at]) for at, pair in enumerate(pairs)]
        for copy in copies:
            copy.start()
        spread_limits(me, *setup, offsets_ref, span_ref, limits_ref)
        for copy in copies:
            copy.wait()
        refs = [limits_ref, q_ref, k_ref, v_ref] + refs[5:]
    else:
        scratch = [refs.pop() for _ in range(3)][::-1]
        limits_ref, q_ref = refs[:2]
    keys = refs[2 : 2 + 2 * len(blocks) : 2]
    values = refs[3 : 3 + 2 * len(blocks) : 2]
    rest = list(refs[2 + 2 * len(blocks) :])
    rows, width = q_ref.shape
    tile = scratch[0].shape[2]
    spans = [slice(at, at + tile) for at in range(0, rows, tile)]
    states = [None] * len(spans)
    if has_state:
        states = [tuple(ref[:, span] for ref in rest[:3]) for span in spans]
        rest = rest[3:]
    limits = [limits_ref[index : index + 1, :] - (me ^ b) * keys[0].shape[0] for b in blocks]
    states = attend_tiles(scale, q_ref[...], keys, values, limits, states, *scratch)
    for span, state in zip(spans, states):
        if form == "state":
            for ref, value in zip(rest, state):
                ref[:, span] = value
            continue
        top, den, num = state
        level = top + jnp.log2(den)
        out = num * (1.0 / den)
        outs = rest
        if own_rows:
            own_span = slice(span.start, min(span.stop, own_rows))
            if own_span.start < own_span.stop:
                outs[0][:, own_span] = out[:, : own_span.stop - own_span.start]
                outs[1][:, own_span] = level[:, : own_span.stop - own_span.start]
            outs = outs[2:]
        if outs:
            code, tail = encode(out, level)
            outs[0][:width, span] = code
            outs[0][width:, span] = tail


def merge_kernel(count, *refs):
    own_ref, own_level_ref = refs[:2]
    parts, out_ref = refs[2 : 1 + count], refs[1 + count]
    width = own_ref.shape[0]
    values, levels = [own_ref[...]], [own_level_ref[...]]
    for part in parts:
        value, level = decode(part[:width, :], part[width:, :])
        values.append(value)
        levels.append(level)
    top = functools.reduce(jnp.maximum, levels)
    factors = [jnp.exp2(level - top) for level in levels]
    inverse = 1.0 / functools.reduce(jnp.add, factors)
    num = functools.reduce(jnp.add, [value * (factor * inverse) for value, factor in zip(values, factors)])
    out_ref[...] = num.T.astype(out_ref.dtype)


def local(size, queries, cache_keys, cache_values, span_offset, positions):
    own_tokens, head_count, head_width = queries.shape
    shard_keys = cache_keys.shape[0]
    outer = size // inner
    rows = own_tokens * head_count
    me = lax.axis_index("ctx")
    place, owner = me % inner, me // inner
    scale = head_width ** (-0.5) * log2_e

    def swap(array, step):
        return lax.ppermute(array, "ctx", [(i, i ^ step) for i in range(size)])

    query = queries.reshape(rows, head_width)
    per_stage = max(outer // 4, 1)
    stages = [list(range(s, s + per_stage)) for s in range(0, outer, per_stage)]
    last = len(stages) - 1

    far_pair = [swap(cache_keys, 2), swap(cache_values, 2)]
    near_pair = [swap(cache_keys, 1), swap(cache_values, 1)]
    got = [query] + [None] * (outer - 1)

    def gather(index):
        for k in stages[index]:
            if k:
                low = k & -k
                got[k] = swap(got[k ^ low], inner * low)

    stage_rows = rows * per_stage
    tile = 256 if stage_rows % 256 == 0 else stage_rows

    fused_setup = per_stage == 1 and positions.shape[0] % 128 == 0 and 128 % own_tokens == 0
    if fused_setup:
        chain = [None]
    else:
        limits = (span_offset[0] + positions).reshape(outer, inner, own_tokens)
        limits = lax.dynamic_index_in_dim(limits, place, 1, keepdims=False)
        limits = [lax.dynamic_slice_in_dim(limits, owner ^ k, 1, axis=0) for k in range(outer)]
        limits = jnp.repeat(jnp.concatenate(limits, axis=0), head_count, axis=1)
        chain = [limits.reshape(len(stages), stage_rows)]

    def join(items, axis):
        return items[0] if len(items) == 1 else jnp.concatenate(items, axis=axis)

    vmem = pl.BlockSpec(memory_space=pltpu.VMEM)
    params = pltpu.CompilerParams(vmem_limit_bytes=20 << 20)
    pairs = [[cache_keys, cache_values], near_pair]
    stat = jax.ShapeDtypeStruct((1, stage_rows), jnp.float32)
    state_shapes = [stat, stat, jax.ShapeDtypeStruct((head_width, stage_rows), jnp.float32)]
    packed_shape = jax.ShapeDtypeStruct((head_width + tail_rows, stage_rows), jnp.bfloat16)
    own_shapes = [jax.ShapeDtypeStruct((head_width, rows), jnp.float32), jax.ShapeDtypeStruct((1, rows), jnp.float32)]
    states = [None] * len(stages)

    def attend(index, blocks, form):
        own_rows = rows if form == "packed" and index == 0 else 0
        if form == "state":
            shapes = state_shapes
        else:
            shapes = (own_shapes if own_rows else []) + ([packed_shape] if index or per_stage > 1 else [])
        setup = None
        if chain[0] is None:
            setup = (own_tokens, head_count)
            shapes = shapes + [jax.ShapeDtypeStruct((len(stages), stage_rows), jnp.int32)]
            shapes += [jax.ShapeDtypeStruct(array.shape, array.dtype) for array in pairs[0]]
            own = [pltpu.with_memory_space_constraint(array, pltpu.HBM) for array in (query, *pairs[0])]
            operands = [positions.reshape(-1, 128), span_offset.reshape(1, 1)] + own
            specs = [vmem] * 2 + [pl.BlockSpec(memory_space=pltpu.HBM)] * 3
            extra = [pltpu.VMEM(query.shape, query.dtype), pltpu.SemaphoreType.DMA((3,))]
            operands += [array for b in blocks[1:] for array in pairs[b]]
        else:
            operands = [chain[0], stage_query[index]] + [array for b in blocks for array in pairs[b]]
            operands += list(states[index] or ())
            specs, extra = [], []
        results = pl.pallas_call(
            functools.partial(attend_kernel, scale, index, blocks, states[index] is not None, form, own_rows, setup),
            in_specs=specs + [vmem] * (len(operands) - len(specs)),
            out_specs=[vmem] * len(shapes),
            out_shape=shapes,
            scratch_shapes=[
                pltpu.VMEM((2, shard_keys, tile), jnp.float32),
                pltpu.VMEM((2, shard_keys, tile), jnp.bfloat16),
                pltpu.VMEM((len(blocks), head_width + extra_rows, shard_keys), jnp.bfloat16),
            ]
            + extra,
            compiler_params=params,
        )(*operands)
        if setup:
            chain[0], pairs[0], results = results[-3], list(results[-2:]), results[:-3]
        chain[0], results = lax.optimization_barrier((chain[0], results))
        if form == "state":
            states[index] = results
        return results

    def hold(*arrays):
        chain[0], arrays = lax.optimization_barrier((chain[0], arrays))
        return list(arrays)

    stage_query = [None] * len(stages)

    def ready(index):
        stage_query[index] = join([got[k] for k in stages[index]], 0)

    for index in range(len(stages) - 1):
        gather(index)
        ready(index)
    attend(0, [0, 1], "state")
    source = stages[last][0] ^ (stages[last][0] & -stages[last][0])
    (got[source],) = hold(got[source])
    gather(last)
    ready(last)
    for index in range(1, last):
        attend(index, [0, 1], "state")
    far_pair = hold(*far_pair)
    pairs += [far_pair, [swap(array, 1) for array in far_pair]]
    attend(last, [0, 1], "state")
    parts = [None] * outer

    def send(index, packed):
        for at, k in enumerate(stages[index]):
            if k:
                piece = packed if per_stage == 1 else packed[:, at * rows : (at + 1) * rows]
                parts[k] = swap(piece, inner * k)

    for index in [last - 1, last] + list(range(last - 2, 0, -1)):
        send(index, attend(index, [2, 3], "packed")[0])
    results = attend(0, [2, 3], "packed")
    if per_stage > 1:
        send(0, results[2])
    merged = pl.pallas_call(
        functools.partial(merge_kernel, outer),
        in_specs=[vmem] * (outer + 1),
        out_specs=vmem,
        out_shape=jax.ShapeDtypeStruct((rows, head_width), jnp.bfloat16),
        compiler_params=params,
        name="merge",
    )(results[0], results[1], *parts[1:])
    return merged.reshape(own_tokens, head_count, head_width)


def solution(mesh):
    in_specs = (P("ctx", "kvh", None), P("ctx", "kvh"), P("ctx", "kvh"), P(), P())
    out_specs = P("ctx", "kvh", None)
    size = mesh.shape["ctx"]

    def body(*args):
        return local(size, *args)

    return jax.shard_map(body, mesh=mesh, in_specs=in_specs, out_specs=out_specs, check_vma=False)
```

profile of v0, /device:TPU:0, one launch (start us, length us, event | category | flops | bytes accessed | tf_op | source)
XLA Modules:
  0.0 45.3 jit_solution(6334549469911819763)
XLA Ops:
  0.0 0.5 %collective-permute-start = (bf16[1024,128]{1,0:T(8,128)(2,1)}, bf16[1024,128]{1,0:T(8,128)(2,1)S(1)}, u32[]{:S(2)}, u32[]{:S(2)}) collective-permute-start(bf16[1024,128]{1,0:T(8,128)(2,1)} %refs_3_.1), channel_id=1, source_target_pairs={{0,1},{1,0},{2,3},{3,2},{4,5},{5,4},{6,7},{7,6},{8,9},{9,8},{10,11... | collective-permute-start | bytes 786440 | tf_op jit(solution)/shard_map/ppermute | solution.py:201
  0.5 0.0 collective-permute-start.1
  0.5 3.0 %collective-permute-start.4 = (bf16[1024,128]{1,0:T(8,128)(2,1)}, bf16[1024,128]{1,0:T(8,128)(2,1)S(1)}, u32[]{:S(2)}, u32[]{:S(2)}) collective-permute-start(bf16[1024,128]{1,0:T(8,128)(2,1)} %refs_3_.1), channel_id=1, source_target_pairs={{0,2},{1,3},{2,0},{3,1},{4,6},{5,7},{6,4},{7,5},{8,10},{9,11},{10,... | collective-permute-start | bytes 786440 | tf_op jit(solution)/shard_map/ppermute | solution.py:201
  3.5 0.0 collective-permute-start.5
  3.5 3.1 %collective-permute-start.2 = (bf16[512,128]{1,0:T(8,128)(2,1)}, bf16[512,128]{1,0:T(8,128)(2,1)S(1)}, u32[]{:S(2)}, u32[]{:S(2)}) collective-permute-start(bf16[512,128]{1,0:T(8,128)(2,1)} %bitcast.5), channel_id=1, source_target_pairs={{0,8},{1,9},{2,10},{3,11},{4,12},{5,13},{6,14},{7,15},{8,0},{9,1},... | collective-permute-start | bytes 393224 | tf_op jit(solution)/shard_map/ppermute | solution.py:201
  6.6 0.0 collective-permute-done.refs_5_.refs_4_
  6.6 1.6 %collective-permute-start.3 = (bf16[512,128]{1,0:T(8,128)(2,1)}, bf16[512,128]{1,0:T(8,128)(2,1)S(1)}, u32[]{:S(2)}, u32[]{:S(2)}) collective-permute-start(bf16[512,128]{1,0:T(8,128)(2,1)} %bitcast.6), channel_id=1, source_target_pairs={{0,4},{1,5},{2,6},{3,7},{4,0},{5,1},{6,2},{7,3},{8,12},{9,13},{10,... | collective-permute-start | bytes 393224 | tf_op jit(solution)/shard_map/ppermute | solution.py:201
  8.8 0.0 copy-start.1
  8.8 0.0 collective-permute-done.1.refs_6_.refs_5_
  8.9 0.7 %copy-done.1 = s32[512]{0:T(512)S(1)} copy-done((s32[512]{0:T(512)S(1)}, s32[512]{0:T(512)}, u32[]{:S(2)}) %copy-start.1) | copy-done | bytes 2072
  9.5 2.7 %shard_map.55 = (f32[1,512]{1,0:T(1,128)S(1)}, f32[1,512]{1,0:T(1,128)S(1)}, f32[128,512]{1,0:T(8,128)S(1)}, s32[4,512]{1,0:T(4,128)S(1)}, bf16[1024,128]{1,0:T(8,128)(2,1)S(1)}, /*index=5*/bf16[1024,128]{1,0:T(8,128)(2,1)S(1)}) custom-call(s32[4,128]{1,0:T(4,128)S(1)} %bitcast.9, s32[1,1]{1,0:T(1,128)} %bitcast.4.refs_1_, bf16[512,128]{1,0:T(8,128)(2,1)} %bitcast.7, ...), custom_call_target="tpu_custom_call" | custom-call | tf_op jit(solution)/shard_map/pallas_call | solution.py:263
  12.2 0.5 %collective-permute-done.2.refs_1_ = bf16[512,128]{1,0:T(8,128)(2,1)S(1)} collective-permute-done((bf16[512,128]{1,0:T(8,128)(2,1)}, bf16[512,128]{1,0:T(8,128)(2,1)S(1)}, u32[]{:S(2)}, u32[]{:S(2)}) %collective-permute-start.2) | collective-permute-done | bytes 131104 | tf_op jit(solution)/shard_map/ppermute | solution.py:201
  12.7 0.3 collective-permute-done.3.refs_1_
  13.1 1.5 %shard_map.56 = (f32[1,512]{1,0:T(1,128)S(1)}, f32[1,512]{1,0:T(1,128)S(1)}, f32[128,512]{1,0:T(8,128)S(1)}) custom-call(s32[4,512]{1,0:T(4,128)S(1)} %get-tuple-element.86.refs_0_, bf16[512,128]{1,0:T(8,128)(2,1)S(1)} %collective-permute-done.3.refs_1_, bf16[1024,128]{1,0:T(8,128)(2,1)S(1)} %get-tuple-element.57.refs_2_, ...), custom_call_target="tpu_custom_call" | custom-call | tf_op jit(solution)/shard_map/pallas_call | solution.py:263
  14.6 1.5 %shard_map.57 = (f32[1,512]{1,0:T(1,128)S(1)}, f32[1,512]{1,0:T(1,128)S(1)}, f32[128,512]{1,0:T(8,128)S(1)}) custom-call(s32[4,512]{1,0:T(4,128)S(1)} %get-tuple-element.86.refs_0_, bf16[512,128]{1,0:T(8,128)(2,1)S(1)} %collective-permute-done.2.refs_1_, bf16[1024,128]{1,0:T(8,128)(2,1)S(1)} %get-tuple-element.57.refs_2_, ...), custom_call_target="tpu_custom_call" | custom-call | tf_op jit(solution)/shard_map/pallas_call | solution.py:263
  16.1 0.0 collective-permute-done.4.refs_2_
  16.1 0.0 collective-permute-done.5.refs_3_
  16.1 0.1 collective-permute-start.7
  16.2 0.5 %collective-permute-start.8 = (bf16[1024,128]{1,0:T(8,128)(2,1)S(1)}, bf16[1024,128]{1,0:T(8,128)(2,1)S(1)}, u32[]{:S(2)}, u32[]{:S(2)}) collective-permute-start(bf16[1024,128]{1,0:T(8,128)(2,1)S(1)} %collective-permute-done.5.refs_3_), channel_id=1, source_target_pairs={{0,1},{1,0},{2,3},{3,2},{4,5},{5,4},{6,7},{7,6},{8,9},{9,8},{10,11... | collective-permute-start | bytes 786440 | tf_op jit(solution)/shard_map/ppermute | solution.py:201
  16.7 1.4 %collective-permute-start.6 = (bf16[512,128]{1,0:T(8,128)(2,1)S(1)}, bf16[512,128]{1,0:T(8,128)(2,1)S(1)}, u32[]{:S(2)}, u32[]{:S(2)}) collective-permute-start(bf16[512,128]{1,0:T(8,128)(2,1)S(1)} %collective-permute-done.2.refs_1_), channel_id=1, source_target_pairs={{0,4},{1,5},{2,6},{3,7},{4,0},{5,1},{6,2},{7,3},{8,12},{9,13},{10,... | collective-permute-start | bytes 393224 | tf_op jit(solution)/shard_map/ppermute | solution.py:201
  18.1 4.1 %collective-permute-done.6.refs_1_ = bf16[512,128]{1,0:T(8,128)(2,1)S(1)} collective-permute-done((bf16[512,128]{1,0:T(8,128)(2,1)S(1)}, bf16[512,128]{1,0:T(8,128)(2,1)S(1)}, u32[]{:S(2)}, u32[]{:S(2)}) %collective-permute-start.6) | collective-permute-done | bytes 131104 | tf_op jit(solution)/shard_map/ppermute | solution.py:201
  22.2 1.5 %shard_map.58 = (f32[1,512]{1,0:T(1,128)S(1)}, f32[1,512]{1,0:T(1,128)S(1)}, f32[128,512]{1,0:T(8,128)S(1)}) custom-call(s32[4,512]{1,0:T(4,128)S(1)} %get-tuple-element.86.refs_0_, bf16[512,128]{1,0:T(8,128)(2,1)S(1)} %collective-permute-done.6.refs_1_, bf16[1024,128]{1,0:T(8,128)(2,1)S(1)} %get-tuple-element.57.refs_2_, ...), custom_call_target="tpu_custom_call" | custom-call | tf_op jit(solution)/shard_map/pallas_call | solution.py:263
  23.7 0.0 collective-permute-done.7.refs_4_
  23.7 0.0 collective-permute-done.8.refs_5_
  23.7 1.6 %shard_map.59 = bf16[136,512]{1,0:T(8,128)(2,1)S(1)} custom-call(s32[4,512]{1,0:T(4,128)S(1)} %get-tuple-element.86.refs_0_, bf16[512,128]{1,0:T(8,128)(2,1)S(1)} %collective-permute-done.2.refs_1_, bf16[1024,128]{1,0:T(8,128)(2,1)S(1)} %collective-permute-done.4.refs_2_, bf16[1024,128]{1,0:T(8,128)(2,1)S(1)} %collective-permute-done.5.refs_3_, ...), custom_call_target="tpu_custom_call" | custom-call | tf_op jit(solution)/shard_map/pallas_call | solution.py:263
  25.4 1.6 %shard_map.60 = bf16[136,512]{1,0:T(8,128)(2,1)S(1)} custom-call(s32[4,512]{1,0:T(4,128)S(1)} %get-tuple-element.86.refs_0_, bf16[512,128]{1,0:T(8,128)(2,1)S(1)} %collective-permute-done.6.refs_1_, bf16[1024,128]{1,0:T(8,128)(2,1)S(1)} %collective-permute-done.4.refs_2_, bf16[1024,128]{1,0:T(8,128)(2,1)S(1)} %collective-permute-done.5.refs_3_, ...), custom_call_target="tpu_custom_call" | custom-call | tf_op jit(solution)/shard_map/pallas_call | solution.py:263
  27.0 0.0 copy-start
  27.0 1.6 %shard_map.61 = bf16[136,512]{1,0:T(8,128)(2,1)S(1)} custom-call(s32[4,512]{1,0:T(4,128)S(1)} %get-tuple-element.86.refs_0_, bf16[512,128]{1,0:T(8,128)(2,1)S(1)} %collective-permute-done.3.refs_1_, bf16[1024,128]{1,0:T(8,128)(2,1)S(1)} %collective-permute-done.4.refs_2_, bf16[1024,128]{1,0:T(8,128)(2,1)S(1)} %collective-permute-done.5.refs_3_, ...), custom_call_target="tpu_custom_call" | custom-call | tf_op jit(solution)/shard_map/pallas_call | solution.py:263
  28.6 1.5 %collective-permute-start.9 = (bf16[136,512]{1,0:T(8,128)(2,1)S(1)}, bf16[136,512]{1,0:T(8,128)(2,1)S(1)}, u32[]{:S(2)}, u32[]{:S(2)}) collective-permute-start(bf16[136,512]{1,0:T(8,128)(2,1)S(1)} %shard_map.61), channel_id=1, source_target_pairs={{0,4},{1,5},{2,6},{3,7},{4,0},{5,1},{6,2},{7,3},{8,12},{9,13},{10,... | collective-permute-start | bytes 417800 | tf_op jit(solution)/shard_map/ppermute | solution.py:201
  30.1 2.4 %collective-permute-start.11 = (bf16[136,512]{1,0:T(8,128)(2,1)S(1)}, bf16[136,512]{1,0:T(8,128)(2,1)S(1)}, u32[]{:S(2)}, u32[]{:S(2)}) collective-permute-start(bf16[136,512]{1,0:T(8,128)(2,1)S(1)} %shard_map.60), channel_id=1, source_target_pairs={{0,12},{1,13},{2,14},{3,15},{4,8},{5,9},{6,10},{7,11},{8,4},{9,5},... | collective-permute-start | bytes 417800 | tf_op jit(solution)/shard_map/ppermute | solution.py:201
  32.5 0.1 collective-permute-start.10
  32.6 0.0 copy-done
  32.6 1.5 %shard_map.62 = (f32[128,512]{1,0:T(8,128)S(1)}, f32[1,512]{1,0:T(1,128)S(1)}) custom-call(s32[4,512]{1,0:T(4,128)S(1)} %get-tuple-element.86.refs_0_, bf16[512,128]{1,0:T(8,128)(2,1)S(1)} %bitcast.8, bf16[1024,128]{1,0:T(8,128)(2,1)S(1)} %collective-permute-done.4.refs_2_, bf16[1024,128]{1,0:T(8,128)(2,1)S(1)} %collective-permute-done.5.refs_3_, ...), custom_call_target="tpu_custom_call" | custom-call | tf_op jit(solution)/shard_map/pallas_call | solution.py:263
  34.1 0.0 collective-permute-done.9.refs_2_
  34.1 5.5 %collective-permute-done.11.refs_4_ = bf16[136,512]{1,0:T(8,128)(2,1)S(1)} collective-permute-done((bf16[136,512]{1,0:T(8,128)(2,1)S(1)}, bf16[136,512]{1,0:T(8,128)(2,1)S(1)}, u32[]{:S(2)}, u32[]{:S(2)}) %collective-permute-start.11) | collective-permute-done | bytes 139296 | tf_op jit(solution)/shard_map/ppermute | solution.py:201
  39.7 4.6 %collective-permute-done.10.refs_3_ = bf16[136,512]{1,0:T(8,128)(2,1)S(1)} collective-permute-done((bf16[136,512]{1,0:T(8,128)(2,1)S(1)}, bf16[136,512]{1,0:T(8,128)(2,1)S(1)}, u32[]{:S(2)}, u32[]{:S(2)}) %collective-permute-start.10) | collective-permute-done | bytes 139296 | tf_op jit(solution)/shard_map/ppermute | solution.py:201
  44.3 1.0 %merge.1 = bf16[512,128]{1,0:T(8,128)(2,1)} custom-call(f32[128,512]{1,0:T(8,128)S(1)} %get-tuple-element.92.refs_0_, f32[1,512]{1,0:T(1,128)S(1)} %get-tuple-element.93.refs_1_, bf16[136,512]{1,0:T(8,128)(2,1)S(1)} %collective-permute-done.9.refs_2_, bf16[136,512]{1,0:T(8,128)(2,1)S(1)} %collective-permute-done.10.refs_3_, ...), custom_call_target="tpu_custom_call" | custom-call | tf_op jit(solution)/shard_map/merge/pallas_call | solution.py:318
Async XLA Ops:
  0.0 6.6 %collective-permute-start = (bf16[1024,128]{1,0:T(8,128)(2,1)}, bf16[1024,128]{1,0:T(8,128)(2,1)S(1)}, u32[]{:S(2)}, u32[]{:S(2)}) collective-permute-start(bf16[1024,128]{1,0:T(8,128)(2,1)} %refs_3_.1), channel_id=1, source_target_pairs={{0,1},{1,0},{2,3},{3,2},{4,5},{5,4},{6,7},{7,6},{8,9},{9,8},{10,11... | collective-permute-start | bytes 786440 | tf_op jit(solution)/shard_map/ppermute | solution.py:201
  0.5 8.4 %collective-permute-start.1 = (bf16[1024,128]{1,0:T(8,128)(2,1)}, bf16[1024,128]{1,0:T(8,128)(2,1)S(1)}, u32[]{:S(2)}, u32[]{:S(2)}) collective-permute-start(bf16[1024,128]{1,0:T(8,128)(2,1)} %refs_4_.1), channel_id=1, source_target_pairs={{0,1},{1,0},{2,3},{3,2},{4,5},{5,4},{6,7},{7,6},{8,9},{9,8},{10,11... | collective-permute-start | bytes 786440 | tf_op jit(solution)/shard_map/ppermute | solution.py:201
  0.5 15.6 %collective-permute-start.4 = (bf16[1024,128]{1,0:T(8,128)(2,1)}, bf16[1024,128]{1,0:T(8,128)(2,1)S(1)}, u32[]{:S(2)}, u32[]{:S(2)}) collective-permute-start(bf16[1024,128]{1,0:T(8,128)(2,1)} %refs_3_.1), channel_id=1, source_target_pairs={{0,2},{1,3},{2,0},{3,1},{4,6},{5,7},{6,4},{7,5},{8,10},{9,11},{10,... | collective-permute-start | bytes 786440 | tf_op jit(solution)/shard_map/ppermute | solution.py:201
  3.5 12.6 %collective-permute-start.5 = (bf16[1024,128]{1,0:T(8,128)(2,1)}, bf16[1024,128]{1,0:T(8,128)(2,1)S(1)}, u32[]{:S(2)}, u32[]{:S(2)}) collective-permute-start(bf16[1024,128]{1,0:T(8,128)(2,1)} %refs_4_.1), channel_id=1, source_target_pairs={{0,2},{1,3},{2,0},{3,1},{4,6},{5,7},{6,4},{7,5},{8,10},{9,11},{10,... | collective-permute-start | bytes 786440 | tf_op jit(solution)/shard_map/ppermute | solution.py:201
  3.5 9.2 %collective-permute-start.2 = (bf16[512,128]{1,0:T(8,128)(2,1)}, bf16[512,128]{1,0:T(8,128)(2,1)S(1)}, u32[]{:S(2)}, u32[]{:S(2)}) collective-permute-start(bf16[512,128]{1,0:T(8,128)(2,1)} %bitcast.5), channel_id=1, source_target_pairs={{0,8},{1,9},{2,10},{3,11},{4,12},{5,13},{6,14},{7,15},{8,0},{9,1},... | collective-permute-start | bytes 393224 | tf_op jit(solution)/shard_map/ppermute | solution.py:201
  6.6 6.5 %collective-permute-start.3 = (bf16[512,128]{1,0:T(8,128)(2,1)}, bf16[512,128]{1,0:T(8,128)(2,1)S(1)}, u32[]{:S(2)}, u32[]{:S(2)}) collective-permute-start(bf16[512,128]{1,0:T(8,128)(2,1)} %bitcast.6), channel_id=1, source_target_pairs={{0,4},{1,5},{2,6},{3,7},{4,0},{5,1},{6,2},{7,3},{8,12},{9,13},{10,... | collective-permute-start | bytes 393224 | tf_op jit(solution)/shard_map/ppermute | solution.py:201
  8.8 0.7 %copy-start.1 = (s32[512]{0:T(512)S(1)}, s32[512]{0:T(512)}, u32[]{:S(2)}) copy-start(s32[512]{0:T(512)} %param.9) | copy-start | bytes 6148
  16.1 7.6 %collective-permute-start.7 = (bf16[1024,128]{1,0:T(8,128)(2,1)S(1)}, bf16[1024,128]{1,0:T(8,128)(2,1)S(1)}, u32[]{:S(2)}, u32[]{:S(2)}) collective-permute-start(bf16[1024,128]{1,0:T(8,128)(2,1)S(1)} %collective-permute-done.4.refs_2_), channel_id=1, source_target_pairs={{0,1},{1,0},{2,3},{3,2},{4,5},{5,4},{6,7},{7,6},{8,9},{9,8},{10,11... | collective-permute-start | bytes 786440 | tf_op jit(solution)/shard_map/ppermute | solution.py:201
  16.2 7.5 %collective-permute-start.8 = (bf16[1024,128]{1,0:T(8,128)(2,1)S(1)}, bf16[1024,128]{1,0:T(8,128)(2,1)S(1)}, u32[]{:S(2)}, u32[]{:S(2)}) collective-permute-start(bf16[1024,128]{1,0:T(8,128)(2,1)S(1)} %collective-permute-done.5.refs_3_), channel_id=1, source_target_pairs={{0,1},{1,0},{2,3},{3,2},{4,5},{5,4},{6,7},{7,6},{8,9},{9,8},{10,11... | collective-permute-start | bytes 786440 | tf_op jit(solution)/shard_map/ppermute | solution.py:201
  16.7 5.5 %collective-permute-start.6 = (bf16[512,128]{1,0:T(8,128)(2,1)S(1)}, bf16[512,128]{1,0:T(8,128)(2,1)S(1)}, u32[]{:S(2)}, u32[]{:S(2)}) collective-permute-start(bf16[512,128]{1,0:T(8,128)(2,1)S(1)} %collective-permute-done.2.refs_1_), channel_id=1, source_target_pairs={{0,4},{1,5},{2,6},{3,7},{4,0},{5,1},{6,2},{7,3},{8,12},{9,13},{10,... | collective-permute-start | bytes 393224 | tf_op jit(solution)/shard_map/ppermute | solution.py:201
  27.0 5.6 %copy-start = (bf16[32,16,128]{2,1,0:T(8,128)(2,1)S(1)}, bf16[32,16,128]{2,1,0:T(8,128)(2,1)}, u32[]{:S(2)}) copy-start(bf16[32,16,128]{2,1,0:T(8,128)(2,1)} %param.5) | copy-start | bytes 393220
  28.6 5.5 %collective-permute-start.9 = (bf16[136,512]{1,0:T(8,128)(2,1)S(1)}, bf16[136,512]{1,0:T(8,128)(2,1)S(1)}, u32[]{:S(2)}, u32[]{:S(2)}) collective-permute-start(bf16[136,512]{1,0:T(8,128)(2,1)S(1)} %shard_map.61), channel_id=1, source_target_pairs={{0,4},{1,5},{2,6},{3,7},{4,0},{5,1},{6,2},{7,3},{8,12},{9,13},{10,... | collective-permute-start | bytes 417800 | tf_op jit(solution)/shard_map/ppermute | solution.py:201
  30.1 9.6 %collective-permute-start.11 = (bf16[136,512]{1,0:T(8,128)(2,1)S(1)}, bf16[136,512]{1,0:T(8,128)(2,1)S(1)}, u32[]{:S(2)}, u32[]{:S(2)}) collective-permute-start(bf16[136,512]{1,0:T(8,128)(2,1)S(1)} %shard_map.60), channel_id=1, source_target_pairs={{0,12},{1,13},{2,14},{3,15},{4,8},{5,9},{6,10},{7,11},{8,4},{9,5},... | collective-permute-start | bytes 417800 | tf_op jit(solution)/shard_map/ppermute | solution.py:201
  32.5 11.8 %collective-permute-start.10 = (bf16[136,512]{1,0:T(8,128)(2,1)S(1)}, bf16[136,512]{1,0:T(8,128)(2,1)S(1)}, u32[]{:S(2)}, u32[]{:S(2)}) collective-permute-start(bf16[136,512]{1,0:T(8,128)(2,1)S(1)} %shard_map.59), channel_id=1, source_target_pairs={{0,8},{1,9},{2,10},{3,11},{4,12},{5,13},{6,14},{7,15},{8,0},{9,1},... | collective-permute-start | bytes 417800 | tf_op jit(solution)/shard_map/ppermute | solution.py:201
where the time goes:
time: 45.5 us; the launch traced here: 45.3 us
  waiting for transfers between devices  15 us (33%)
  Pallas kernels  14.7 us (32%)
  starting transfers between devices  14.1 us (31%)
  between operations  0.8 us (2%)
  local copies, waits for them, and re-layouts  0.67 us (1%)
    ppermute x12, waiting for transfers between devices, swap(): return lax.ppermute(array, 'ctx', [(i, i ^ step) for i in range(size)])  15 us
    ppermute x12, starting transfers between devices, swap(): return lax.ppermute(array, 'ctx', [(i, i ^ step) for i in range(size)])  14.1 us
    pallas_call x8, Pallas kernels, attend(): pl.pallas_call(functools.partial(attend_kernel, scale, index, blocks, sta...  13.6 us
    pallas_call x1, Pallas kernels, local(): pl.pallas_call(functools.partial(merge_kernel, outer), in_specs=[vmem] *...  1.03 us
  transfers between devices with their start and end apart: 12, of which 5 were waited for; matrix products, arithmetic and copies ran while one was open for 0% of the time, Pallas kernels for 19%

commit v1 on v0

--- a/solution.py
+++ b/solution.py
@@ -120,7 +120,7 @@
         limits_ref[k : k + 1, :] = wide[2 * k : 2 * k + 1] * 256 + wide[2 * k + 1 : 2 * k + 2] + span_ref[...]
 
 
-def attend_kernel(scale, index, blocks, has_state, form, own_rows, setup, *refs):
+def attend_kernel(scale, index, blocks, has_state, plan, setup, *refs):
     me = lax.axis_index("ctx")
     refs = list(refs)
     if setup:
@@ -142,7 +142,7 @@
     keys = refs[2 : 2 + 2 * len(blocks) : 2]
     values = refs[3 : 3 + 2 * len(blocks) : 2]
     rest = list(refs[2 + 2 * len(blocks) :])
-    rows, width = q_ref.shape
+    rows, _ = q_ref.shape
     tile = scratch[0].shape[2]
     spans = [slice(at, at + tile) for at in range(0, rows, tile)]
     states = [None] * len(spans)
@@ -151,41 +151,55 @@
         rest = rest[3:]
     limits = [limits_ref[index : index + 1, :] - (me ^ b) * keys[0].shape[0] for b in blocks]
     states = attend_tiles(scale, q_ref[...], keys, values, limits, states, *scratch)
-    for span, state in zip(spans, states):
-        if form == "state":
+    if plan is None:
+        for span, state in zip(spans, states):
             for ref, value in zip(rest, state):
                 ref[:, span] = value
-            continue
-        top, den, num = state
-        level = top + jnp.log2(den)
-        out = num * (1.0 / den)
-        outs = rest
-        if own_rows:
-            own_span = slice(span.start, min(span.stop, own_rows))
-            if own_span.start < own_span.stop:
-                outs[0][:, own_span] = out[:, : own_span.stop - own_span.start]
-                outs[1][:, own_span] = level[:, : own_span.stop - own_span.start]
-            outs = outs[2:]
-        if outs:
-            code, tail = encode(out, level)
-            outs[0][:width, span] = code
-            outs[0][width:, span] = tail
-
-
-def merge_kernel(count, *refs):
-    own_ref, own_level_ref = refs[:2]
-    parts, out_ref = refs[2 : 1 + count], refs[1 + count]
-    width = own_ref.shape[0]
-    values, levels = [own_ref[...]], [own_level_ref[...]]
-    for part in parts:
-        value, level = decode(part[:width, :], part[width:, :])
-        values.append(value)
-        levels.append(level)
+        return
+    for at, form, out, offset, count in plan:
+        top, den, num = (value[:, :count] for value in states[at])
+        write_partial(rest[out:], form, slice(offset, offset + count), num * (1.0 / den), top + jnp.log2(den))
+
+
+def write_partial(refs, form, span, value, level):
+    width = value.shape[0]
+    if form == "float":
+        refs[0][:, span] = value
+        refs[1][:, span] = level
+    else:
+        code, tail = encode(value, level)
+        refs[0][:width, span] = code
+        refs[0][width:, span] = tail
+
+
+def combine(values, levels):
     top = functools.reduce(jnp.maximum, levels)
     factors = [jnp.exp2(level - top) for level in levels]
-    inverse = 1.0 / functools.reduce(jnp.add, factors)
-    num = functools.reduce(jnp.add, [value * (factor * inverse) for value, factor in zip(values, factors)])
-    out_ref[...] = num.T.astype(out_ref.dtype)
+    total = functools.reduce(jnp.add, factors)
+    inverse = 1.0 / total
+    value = functools.reduce(jnp.add, [value * (factor * inverse) for value, factor in zip(values, factors)])
+    return value, top + jnp.log2(total)
+
+
+def combine_kernel(value_ref, level_ref, part_ref, out_ref):
+    width, lanes = value_ref.shape
+    value, level = decode(part_ref[:width, :], part_ref[width:, :])
+    value, level = combine([value_ref[...], value], [level_ref[...], level])
+    write_partial([out_ref], "code", slice(0, lanes), value, level)
+
+
+def merge_kernel(groups, *refs):
+    own_ref, own_level_ref = refs[:2]
+    parts, out_ref = refs[2:-1], refs[-1]
+    width = own_ref.shape[0]
+    for span, members in groups:
+        values, levels = [own_ref[:, span]], [own_level_ref[:, span]]
+        for at, offset in members:
+            lanes = slice(offset, offset + span.stop - span.start)
+            value, level = decode(parts[at][:width, lanes], parts[at][width:, lanes])
+            values.append(value)
+            levels.append(level)
+        out_ref[span, :] = combine(values, levels)[0].T.astype(out_ref.dtype)
 
 
 def local(size, queries, cache_keys, cache_values, span_offset, positions):
@@ -236,16 +250,18 @@
     pairs = [[cache_keys, cache_values], near_pair]
     stat = jax.ShapeDtypeStruct((1, stage_rows), jnp.float32)
     state_shapes = [stat, stat, jax.ShapeDtypeStruct((head_width, stage_rows), jnp.float32)]
-    packed_shape = jax.ShapeDtypeStruct((head_width + tail_rows, stage_rows), jnp.bfloat16)
-    own_shapes = [jax.ShapeDtypeStruct((head_width, rows), jnp.float32), jax.ShapeDtypeStruct((1, rows), jnp.float32)]
+
+    def packed_shape(lanes):
+        return jax.ShapeDtypeStruct((head_width + tail_rows, lanes), jnp.bfloat16)
+
+    def float_shapes(lanes):
+        return [jax.ShapeDtypeStruct((size_of, lanes), jnp.float32) for size_of in (head_width, 1)]
+
+    tiles = range(stage_rows // tile)
+    whole_plan = [(at, "code", 0, at * tile, tile) for at in tiles]
     states = [None] * len(stages)
 
-    def attend(index, blocks, form):
-        own_rows = rows if form == "packed" and index == 0 else 0
-        if form == "state":
-            shapes = state_shapes
-        else:
-            shapes = (own_shapes if own_rows else []) + ([packed_shape] if index or per_stage > 1 else [])
+    def attend(index, blocks, plan=None, shapes=state_shapes):
         setup = None
         if chain[0] is None:
             setup = (own_tokens, head_count)
@@ -261,7 +277,9 @@
             operands += list(states[index] or ())
             specs, extra = [], []
         results = pl.pallas_call(
-            functools.partial(attend_kernel, scale, index, blocks, states[index] is not None, form, own_rows, setup),
+            functools.partial(
+                attend_kernel, scale, index, blocks, states[index] is not None, plan, setup
+            ),
             in_specs=specs + [vmem] * (len(operands) - len(specs)),
             out_specs=[vmem] * len(shapes),
             out_shape=shapes,
@@ -276,7 +294,7 @@
         if setup:
             chain[0], pairs[0], results = results[-3], list(results[-2:]), results[:-3]
         chain[0], results = lax.optimization_barrier((chain[0], results))
-        if form == "state":
+        if plan is None:
             states[index] = results
         return results
 
@@ -292,37 +310,70 @@
     for index in range(len(stages) - 1):
         gather(index)
         ready(index)
-    attend(0, [0, 1], "state")
+    attend(0, [0, 1])
     source = stages[last][0] ^ (stages[last][0] & -stages[last][0])
     (got[source],) = hold(got[source])
     gather(last)
     ready(last)
     for index in range(1, last):
-        attend(index, [0, 1], "state")
+        attend(index, [0, 1])
     far_pair = hold(*far_pair)
     pairs += [far_pair, [swap(array, 1) for array in far_pair]]
-    attend(last, [0, 1], "state")
-    parts = [None] * outer
-
-    def send(index, packed):
-        for at, k in enumerate(stages[index]):
-            if k:
-                piece = packed if per_stage == 1 else packed[:, at * rows : (at + 1) * rows]
-                parts[k] = swap(piece, inner * k)
-
-    for index in [last - 1, last] + list(range(last - 2, 0, -1)):
-        send(index, attend(index, [2, 3], "packed")[0])
-    results = attend(0, [2, 3], "packed")
-    if per_stage > 1:
-        send(0, results[2])
+    attend(last, [0, 1])
+    own_plan = [(at, "float", 0, at * tile, tile) for at in tiles]
+    if outer == 4 and stage_rows == 2 * tile:
+        halves = [slice(0, tile), slice(tile, 2 * tile)]
+        plan = [(0, "code", 0, 0, tile), (1, "code", 1, 0, tile)]
+        direct, handed = attend(3, [2, 3], plan, [packed_shape(tile)] * 2)
+        handed = swap(handed, inner)
+        third = swap(direct, 3 * inner)
+        plan = [(0, "code", 0, 0, tile), (1, "float", 1, 0, tile)]
+        direct, value, level = attend(2, [2, 3], plan, [packed_shape(tile)] + float_shapes(tile))
+        second = swap(direct, 2 * inner)
+        (packed,) = attend(1, [2, 3], whole_plan, [packed_shape(stage_rows)])
+        first = swap(packed, inner)
+        (handed,) = hold(handed)
+        joined = pl.pallas_call(
+            combine_kernel,
+            in_specs=[vmem] * 3,
+            out_specs=vmem,
+            out_shape=packed_shape(tile),
+            compiler_params=params,
+            name="combine",
+        )(value, level, handed)
+        (joined,) = hold(joined)
+        joined = swap(joined, 2 * inner)
+        own = attend(0, [2, 3], own_plan, float_shapes(stage_rows))
+        parts = [first, second, third, joined]
+        groups = [(halves[0], [(0, 0), (1, 0), (2, 0)]), (halves[1], [(0, tile), (3, 0)])]
+    else:
+        parts = []
+
+        def send(index, packed):
+            for at, k in enumerate(stages[index]):
+                if k:
+                    piece = packed if per_stage == 1 else packed[:, at * rows : (at + 1) * rows]
+                    parts.append(swap(piece, inner * k))
+
+        for index in range(last, 0, -1):
+            send(index, attend(index, [2, 3], whole_plan, [packed_shape(stage_rows)])[0])
+        if per_stage == 1:
+            own = attend(0, [2, 3], own_plan, float_shapes(rows))
+        else:
+            own_plan = [(0, "float", 1, 0, rows)]
+            packed, *own = attend(
+                0, [2, 3], whole_plan + own_plan, [packed_shape(stage_rows)] + float_shapes(rows)
+            )
+            send(0, packed)
+        groups = [(slice(0, rows), [(at, 0) for at in range(len(parts))])]
     merged = pl.pallas_call(
-        functools.partial(merge_kernel, outer),
-        in_specs=[vmem] * (outer + 1),
+        functools.partial(merge_kernel, groups),
+        in_specs=[vmem] * (2 + len(parts)),
         out_specs=vmem,
         out_shape=jax.ShapeDtypeStruct((rows, head_width), jnp.bfloat16),
         compiler_params=params,
         name="merge",
-    )(results[0], results[1], *parts[1:])
+    )(*own, *parts)
     return merged.reshape(own_tokens, head_count, head_width)
 
 

time: 45.5 us -> 44.3 us (0.974)
  waiting for transfers between devices: 15 us -> 10.3 us
  starting transfers between devices: 14.1 us -> 17.7 us
    ppermute x12 -> x14, waiting for transfers between devices: 15 us -> 10.3 us  [swap(): return lax.ppermute(array, 'ctx', [(i, i ^ step) for i in range(size)])]
    ppermute x12 -> x14, starting transfers between devices: 14.1 us -> 17.7 us  [swap(): return lax.ppermute(array, 'ctx', [(i, i ^ step) for i in range(size)])]
    pallas_call x1 -> x2, Pallas kernels: 1.03 us -> 1.12 us  [the longest x1 0.99 us: local(): pl.pallas_call(functools.partial(merge_kernel, groups), in_specs=[vmem] *...]
  transfers between devices with their start and end apart: 12 -> 14, of which waited for: 5 -> 5; matrix products, arithmetic and copies ran while one was open for 0% -> 0% of each run, Pallas kernels for 19% -> 27%
where the time goes in v1:
time: 44.3 us; the launch traced here: 44.1 us
  starting transfers between devices  17.7 us (40%)
  Pallas kernels  14.7 us (33%)
  waiting for transfers between devices  10.3 us (23%)
  between operations  0.79 us (2%)
  local copies, waits for them, and re-layouts  0.67 us (2%)
    ppermute x14, starting transfers between devices, swap(): return lax.ppermute(array, 'ctx', [(i, i ^ step) for i in range(size)])  17.7 us
    pallas_call x8, Pallas kernels, attend(): pl.pallas_call(functools.partial(attend_kernel, scale, index, blocks, sta...  13.6 us
    ppermute x14, waiting for transfers between devices, swap(): return lax.ppermute(array, 'ctx', [(i, i ^ step) for i in range(size)])  10.3 us
    pallas_call x1, Pallas kernels, local(): pl.pallas_call(functools.partial(merge_kernel, groups), in_specs=[vmem] *...  0.99 us
  transfers between devices with their start and end apart: 14, of which 5 were waited for; matrix products, arithmetic and copies ran while one was open for 0% of the time, Pallas kernels for 27%

profile of v1, /device:TPU:0, one launch (start us, length us, event | category | flops | bytes accessed | tf_op | source)
XLA Modules:
  0.0 44.1 jit_solution(10644343207499383003)
XLA Ops:
  0.0 0.5 %collective-permute-start = (bf16[1024,128]{1,0:T(8,128)(2,1)}, bf16[1024,128]{1,0:T(8,128)(2,1)S(1)}, u32[]{:S(2)}, u32[]{:S(2)}) collective-permute-start(bf16[1024,128]{1,0:T(8,128)(2,1)} %refs_3_.1), channel_id=1, source_target_pairs={{0,1},{1,0},{2,3},{3,2},{4,5},{5,4},{6,7},{7,6},{8,9},{9,8},{10,11... | collective-permute-start | bytes 786440 | tf_op jit(solution)/shard_map/ppermute | solution.py:215
  0.5 0.0 collective-permute-start.1
  0.5 3.0 %collective-permute-start.4 = (bf16[1024,128]{1,0:T(8,128)(2,1)}, bf16[1024,128]{1,0:T(8,128)(2,1)S(1)}, u32[]{:S(2)}, u32[]{:S(2)}) collective-permute-start(bf16[1024,128]{1,0:T(8,128)(2,1)} %refs_3_.1), channel_id=1, source_target_pairs={{0,2},{1,3},{2,0},{3,1},{4,6},{5,7},{6,4},{7,5},{8,10},{9,11},{10,... | collective-permute-start | bytes 786440 | tf_op jit(solution)/shard_map/ppermute | solution.py:215
  3.5 0.0 collective-permute-start.5
  3.5 3.1 %collective-permute-start.2 = (bf16[512,128]{1,0:T(8,128)(2,1)}, bf16[512,128]{1,0:T(8,128)(2,1)S(1)}, u32[]{:S(2)}, u32[]{:S(2)}) collective-permute-start(bf16[512,128]{1,0:T(8,128)(2,1)} %bitcast.5), channel_id=1, source_target_pairs={{0,8},{1,9},{2,10},{3,11},{4,12},{5,13},{6,14},{7,15},{8,0},{9,1},... | collective-permute-start | bytes 393224 | tf_op jit(solution)/shard_map/ppermute | solution.py:215
  6.6 0.0 collective-permute-done.refs_5_.refs_4_
  6.6 1.6 %collective-permute-start.3 = (bf16[512,128]{1,0:T(8,128)(2,1)}, bf16[512,128]{1,0:T(8,128)(2,1)S(1)}, u32[]{:S(2)}, u32[]{:S(2)}) collective-permute-start(bf16[512,128]{1,0:T(8,128)(2,1)} %bitcast.6), channel_id=1, source_target_pairs={{0,4},{1,5},{2,6},{3,7},{4,0},{5,1},{6,2},{7,3},{8,12},{9,13},{10,... | collective-permute-start | bytes 393224 | tf_op jit(solution)/shard_map/ppermute | solution.py:215
  8.8 0.0 copy-start.1
  8.8 0.0 collective-permute-done.1.refs_6_.refs_5_
  8.9 0.7 %copy-done.1 = s32[512]{0:T(512)S(1)} copy-done((s32[512]{0:T(512)S(1)}, s32[512]{0:T(512)}, u32[]{:S(2)}) %copy-start.1) | copy-done | bytes 2072
  9.5 2.7 %shard_map.55 = (f32[1,512]{1,0:T(1,128)S(1)}, f32[1,512]{1,0:T(1,128)S(1)}, f32[128,512]{1,0:T(8,128)S(1)}, s32[4,512]{1,0:T(4,128)S(1)}, bf16[1024,128]{1,0:T(8,128)(2,1)S(1)}, /*index=5*/bf16[1024,128]{1,0:T(8,128)(2,1)S(1)}) custom-call(s32[4,128]{1,0:T(4,128)S(1)} %bitcast.9, s32[1,1]{1,0:T(1,128)} %bitcast.4.refs_1_, bf16[512,128]{1,0:T(8,128)(2,1)} %bitcast.7, ...), custom_call_target="tpu_custom_call" | custom-call | tf_op jit(solution)/shard_map/pallas_call | solution.py:279
  12.2 0.5 %collective-permute-done.2.refs_1_ = bf16[512,128]{1,0:T(8,128)(2,1)S(1)} collective-permute-done((bf16[512,128]{1,0:T(8,128)(2,1)}, bf16[512,128]{1,0:T(8,128)(2,1)S(1)}, u32[]{:S(2)}, u32[]{:S(2)}) %collective-permute-start.2) | collective-permute-done | bytes 131104 | tf_op jit(solution)/shard_map/ppermute | solution.py:215
  12.7 0.3 collective-permute-done.3.refs_1_
  13.1 1.5 %shard_map.56 = (f32[1,512]{1,0:T(1,128)S(1)}, f32[1,512]{1,0:T(1,128)S(1)}, f32[128,512]{1,0:T(8,128)S(1)}) custom-call(s32[4,512]{1,0:T(4,128)S(1)} %get-tuple-element.109.refs_0_, bf16[512,128]{1,0:T(8,128)(2,1)S(1)} %collective-permute-done.3.refs_1_, bf16[1024,128]{1,0:T(8,128)(2,1)S(1)} %get-tuple-element.69.refs_2_, ...), custom_call_target="tpu_custom_call" | custom-call | tf_op jit(solution)/shard_map/pallas_call | solution.py:279
  14.6 1.5 %shard_map.57 = (f32[1,512]{1,0:T(1,128)S(1)}, f32[1,512]{1,0:T(1,128)S(1)}, f32[128,512]{1,0:T(8,128)S(1)}) custom-call(s32[4,512]{1,0:T(4,128)S(1)} %get-tuple-element.109.refs_0_, bf16[512,128]{1,0:T(8,128)(2,1)S(1)} %collective-permute-done.2.refs_1_, bf16[1024,128]{1,0:T(8,128)(2,1)S(1)} %get-tuple-element.69.refs_2_, ...), custom_call_target="tpu_custom_call" | custom-call | tf_op jit(solution)/shard_map/pallas_call | solution.py:279
  16.1 0.0 collective-permute-done.4.refs_2_
  16.1 0.0 collective-permute-done.5.refs_3_
  16.1 0.1 collective-permute-start.7
  16.2 0.5 %collective-permute-start.8 = (bf16[1024,128]{1,0:T(8,128)(2,1)S(1)}, bf16[1024,128]{1,0:T(8,128)(2,1)S(1)}, u32[]{:S(2)}, u32[]{:S(2)}) collective-permute-start(bf16[1024,128]{1,0:T(8,128)(2,1)S(1)} %collective-permute-done.5.refs_3_), channel_id=1, source_target_pairs={{0,1},{1,0},{2,3},{3,2},{4,5},{5,4},{6,7},{7,6},{8,9},{9,8},{10,11... | collective-permute-start | bytes 786440 | tf_op jit(solution)/shard_map/ppermute | solution.py:215
  16.7 1.4 %collective-permute-start.6 = (bf16[512,128]{1,0:T(8,128)(2,1)S(1)}, bf16[512,128]{1,0:T(8,128)(2,1)S(1)}, u32[]{:S(2)}, u32[]{:S(2)}) collective-permute-start(bf16[512,128]{1,0:T(8,128)(2,1)S(1)} %collective-permute-done.2.refs_1_), channel_id=1, source_target_pairs={{0,4},{1,5},{2,6},{3,7},{4,0},{5,1},{6,2},{7,3},{8,12},{9,13},{10,... | collective-permute-start | bytes 393224 | tf_op jit(solution)/shard_map/ppermute | solution.py:215
  18.1 4.1 %collective-permute-done.6.refs_1_ = bf16[512,128]{1,0:T(8,128)(2,1)S(1)} collective-permute-done((bf16[512,128]{1,0:T(8,128)(2,1)S(1)}, bf16[512,128]{1,0:T(8,128)(2,1)S(1)}, u32[]{:S(2)}, u32[]{:S(2)}) %collective-permute-start.6) | collective-permute-done | bytes 131104 | tf_op jit(solution)/shard_map/ppermute | solution.py:215
  22.2 1.5 %shard_map.58 = (f32[1,512]{1,0:T(1,128)S(1)}, f32[1,512]{1,0:T(1,128)S(1)}, f32[128,512]{1,0:T(8,128)S(1)}) custom-call(s32[4,512]{1,0:T(4,128)S(1)} %get-tuple-element.109.refs_0_, bf16[512,128]{1,0:T(8,128)(2,1)S(1)} %collective-permute-done.6.refs_1_, bf16[1024,128]{1,0:T(8,128)(2,1)S(1)} %get-tuple-element.69.refs_2_, ...), custom_call_target="tpu_custom_call" | custom-call | tf_op jit(solution)/shard_map/pallas_call | solution.py:279
  23.7 0.0 collective-permute-done.7.refs_4_
  23.7 0.0 collective-permute-done.8.refs_5_
  23.7 1.6 %shard_map.59 = (bf16[136,256]{1,0:T(8,128)(2,1)S(1)}, bf16[136,256]{1,0:T(8,128)(2,1)S(1)}) custom-call(s32[4,512]{1,0:T(4,128)S(1)} %get-tuple-element.109.refs_0_, bf16[512,128]{1,0:T(8,128)(2,1)S(1)} %collective-permute-done.6.refs_1_, bf16[1024,128]{1,0:T(8,128)(2,1)S(1)} %collective-permute-done.4.refs_2_, ...), custom_call_target="tpu_custom_call" | custom-call | tf_op jit(solution)/shard_map/pallas_call | solution.py:279
  25.4 1.5 %collective-permute-start.9 = (bf16[136,256]{1,0:T(8,128)(2,1)S(1)}, bf16[136,256]{1,0:T(8,128)(2,1)S(1)}, u32[]{:S(2)}, u32[]{:S(2)}) collective-permute-start(bf16[136,256]{1,0:T(8,128)(2,1)S(1)} %get-tuple-element.104), channel_id=1, source_target_pairs={{0,4},{1,5},{2,6},{3,7},{4,0},{5,1},{6,2},{7,3},{8,12},{9,13},{10,... | collective-permute-start | bytes 208904 | tf_op jit(solution)/shard_map/ppermute | solution.py:215
  26.8 1.5 %shard_map.60 = (bf16[136,256]{1,0:T(8,128)(2,1)S(1)}, f32[128,256]{1,0:T(8,128)S(1)}, f32[1,256]{1,0:T(1,128)S(1)}) custom-call(s32[4,512]{1,0:T(4,128)S(1)} %get-tuple-element.109.refs_0_, bf16[512,128]{1,0:T(8,128)(2,1)S(1)} %collective-permute-done.2.refs_1_, bf16[1024,128]{1,0:T(8,128)(2,1)S(1)} %collective-permute-done.4.refs_2_, ...), custom_call_target="tpu_custom_call" | custom-call | tf_op jit(solution)/shard_map/pallas_call | solution.py:279
  28.4 1.6 %shard_map.61 = bf16[136,512]{1,0:T(8,128)(2,1)S(1)} custom-call(s32[4,512]{1,0:T(4,128)S(1)} %get-tuple-element.109.refs_0_, bf16[512,128]{1,0:T(8,128)(2,1)S(1)} %collective-permute-done.3.refs_1_, bf16[1024,128]{1,0:T(8,128)(2,1)S(1)} %collective-permute-done.4.refs_2_, bf16[1024,128]{1,0:T(8,128)(2,1)S(1)} %collective-permute-done.5.refs_3_, ...), custom_call_target="tpu_custom_call" | custom-call | tf_op jit(solution)/shard_map/pallas_call | solution.py:279
  30.0 0.0 copy-start
  30.0 0.7 %collective-permute-start.10 = (bf16[136,512]{1,0:T(8,128)(2,1)S(1)}, bf16[136,512]{1,0:T(8,128)(2,1)S(1)}, u32[]{:S(2)}, u32[]{:S(2)}) collective-permute-start(bf16[136,512]{1,0:T(8,128)(2,1)S(1)} %shard_map.61), channel_id=1, source_target_pairs={{0,4},{1,5},{2,6},{3,7},{4,0},{5,1},{6,2},{7,3},{8,12},{9,13},{10,... | collective-permute-start | bytes 417800 | tf_op jit(solution)/shard_map/ppermute | solution.py:215
  30.7 2.3 %collective-permute-start.11 = (bf16[136,256]{1,0:T(8,128)(2,1)S(1)}, bf16[136,256]{1,0:T(8,128)(2,1)S(1)}, u32[]{:S(2)}, u32[]{:S(2)}) collective-permute-start(bf16[136,256]{1,0:T(8,128)(2,1)S(1)} %get-tuple-element.118), channel_id=1, source_target_pairs={{0,8},{1,9},{2,10},{3,11},{4,12},{5,13},{6,14},{7,15},{8,0},{9,1},... | collective-permute-start | bytes 208904 | tf_op jit(solution)/shard_map/ppermute | solution.py:215
  33.0 1.4 %collective-permute-start.12 = (bf16[136,256]{1,0:T(8,128)(2,1)S(1)}, bf16[136,256]{1,0:T(8,128)(2,1)S(1)}, u32[]{:S(2)}, u32[]{:S(2)}) collective-permute-start(bf16[136,256]{1,0:T(8,128)(2,1)S(1)} %get-tuple-element.119), channel_id=1, source_target_pairs={{0,12},{1,13},{2,14},{3,15},{4,8},{5,9},{6,10},{7,11},{8,4},{9,5},... | collective-permute-start | bytes 208904 | tf_op jit(solution)/shard_map/ppermute | solution.py:215
  34.5 0.0 collective-permute-done.9.part_ref
  34.5 0.1 combine.1
  34.6 1.7 %collective-permute-start.13 = (bf16[136,256]{1,0:T(8,128)(2,1)S(1)}, bf16[136,256]{1,0:T(8,128)(2,1)S(1)}, u32[]{:S(2)}, u32[]{:S(2)}) collective-permute-start(bf16[136,256]{1,0:T(8,128)(2,1)S(1)} %combine.1), channel_id=1, source_target_pairs={{0,8},{1,9},{2,10},{3,11},{4,12},{5,13},{6,14},{7,15},{8,0},{9,1},... | collective-permute-start | bytes 208904 | tf_op jit(solution)/shard_map/ppermute | solution.py:215
  36.3 0.0 copy-done
  36.3 1.5 %shard_map.62 = (f32[128,512]{1,0:T(8,128)S(1)}, f32[1,512]{1,0:T(1,128)S(1)}) custom-call(s32[4,512]{1,0:T(4,128)S(1)} %get-tuple-element.109.refs_0_, bf16[512,128]{1,0:T(8,128)(2,1)S(1)} %bitcast.8, bf16[1024,128]{1,0:T(8,128)(2,1)S(1)} %collective-permute-done.4.refs_2_, bf16[1024,128]{1,0:T(8,128)(2,1)S(1)} %collective-permute-done.5.refs_3_, ...), custom_call_target="tpu_custom_call" | custom-call | tf_op jit(solution)/shard_map/pallas_call | solution.py:279
  37.8 3.2 %collective-permute-done.11.refs_3_ = bf16[136,256]{1,0:T(8,128)(2,1)S(1)} collective-permute-done((bf16[136,256]{1,0:T(8,128)(2,1)S(1)}, bf16[136,256]{1,0:T(8,128)(2,1)S(1)}, u32[]{:S(2)}, u32[]{:S(2)}) %collective-permute-start.11) | collective-permute-done | bytes 69664 | tf_op jit(solution)/shard_map/ppermute | solution.py:215
  41.0 0.0 collective-permute-done.12.refs_4_
  41.0 2.1 %collective-permute-done.13.refs_5_ = bf16[136,256]{1,0:T(8,128)(2,1)S(1)} collective-permute-done((bf16[136,256]{1,0:T(8,128)(2,1)S(1)}, bf16[136,256]{1,0:T(8,128)(2,1)S(1)}, u32[]{:S(2)}, u32[]{:S(2)}) %collective-permute-start.13) | collective-permute-done | bytes 69664 | tf_op jit(solution)/shard_map/ppermute | solution.py:215
  43.1 0.0 collective-permute-done.10.refs_2_
  43.1 1.0 %merge.1 = bf16[512,128]{1,0:T(8,128)(2,1)} custom-call(f32[128,512]{1,0:T(8,128)S(1)} %get-tuple-element.115.refs_0_, f32[1,512]{1,0:T(1,128)S(1)} %get-tuple-element.116.refs_1_, bf16[136,512]{1,0:T(8,128)(2,1)S(1)} %collective-permute-done.10.refs_2_, bf16[136,256]{1,0:T(8,128)(2,1)S(1)} %collective-permute-done.11.refs_3_, ...), custom_call_target="tpu_custom_call" | custom-call | tf_op jit(solution)/shard_map/merge/pallas_call | solution.py:369
Async XLA Ops:
  0.0 6.6 %collective-permute-start = (bf16[1024,128]{1,0:T(8,128)(2,1)}, bf16[1024,128]{1,0:T(8,128)(2,1)S(1)}, u32[]{:S(2)}, u32[]{:S(2)}) collective-permute-start(bf16[1024,128]{1,0:T(8,128)(2,1)} %refs_3_.1), channel_id=1, source_target_pairs={{0,1},{1,0},{2,3},{3,2},{4,5},{5,4},{6,7},{7,6},{8,9},{9,8},{10,11... | collective-permute-start | bytes 786440 | tf_op jit(solution)/shard_map/ppermute | solution.py:215
  0.5 8.4 %collective-permute-start.1 = (bf16[1024,128]{1,0:T(8,128)(2,1)}, bf16[1024,128]{1,0:T(8,128)(2,1)S(1)}, u32[]{:S(2)}, u32[]{:S(2)}) collective-permute-start(bf16[1024,128]{1,0:T(8,128)(2,1)} %refs_4_.1), channel_id=1, source_target_pairs={{0,1},{1,0},{2,3},{3,2},{4,5},{5,4},{6,7},{7,6},{8,9},{9,8},{10,11... | collective-permute-start | bytes 786440 | tf_op jit(solution)/shard_map/ppermute | solution.py:215
  0.5 15.6 %collective-permute-start.4 = (bf16[1024,128]{1,0:T(8,128)(2,1)}, bf16[1024,128]{1,0:T(8,128)(2,1)S(1)}, u32[]{:S(2)}, u32[]{:S(2)}) collective-permute-start(bf16[1024,128]{1,0:T(8,128)(2,1)} %refs_3_.1), channel_id=1, source_target_pairs={{0,2},{1,3},{2,0},{3,1},{4,6},{5,7},{6,4},{7,5},{8,10},{9,11},{10,... | collective-permute-start | bytes 786440 | tf_op jit(solution)/shard_map/ppermute | solution.py:215
  3.5 12.6 %collective-permute-start.5 = (bf16[1024,128]{1,0:T(8,128)(2,1)}, bf16[1024,128]{1,0:T(8,128)(2,1)S(1)}, u32[]{:S(2)}, u32[]{:S(2)}) collective-permute-start(bf16[1024,128]{1,0:T(8,128)(2,1)} %refs_4_.1), channel_id=1, source_target_pairs={{0,2},{1,3},{2,0},{3,1},{4,6},{5,7},{6,4},{7,5},{8,10},{9,11},{10,... | collective-permute-start | bytes 786440 | tf_op jit(solution)/shard_map/ppermute | solution.py:215
  3.5 9.2 %collective-permute-start.2 = (bf16[512,128]{1,0:T(8,128)(2,1)}, bf16[512,128]{1,0:T(8,128)(2,1)S(1)}, u32[]{:S(2)}, u32[]{:S(2)}) collective-permute-start(bf16[512,128]{1,0:T(8,128)(2,1)} %bitcast.5), channel_id=1, source_target_pairs={{0,8},{1,9},{2,10},{3,11},{4,12},{5,13},{6,14},{7,15},{8,0},{9,1},... | collective-permute-start | bytes 393224 | tf_op jit(solution)/shard_map/ppermute | solution.py:215
  6.6 6.5 %collective-permute-start.3 = (bf16[512,128]{1,0:T(8,128)(2,1)}, bf16[512,128]{1,0:T(8,128)(2,1)S(1)}, u32[]{:S(2)}, u32[]{:S(2)}) collective-permute-start(bf16[512,128]{1,0:T(8,128)(2,1)} %bitcast.6), channel_id=1, source_target_pairs={{0,4},{1,5},{2,6},{3,7},{4,0},{5,1},{6,2},{7,3},{8,12},{9,13},{10,... | collective-permute-start | bytes 393224 | tf_op jit(solution)/shard_map/ppermute | solution.py:215
  8.8 0.7 %copy-start.1 = (s32[512]{0:T(512)S(1)}, s32[512]{0:T(512)}, u32[]{:S(2)}) copy-start(s32[512]{0:T(512)} %param.9) | copy-start | bytes 6148
  16.1 7.6 %collective-permute-start.7 = (bf16[1024,128]{1,0:T(8,128)(2,1)S(1)}, bf16[1024,128]{1,0:T(8,128)(2,1)S(1)}, u32[]{:S(2)}, u32[]{:S(2)}) collective-permute-start(bf16[1024,128]{1,0:T(8,128)(2,1)S(1)} %collective-permute-done.4.refs_2_), channel_id=1, source_target_pairs={{0,1},{1,0},{2,3},{3,2},{4,5},{5,4},{6,7},{7,6},{8,9},{9,8},{10,11... | collective-permute-start | bytes 786440 | tf_op jit(solution)/shard_map/ppermute | solution.py:215
  16.2 7.5 %collective-permute-start.8 = (bf16[1024,128]{1,0:T(8,128)(2,1)S(1)}, bf16[1024,128]{1,0:T(8,128)(2,1)S(1)}, u32[]{:S(2)}, u32[]{:S(2)}) collective-permute-start(bf16[1024,128]{1,0:T(8,128)(2,1)S(1)} %collective-permute-done.5.refs_3_), channel_id=1, source_target_pairs={{0,1},{1,0},{2,3},{3,2},{4,5},{5,4},{6,7},{7,6},{8,9},{9,8},{10,11... | collective-permute-start | bytes 786440 | tf_op jit(solution)/shard_map/ppermute | solution.py:215
  16.7 5.5 %collective-permute-start.6 = (bf16[512,128]{1,0:T(8,128)(2,1)S(1)}, bf16[512,128]{1,0:T(8,128)(2,1)S(1)}, u32[]{:S(2)}, u32[]{:S(2)}) collective-permute-start(bf16[512,128]{1,0:T(8,128)(2,1)S(1)} %collective-permute-done.2.refs_1_), channel_id=1, source_target_pairs={{0,4},{1,5},{2,6},{3,7},{4,0},{5,1},{6,2},{7,3},{8,12},{9,13},{10,... | collective-permute-start | bytes 393224 | tf_op jit(solution)/shard_map/ppermute | solution.py:215
  25.4 9.1 %collective-permute-start.9 = (bf16[136,256]{1,0:T(8,128)(2,1)S(1)}, bf16[136,256]{1,0:T(8,128)(2,1)S(1)}, u32[]{:S(2)}, u32[]{:S(2)}) collective-permute-start(bf16[136,256]{1,0:T(8,128)(2,1)S(1)} %get-tuple-element.104), channel_id=1, source_target_pairs={{0,4},{1,5},{2,6},{3,7},{4,0},{5,1},{6,2},{7,3},{8,12},{9,13},{10,... | collective-permute-start | bytes 208904 | tf_op jit(solution)/shard_map/ppermute | solution.py:215
  30.0 6.3 %copy-start = (bf16[32,16,128]{2,1,0:T(8,128)(2,1)S(1)}, bf16[32,16,128]{2,1,0:T(8,128)(2,1)}, u32[]{:S(2)}) copy-start(bf16[32,16,128]{2,1,0:T(8,128)(2,1)} %param.5) | copy-start | bytes 393220
  30.0 13.1 %collective-permute-start.10 = (bf16[136,512]{1,0:T(8,128)(2,1)S(1)}, bf16[136,512]{1,0:T(8,128)(2,1)S(1)}, u32[]{:S(2)}, u32[]{:S(2)}) collective-permute-start(bf16[136,512]{1,0:T(8,128)(2,1)S(1)} %shard_map.61), channel_id=1, source_target_pairs={{0,4},{1,5},{2,6},{3,7},{4,0},{5,1},{6,2},{7,3},{8,12},{9,13},{10,... | collective-permute-start | bytes 417800 | tf_op jit(solution)/shard_map/ppermute | solution.py:215
  30.7 10.3 %collective-permute-start.11 = (bf16[136,256]{1,0:T(8,128)(2,1)S(1)}, bf16[136,256]{1,0:T(8,128)(2,1)S(1)}, u32[]{:S(2)}, u32[]{:S(2)}) collective-permute-start(bf16[136,256]{1,0:T(8,128)(2,1)S(1)} %get-tuple-element.118), channel_id=1, source_target_pairs={{0,8},{1,9},{2,10},{3,11},{4,12},{5,13},{6,14},{7,15},{8,0},{9,1},... | collective-permute-start | bytes 208904 | tf_op jit(solution)/shard_map/ppermute | solution.py:215
  33.0 8.0 %collective-permute-start.12 = (bf16[136,256]{1,0:T(8,128)(2,1)S(1)}, bf16[136,256]{1,0:T(8,128)(2,1)S(1)}, u32[]{:S(2)}, u32[]{:S(2)}) collective-permute-start(bf16[136,256]{1,0:T(8,128)(2,1)S(1)} %get-tuple-element.119), channel_id=1, source_target_pairs={{0,12},{1,13},{2,14},{3,15},{4,8},{5,9},{6,10},{7,11},{8,4},{9,5},... | collective-permute-start | bytes 208904 | tf_op jit(solution)/shard_map/ppermute | solution.py:215
  34.6 8.5 %collective-permute-start.13 = (bf16[136,256]{1,0:T(8,128)(2,1)S(1)}, bf16[136,256]{1,0:T(8,128)(2,1)S(1)}, u32[]{:S(2)}, u32[]{:S(2)}) collective-permute-start(bf16[136,256]{1,0:T(8,128)(2,1)S(1)} %combine.1), channel_id=1, source_target_pairs={{0,8},{1,9},{2,10},{3,11},{4,12},{5,13},{6,14},{7,15},{8,0},{9,1},... | collective-permute-start | bytes 208904 | tf_op jit(solution)/shard_map/ppermute | solution.py:215

commit v2 on v1

--- a/solution.py
+++ b/solution.py
@@ -181,13 +181,6 @@
     return value, top + jnp.log2(total)
 
 
-def combine_kernel(value_ref, level_ref, part_ref, out_ref):
-    width, lanes = value_ref.shape
-    value, level = decode(part_ref[:width, :], part_ref[width:, :])
-    value, level = combine([value_ref[...], value], [level_ref[...], level])
-    write_partial([out_ref], "code", slice(0, lanes), value, level)
-
-
 def merge_kernel(groups, *refs):
     own_ref, own_level_ref = refs[:2]
     parts, out_ref = refs[2:-1], refs[-1]
@@ -315,57 +308,31 @@
     (got[source],) = hold(got[source])
     gather(last)
     ready(last)
-    for index in range(1, last):
+    for index in range(last - 1, 0, -1):
         attend(index, [0, 1])
     far_pair = hold(*far_pair)
     pairs += [far_pair, [swap(array, 1) for array in far_pair]]
     attend(last, [0, 1])
     own_plan = [(at, "float", 0, at * tile, tile) for at in tiles]
-    if outer == 4 and stage_rows == 2 * tile:
-        halves = [slice(0, tile), slice(tile, 2 * tile)]
-        plan = [(0, "code", 0, 0, tile), (1, "code", 1, 0, tile)]
-        direct, handed = attend(3, [2, 3], plan, [packed_shape(tile)] * 2)
-        handed = swap(handed, inner)
-        third = swap(direct, 3 * inner)
-        plan = [(0, "code", 0, 0, tile), (1, "float", 1, 0, tile)]
-        direct, value, level = attend(2, [2, 3], plan, [packed_shape(tile)] + float_shapes(tile))
-        second = swap(direct, 2 * inner)
-        (packed,) = attend(1, [2, 3], whole_plan, [packed_shape(stage_rows)])
-        first = swap(packed, inner)
-        (handed,) = hold(handed)
-        joined = pl.pallas_call(
-            combine_kernel,
-            in_specs=[vmem] * 3,
-            out_specs=vmem,
-            out_shape=packed_shape(tile),
-            compiler_params=params,
-            name="combine",
-        )(value, level, handed)
-        (joined,) = hold(joined)
-        joined = swap(joined, 2 * inner)
-        own = attend(0, [2, 3], own_plan, float_shapes(stage_rows))
-        parts = [first, second, third, joined]
-        groups = [(halves[0], [(0, 0), (1, 0), (2, 0)]), (halves[1], [(0, tile), (3, 0)])]
+    parts = []
+
+    def send(index, packed):
+        for at, k in enumerate(stages[index]):
+            if k:
+                piece = packed if per_stage == 1 else packed[:, at * rows : (at + 1) * rows]
+                parts.append(swap(piece, inner * k))
+
+    for index in range(last, 0, -1):
+        send(index, attend(index, [2, 3], whole_plan, [packed_shape(stage_rows)])[0])
+    if per_stage == 1:
+        own = attend(0, [2, 3], own_plan, float_shapes(rows))
     else:
-        parts = []
-
-        def send(index, packed):
-            for at, k in enumerate(stages[index]):
-                if k:
-                    piece = packed if per_stage == 1 else packed[:, at * rows : (at + 1) * rows]
-                    parts.append(swap(piece, inner * k))
-
-        for index in range(last, 0, -1):
-            send(index, attend(index, [2, 3], whole_plan, [packed_shape(stage_rows)])[0])
-        if per_stage == 1:
-            own = attend(0, [2, 3], own_plan, float_shapes(rows))
-        else:
-            own_plan = [(0, "float", 1, 0, rows)]
-            packed, *own = attend(
-                0, [2, 3], whole_plan + own_plan, [packed_shape(stage_rows)] + float_shapes(rows)
-            )
-            send(0, packed)
-        groups = [(slice(0, rows), [(at, 0) for at in range(len(parts))])]
+        own_plan = [(0, "float", 1, 0, rows)]
+        packed, *own = attend(
+            0, [2, 3], whole_plan + own_plan, [packed_shape(stage_rows)] + float_shapes(rows)
+        )
+        send(0, packed)
+    groups = [(slice(0, rows), [(at, 0) for at in range(len(parts))])]
     merged = pl.pallas_call(
         functools.partial(merge_kernel, groups),
         in_specs=[vmem] * (2 + len(parts)),

time: 44.3 us -> 44.1 us (level)
  starting transfers between devices: 17.7 us -> 14.9 us
  waiting for transfers between devices: 10.3 us -> 12.8 us
    ppermute x14 -> x12, starting transfers between devices: 17.7 us -> 14.9 us  [swap(): return lax.ppermute(array, 'ctx', [(i, i ^ step) for i in range(size)])]
    ppermute x14 -> x12, waiting for transfers between devices: 10.3 us -> 12.8 us  [swap(): return lax.ppermute(array, 'ctx', [(i, i ^ step) for i in range(size)])]
  transfers between devices with their start and end apart: 14 -> 12, of which waited for: 5 -> 4; matrix products, arithmetic and copies ran while one was open for 0% -> 0% of each run, Pallas kernels for 27% -> 20%
where the time goes in v2:
time: 44.1 us; the launch traced here: 43.9 us
  starting transfers between devices  14.9 us (34%)
  Pallas kernels  14.7 us (33%)
  waiting for transfers between devices  12.8 us (29%)
  between operations  0.79 us (2%)
  local copies, waits for them, and re-layouts  0.67 us (2%)
    ppermute x12, starting transfers between devices, swap(): return lax.ppermute(array, 'ctx', [(i, i ^ step) for i in range(size)])  14.9 us
    pallas_call x8, Pallas kernels, attend(): pl.pallas_call(functools.partial(attend_kernel, scale, index, blocks, sta...  13.6 us
    ppermute x12, waiting for transfers between devices, swap(): return lax.ppermute(array, 'ctx', [(i, i ^ step) for i in range(size)])  12.8 us
    pallas_call x1, Pallas kernels, local(): pl.pallas_call(functools.partial(merge_kernel, groups), in_specs=[vmem] *...  1.03 us
  transfers between devices with their start and end apart: 12, of which 4 were waited for; matrix products, arithmetic and copies ran while one was open for 0% of the time, Pallas kernels for 20%

profile of v2, /device:TPU:0, one launch (start us, length us, event | category | flops | bytes accessed | tf_op | source)
XLA Modules:
  0.0 43.9 jit_solution(11631149166241808647)
XLA Ops:
  0.0 0.5 %collective-permute-start = (bf16[1024,128]{1,0:T(8,128)(2,1)}, bf16[1024,128]{1,0:T(8,128)(2,1)S(1)}, u32[]{:S(2)}, u32[]{:S(2)}) collective-permute-start(bf16[1024,128]{1,0:T(8,128)(2,1)} %refs_3_.1), channel_id=1, source_target_pairs={{0,1},{1,0},{2,3},{3,2},{4,5},{5,4},{6,7},{7,6},{8,9},{9,8},{10,11... | collective-permute-start | bytes 786440 | tf_op jit(solution)/shard_map/ppermute | solution.py:208
  0.5 0.0 collective-permute-start.1
  0.5 3.0 %collective-permute-start.4 = (bf16[1024,128]{1,0:T(8,128)(2,1)}, bf16[1024,128]{1,0:T(8,128)(2,1)S(1)}, u32[]{:S(2)}, u32[]{:S(2)}) collective-permute-start(bf16[1024,128]{1,0:T(8,128)(2,1)} %refs_3_.1), channel_id=1, source_target_pairs={{0,2},{1,3},{2,0},{3,1},{4,6},{5,7},{6,4},{7,5},{8,10},{9,11},{10,... | collective-permute-start | bytes 786440 | tf_op jit(solution)/shard_map/ppermute | solution.py:208
  3.5 0.0 collective-permute-start.5
  3.5 3.1 %collective-permute-start.2 = (bf16[512,128]{1,0:T(8,128)(2,1)}, bf16[512,128]{1,0:T(8,128)(2,1)S(1)}, u32[]{:S(2)}, u32[]{:S(2)}) collective-permute-start(bf16[512,128]{1,0:T(8,128)(2,1)} %bitcast.5), channel_id=1, source_target_pairs={{0,8},{1,9},{2,10},{3,11},{4,12},{5,13},{6,14},{7,15},{8,0},{9,1},... | collective-permute-start | bytes 393224 | tf_op jit(solution)/shard_map/ppermute | solution.py:208
  6.6 0.0 collective-permute-done.refs_5_.refs_4_
  6.6 1.6 %collective-permute-start.3 = (bf16[512,128]{1,0:T(8,128)(2,1)}, bf16[512,128]{1,0:T(8,128)(2,1)S(1)}, u32[]{:S(2)}, u32[]{:S(2)}) collective-permute-start(bf16[512,128]{1,0:T(8,128)(2,1)} %bitcast.6), channel_id=1, source_target_pairs={{0,4},{1,5},{2,6},{3,7},{4,0},{5,1},{6,2},{7,3},{8,12},{9,13},{10,... | collective-permute-start | bytes 393224 | tf_op jit(solution)/shard_map/ppermute | solution.py:208
  8.8 0.0 copy-start.1
  8.8 0.0 collective-permute-done.1.refs_6_.refs_5_
  8.9 0.7 %copy-done.1 = s32[512]{0:T(512)S(1)} copy-done((s32[512]{0:T(512)S(1)}, s32[512]{0:T(512)}, u32[]{:S(2)}) %copy-start.1) | copy-done | bytes 2072
  9.5 2.7 %shard_map.55 = (f32[1,512]{1,0:T(1,128)S(1)}, f32[1,512]{1,0:T(1,128)S(1)}, f32[128,512]{1,0:T(8,128)S(1)}, s32[4,512]{1,0:T(4,128)S(1)}, bf16[1024,128]{1,0:T(8,128)(2,1)S(1)}, /*index=5*/bf16[1024,128]{1,0:T(8,128)(2,1)S(1)}) custom-call(s32[4,128]{1,0:T(4,128)S(1)} %bitcast.9, s32[1,1]{1,0:T(1,128)} %bitcast.4.refs_1_, bf16[512,128]{1,0:T(8,128)(2,1)} %bitcast.7, ...), custom_call_target="tpu_custom_call" | custom-call | tf_op jit(solution)/shard_map/pallas_call | solution.py:272
  12.2 0.5 %collective-permute-done.2.refs_1_ = bf16[512,128]{1,0:T(8,128)(2,1)S(1)} collective-permute-done((bf16[512,128]{1,0:T(8,128)(2,1)}, bf16[512,128]{1,0:T(8,128)(2,1)S(1)}, u32[]{:S(2)}, u32[]{:S(2)}) %collective-permute-start.2) | collective-permute-done | bytes 131104 | tf_op jit(solution)/shard_map/ppermute | solution.py:208
  12.7 1.5 %shard_map.56 = (f32[1,512]{1,0:T(1,128)S(1)}, f32[1,512]{1,0:T(1,128)S(1)}, f32[128,512]{1,0:T(8,128)S(1)}) custom-call(s32[4,512]{1,0:T(4,128)S(1)} %get-tuple-element.86.refs_0_, bf16[512,128]{1,0:T(8,128)(2,1)S(1)} %collective-permute-done.2.refs_1_, bf16[1024,128]{1,0:T(8,128)(2,1)S(1)} %get-tuple-element.57.refs_2_, ...), custom_call_target="tpu_custom_call" | custom-call | tf_op jit(solution)/shard_map/pallas_call | solution.py:272
  14.2 0.0 collective-permute-done.3.refs_1_
  14.3 1.5 %shard_map.57 = (f32[1,512]{1,0:T(1,128)S(1)}, f32[1,512]{1,0:T(1,128)S(1)}, f32[128,512]{1,0:T(8,128)S(1)}) custom-call(s32[4,512]{1,0:T(4,128)S(1)} %get-tuple-element.86.refs_0_, bf16[512,128]{1,0:T(8,128)(2,1)S(1)} %collective-permute-done.3.refs_1_, bf16[1024,128]{1,0:T(8,128)(2,1)S(1)} %get-tuple-element.57.refs_2_, ...), custom_call_target="tpu_custom_call" | custom-call | tf_op jit(solution)/shard_map/pallas_call | solution.py:272
  15.8 0.0 collective-permute-done.4.refs_2_
  15.8 0.0 collective-permute-done.5.refs_3_
  15.8 0.1 collective-permute-start.7
  15.9 0.5 %collective-permute-start.8 = (bf16[1024,128]{1,0:T(8,128)(2,1)S(1)}, bf16[1024,128]{1,0:T(8,128)(2,1)S(1)}, u32[]{:S(2)}, u32[]{:S(2)}) collective-permute-start(bf16[1024,128]{1,0:T(8,128)(2,1)S(1)} %collective-permute-done.5.refs_3_), channel_id=1, source_target_pairs={{0,1},{1,0},{2,3},{3,2},{4,5},{5,4},{6,7},{7,6},{8,9},{9,8},{10,11... | collective-permute-start | bytes 786440 | tf_op jit(solution)/shard_map/ppermute | solution.py:208
  16.4 1.7 %collective-permute-start.6 = (bf16[512,128]{1,0:T(8,128)(2,1)S(1)}, bf16[512,128]{1,0:T(8,128)(2,1)S(1)}, u32[]{:S(2)}, u32[]{:S(2)}) collective-permute-start(bf16[512,128]{1,0:T(8,128)(2,1)S(1)} %collective-permute-done.2.refs_1_), channel_id=1, source_target_pairs={{0,4},{1,5},{2,6},{3,7},{4,0},{5,1},{6,2},{7,3},{8,12},{9,13},{10,... | collective-permute-start | bytes 393224 | tf_op jit(solution)/shard_map/ppermute | solution.py:208
  18.1 3.7 %collective-permute-done.6.refs_1_ = bf16[512,128]{1,0:T(8,128)(2,1)S(1)} collective-permute-done((bf16[512,128]{1,0:T(8,128)(2,1)S(1)}, bf16[512,128]{1,0:T(8,128)(2,1)S(1)}, u32[]{:S(2)}, u32[]{:S(2)}) %collective-permute-start.6) | collective-permute-done | bytes 131104 | tf_op jit(solution)/shard_map/ppermute | solution.py:208
  21.9 1.5 %shard_map.58 = (f32[1,512]{1,0:T(1,128)S(1)}, f32[1,512]{1,0:T(1,128)S(1)}, f32[128,512]{1,0:T(8,128)S(1)}) custom-call(s32[4,512]{1,0:T(4,128)S(1)} %get-tuple-element.86.refs_0_, bf16[512,128]{1,0:T(8,128)(2,1)S(1)} %collective-permute-done.6.refs_1_, bf16[1024,128]{1,0:T(8,128)(2,1)S(1)} %get-tuple-element.57.refs_2_, ...), custom_call_target="tpu_custom_call" | custom-call | tf_op jit(solution)/shard_map/pallas_call | solution.py:272
  23.4 0.0 collective-permute-done.7.refs_4_
  23.4 0.0 collective-permute-done.8.refs_5_
  23.4 1.6 %shard_map.59 = bf16[136,512]{1,0:T(8,128)(2,1)S(1)} custom-call(s32[4,512]{1,0:T(4,128)S(1)} %get-tuple-element.86.refs_0_, bf16[512,128]{1,0:T(8,128)(2,1)S(1)} %collective-permute-done.6.refs_1_, bf16[1024,128]{1,0:T(8,128)(2,1)S(1)} %collective-permute-done.4.refs_2_, bf16[1024,128]{1,0:T(8,128)(2,1)S(1)} %collective-permute-done.5.refs_3_, ...), custom_call_target="tpu_custom_call" | custom-call | tf_op jit(solution)/shard_map/pallas_call | solution.py:272
  25.0 1.6 %shard_map.60 = bf16[136,512]{1,0:T(8,128)(2,1)S(1)} custom-call(s32[4,512]{1,0:T(4,128)S(1)} %get-tuple-element.86.refs_0_, bf16[512,128]{1,0:T(8,128)(2,1)S(1)} %collective-permute-done.2.refs_1_, bf16[1024,128]{1,0:T(8,128)(2,1)S(1)} %collective-permute-done.4.refs_2_, bf16[1024,128]{1,0:T(8,128)(2,1)S(1)} %collective-permute-done.5.refs_3_, ...), custom_call_target="tpu_custom_call" | custom-call | tf_op jit(solution)/shard_map/pallas_call | solution.py:272
  26.7 0.0 copy-start
  26.7 1.6 %shard_map.61 = bf16[136,512]{1,0:T(8,128)(2,1)S(1)} custom-call(s32[4,512]{1,0:T(4,128)S(1)} %get-tuple-element.86.refs_0_, bf16[512,128]{1,0:T(8,128)(2,1)S(1)} %collective-permute-done.3.refs_1_, bf16[1024,128]{1,0:T(8,128)(2,1)S(1)} %collective-permute-done.4.refs_2_, bf16[1024,128]{1,0:T(8,128)(2,1)S(1)} %collective-permute-done.5.refs_3_, ...), custom_call_target="tpu_custom_call" | custom-call | tf_op jit(solution)/shard_map/pallas_call | solution.py:272
  28.3 1.7 %collective-permute-start.11 = (bf16[136,512]{1,0:T(8,128)(2,1)S(1)}, bf16[136,512]{1,0:T(8,128)(2,1)S(1)}, u32[]{:S(2)}, u32[]{:S(2)}) collective-permute-start(bf16[136,512]{1,0:T(8,128)(2,1)S(1)} %shard_map.61), channel_id=1, source_target_pairs={{0,4},{1,5},{2,6},{3,7},{4,0},{5,1},{6,2},{7,3},{8,12},{9,13},{10,... | collective-permute-start | bytes 417800 | tf_op jit(solution)/shard_map/ppermute | solution.py:208
  30.0 2.6 %collective-permute-start.10 = (bf16[136,512]{1,0:T(8,128)(2,1)S(1)}, bf16[136,512]{1,0:T(8,128)(2,1)S(1)}, u32[]{:S(2)}, u32[]{:S(2)}) collective-permute-start(bf16[136,512]{1,0:T(8,128)(2,1)S(1)} %shard_map.60), channel_id=1, source_target_pairs={{0,8},{1,9},{2,10},{3,11},{4,12},{5,13},{6,14},{7,15},{8,0},{9,1},... | collective-permute-start | bytes 417800 | tf_op jit(solution)/shard_map/ppermute | solution.py:208
  32.6 0.1 collective-permute-start.9
  32.7 0.0 copy-done
  32.8 1.5 %shard_map.62 = (f32[128,512]{1,0:T(8,128)S(1)}, f32[1,512]{1,0:T(1,128)S(1)}) custom-call(s32[4,512]{1,0:T(4,128)S(1)} %get-tuple-element.86.refs_0_, bf16[512,128]{1,0:T(8,128)(2,1)S(1)} %bitcast.8, bf16[1024,128]{1,0:T(8,128)(2,1)S(1)} %collective-permute-done.4.refs_2_, bf16[1024,128]{1,0:T(8,128)(2,1)S(1)} %collective-permute-done.5.refs_3_, ...), custom_call_target="tpu_custom_call" | custom-call | tf_op jit(solution)/shard_map/pallas_call | solution.py:272
  34.3 0.8 %collective-permute-done.11.refs_4_ = bf16[136,512]{1,0:T(8,128)(2,1)S(1)} collective-permute-done((bf16[136,512]{1,0:T(8,128)(2,1)S(1)}, bf16[136,512]{1,0:T(8,128)(2,1)S(1)}, u32[]{:S(2)}, u32[]{:S(2)}) %collective-permute-start.11) | collective-permute-done | bytes 139296 | tf_op jit(solution)/shard_map/ppermute | solution.py:208
  35.1 7.8 %collective-permute-done.10.refs_3_ = bf16[136,512]{1,0:T(8,128)(2,1)S(1)} collective-permute-done((bf16[136,512]{1,0:T(8,128)(2,1)S(1)}, bf16[136,512]{1,0:T(8,128)(2,1)S(1)}, u32[]{:S(2)}, u32[]{:S(2)}) %collective-permute-start.10) | collective-permute-done | bytes 139296 | tf_op jit(solution)/shard_map/ppermute | solution.py:208
  42.9 0.0 collective-permute-done.9.refs_2_
  42.9 1.0 %merge.1 = bf16[512,128]{1,0:T(8,128)(2,1)} custom-call(f32[128,512]{1,0:T(8,128)S(1)} %get-tuple-element.92.refs_0_, f32[1,512]{1,0:T(1,128)S(1)} %get-tuple-element.93.refs_1_, bf16[136,512]{1,0:T(8,128)(2,1)S(1)} %collective-permute-done.9.refs_2_, bf16[136,512]{1,0:T(8,128)(2,1)S(1)} %collective-permute-done.10.refs_3_, ...), custom_call_target="tpu_custom_call" | custom-call | tf_op jit(solution)/shard_map/merge/pallas_call | solution.py:336
Async XLA Ops:
  0.0 6.6 %collective-permute-start = (bf16[1024,128]{1,0:T(8,128)(2,1)}, bf16[1024,128]{1,0:T(8,128)(2,1)S(1)}, u32[]{:S(2)}, u32[]{:S(2)}) collective-permute-start(bf16[1024,128]{1,0:T(8,128)(2,1)} %refs_3_.1), channel_id=1, source_target_pairs={{0,1},{1,0},{2,3},{3,2},{4,5},{5,4},{6,7},{7,6},{8,9},{9,8},{10,11... | collective-permute-start | bytes 786440 | tf_op jit(solution)/shard_map/ppermute | solution.py:208
  0.5 8.4 %collective-permute-start.1 = (bf16[1024,128]{1,0:T(8,128)(2,1)}, bf16[1024,128]{1,0:T(8,128)(2,1)S(1)}, u32[]{:S(2)}, u32[]{:S(2)}) collective-permute-start(bf16[1024,128]{1,0:T(8,128)(2,1)} %refs_4_.1), channel_id=1, source_target_pairs={{0,1},{1,0},{2,3},{3,2},{4,5},{5,4},{6,7},{7,6},{8,9},{9,8},{10,11... | collective-permute-start | bytes 786440 | tf_op jit(solution)/shard_map/ppermute | solution.py:208
  0.5 15.3 %collective-permute-start.4 = (bf16[1024,128]{1,0:T(8,128)(2,1)}, bf16[1024,128]{1,0:T(8,128)(2,1)S(1)}, u32[]{:S(2)}, u32[]{:S(2)}) collective-permute-start(bf16[1024,128]{1,0:T(8,128)(2,1)} %refs_3_.1), channel_id=1, source_target_pairs={{0,2},{1,3},{2,0},{3,1},{4,6},{5,7},{6,4},{7,5},{8,10},{9,11},{10,... | collective-permute-start | bytes 786440 | tf_op jit(solution)/shard_map/ppermute | solution.py:208
  3.5 12.3 %collective-permute-start.5 = (bf16[1024,128]{1,0:T(8,128)(2,1)}, bf16[1024,128]{1,0:T(8,128)(2,1)S(1)}, u32[]{:S(2)}, u32[]{:S(2)}) collective-permute-start(bf16[1024,128]{1,0:T(8,128)(2,1)} %refs_4_.1), channel_id=1, source_target_pairs={{0,2},{1,3},{2,0},{3,1},{4,6},{5,7},{6,4},{7,5},{8,10},{9,11},{10,... | collective-permute-start | bytes 786440 | tf_op jit(solution)/shard_map/ppermute | solution.py:208
  3.5 9.2 %collective-permute-start.2 = (bf16[512,128]{1,0:T(8,128)(2,1)}, bf16[512,128]{1,0:T(8,128)(2,1)S(1)}, u32[]{:S(2)}, u32[]{:S(2)}) collective-permute-start(bf16[512,128]{1,0:T(8,128)(2,1)} %bitcast.5), channel_id=1, source_target_pairs={{0,8},{1,9},{2,10},{3,11},{4,12},{5,13},{6,14},{7,15},{8,0},{9,1},... | collective-permute-start | bytes 393224 | tf_op jit(solution)/shard_map/ppermute | solution.py:208
  6.6 7.6 %collective-permute-start.3 = (bf16[512,128]{1,0:T(8,128)(2,1)}, bf16[512,128]{1,0:T(8,128)(2,1)S(1)}, u32[]{:S(2)}, u32[]{:S(2)}) collective-permute-start(bf16[512,128]{1,0:T(8,128)(2,1)} %bitcast.6), channel_id=1, source_target_pairs={{0,4},{1,5},{2,6},{3,7},{4,0},{5,1},{6,2},{7,3},{8,12},{9,13},{10,... | collective-permute-start | bytes 393224 | tf_op jit(solution)/shard_map/ppermute | solution.py:208
  8.8 0.7 %copy-start.1 = (s32[512]{0:T(512)S(1)}, s32[512]{0:T(512)}, u32[]{:S(2)}) copy-start(s32[512]{0:T(512)} %param.9) | copy-start | bytes 6148
  15.8 7.6 %collective-permute-start.7 = (bf16[1024,128]{1,0:T(8,128)(2,1)S(1)}, bf16[1024,128]{1,0:T(8,128)(2,1)S(1)}, u32[]{:S(2)}, u32[]{:S(2)}) collective-permute-start(bf16[1024,128]{1,0:T(8,128)(2,1)S(1)} %collective-permute-done.4.refs_2_), channel_id=1, source_target_pairs={{0,1},{1,0},{2,3},{3,2},{4,5},{5,4},{6,7},{7,6},{8,9},{9,8},{10,11... | collective-permute-start | bytes 786440 | tf_op jit(solution)/shard_map/ppermute | solution.py:208
  15.9 7.5 %collective-permute-start.8 = (bf16[1024,128]{1,0:T(8,128)(2,1)S(1)}, bf16[1024,128]{1,0:T(8,128)(2,1)S(1)}, u32[]{:S(2)}, u32[]{:S(2)}) collective-permute-start(bf16[1024,128]{1,0:T(8,128)(2,1)S(1)} %collective-permute-done.5.refs_3_), channel_id=1, source_target_pairs={{0,1},{1,0},{2,3},{3,2},{4,5},{5,4},{6,7},{7,6},{8,9},{9,8},{10,11... | collective-permute-start | bytes 786440 | tf_op jit(solution)/shard_map/ppermute | solution.py:208
  16.4 5.5 %collective-permute-start.6 = (bf16[512,128]{1,0:T(8,128)(2,1)S(1)}, bf16[512,128]{1,0:T(8,128)(2,1)S(1)}, u32[]{:S(2)}, u32[]{:S(2)}) collective-permute-start(bf16[512,128]{1,0:T(8,128)(2,1)S(1)} %collective-permute-done.2.refs_1_), channel_id=1, source_target_pairs={{0,4},{1,5},{2,6},{3,7},{4,0},{5,1},{6,2},{7,3},{8,12},{9,13},{10,... | collective-permute-start | bytes 393224 | tf_op jit(solution)/shard_map/ppermute | solution.py:208
  26.7 6.1 %copy-start = (bf16[32,16,128]{2,1,0:T(8,128)(2,1)S(1)}, bf16[32,16,128]{2,1,0:T(8,128)(2,1)}, u32[]{:S(2)}) copy-start(bf16[32,16,128]{2,1,0:T(8,128)(2,1)} %param.5) | copy-start | bytes 393220
  28.3 6.8 %collective-permute-start.11 = (bf16[136,512]{1,0:T(8,128)(2,1)S(1)}, bf16[136,512]{1,0:T(8,128)(2,1)S(1)}, u32[]{:S(2)}, u32[]{:S(2)}) collective-permute-start(bf16[136,512]{1,0:T(8,128)(2,1)S(1)} %shard_map.61), channel_id=1, source_target_pairs={{0,4},{1,5},{2,6},{3,7},{4,0},{5,1},{6,2},{7,3},{8,12},{9,13},{10,... | collective-permute-start | bytes 417800 | tf_op jit(solution)/shard_map/ppermute | solution.py:208
  30.0 12.8 %collective-permute-start.10 = (bf16[136,512]{1,0:T(8,128)(2,1)S(1)}, bf16[136,512]{1,0:T(8,128)(2,1)S(1)}, u32[]{:S(2)}, u32[]{:S(2)}) collective-permute-start(bf16[136,512]{1,0:T(8,128)(2,1)S(1)} %shard_map.60), channel_id=1, source_target_pairs={{0,8},{1,9},{2,10},{3,11},{4,12},{5,13},{6,14},{7,15},{8,0},{9,1},... | collective-permute-start | bytes 417800 | tf_op jit(solution)/shard_map/ppermute | solution.py:208
  32.6 10.3 %collective-permute-start.9 = (bf16[136,512]{1,0:T(8,128)(2,1)S(1)}, bf16[136,512]{1,0:T(8,128)(2,1)S(1)}, u32[]{:S(2)}, u32[]{:S(2)}) collective-permute-start(bf16[136,512]{1,0:T(8,128)(2,1)S(1)} %shard_map.59), channel_id=1, source_target_pairs={{0,12},{1,13},{2,14},{3,15},{4,8},{5,9},{6,10},{7,11},{8,4},{9,5},... | collective-permute-start | bytes 417800 | tf_op jit(solution)/shard_map/ppermute | solution.py:208

commit v3 on v2

--- a/solution.py
+++ b/solution.py
@@ -304,15 +304,18 @@
         gather(index)
         ready(index)
     attend(0, [0, 1])
+    for index in range(1, last - 1):
+        attend(index, [0, 1])
     source = stages[last][0] ^ (stages[last][0] & -stages[last][0])
     (got[source],) = hold(got[source])
     gather(last)
     ready(last)
-    for index in range(last - 1, 0, -1):
-        attend(index, [0, 1])
-    far_pair = hold(*far_pair)
-    pairs += [far_pair, [swap(array, 1) for array in far_pair]]
-    attend(last, [0, 1])
+    far_pair[0], = hold(far_pair[0])
+    across_keys = swap(far_pair[0], 1)
+    attend(last - 1, [0, 1])
+    far_pair[1], = hold(far_pair[1])
+    across_values = swap(far_pair[1], 1)
+    pairs += [far_pair, [across_keys, across_values]]
     own_plan = [(at, "float", 0, at * tile, tile) for at in tiles]
     parts = []
 
@@ -322,8 +325,12 @@
                 piece = packed if per_stage == 1 else packed[:, at * rows : (at + 1) * rows]
                 parts.append(swap(piece, inner * k))
 
-    for index in range(last, 0, -1):
-        send(index, attend(index, [2, 3], whole_plan, [packed_shape(stage_rows)])[0])
+    coded = [packed_shape(stage_rows)]
+    attend(last - 1, [2])
+    send(last - 1, attend(last - 1, [3], whole_plan, coded)[0])
+    send(last, attend(last, [0, 1, 2, 3], whole_plan, coded)[0])
+    for index in range(last - 2, 0, -1):
+        send(index, attend(index, [2, 3], whole_plan, coded)[0])
     if per_stage == 1:
         own = attend(0, [2, 3], own_plan, float_shapes(rows))
     else:

time: 44.1 us -> 43.5 us (0.986)
  waiting for transfers between devices: 12.8 us -> 12.3 us
    ppermute x12, waiting for transfers between devices: 12.8 us -> 12.3 us  [swap(): return lax.ppermute(array, 'ctx', [(i, i ^ step) for i in range(size)])]
  transfers between devices with their start and end apart: 12 -> 12, of which waited for: 4 -> 5; matrix products, arithmetic and copies ran while one was open for 0% -> 0% of each run, Pallas kernels for 20% -> 21%
where the time goes in v3:
time: 43.5 us; the launch traced here: 43.4 us
  starting transfers between devices  14.9 us (34%)
  Pallas kernels  14.7 us (34%)
  waiting for transfers between devices  12.3 us (28%)
  between operations  0.78 us (2%)
  local copies, waits for them, and re-layouts  0.67 us (2%)
    ppermute x12, starting transfers between devices, swap(): return lax.ppermute(array, 'ctx', [(i, i ^ step) for i in range(size)])  14.9 us
    pallas_call x8, Pallas kernels, attend(): pl.pallas_call(functools.partial(attend_kernel, scale, index, blocks, sta...  13.6 us
    ppermute x12, waiting for transfers between devices, swap(): return lax.ppermute(array, 'ctx', [(i, i ^ step) for i in range(size)])  12.3 us
    pallas_call x1, Pallas kernels, local(): pl.pallas_call(functools.partial(merge_kernel, groups), in_specs=[vmem] *...  1.03 us
  transfers between devices with their start and end apart: 12, of which 5 were waited for; matrix products, arithmetic and copies ran while one was open for 0% of the time, Pallas kernels for 21%

profile of v3, /device:TPU:0, one launch (start us, length us, event | category | flops | bytes accessed | tf_op | source)
XLA Modules:
  0.0 43.4 jit_solution(15201991066135633399)
XLA Ops:
  0.0 0.5 %collective-permute-start = (bf16[1024,128]{1,0:T(8,128)(2,1)}, bf16[1024,128]{1,0:T(8,128)(2,1)S(1)}, u32[]{:S(2)}, u32[]{:S(2)}) collective-permute-start(bf16[1024,128]{1,0:T(8,128)(2,1)} %refs_3_.1), channel_id=1, source_target_pairs={{0,1},{1,0},{2,3},{3,2},{4,5},{5,4},{6,7},{7,6},{8,9},{9,8},{10,11... | collective-permute-start | bytes 786440 | tf_op jit(solution)/shard_map/ppermute | solution.py:208
  0.5 0.0 collective-permute-start.1
  0.5 3.0 %collective-permute-start.4 = (bf16[1024,128]{1,0:T(8,128)(2,1)}, bf16[1024,128]{1,0:T(8,128)(2,1)S(1)}, u32[]{:S(2)}, u32[]{:S(2)}) collective-permute-start(bf16[1024,128]{1,0:T(8,128)(2,1)} %refs_3_.1), channel_id=1, source_target_pairs={{0,2},{1,3},{2,0},{3,1},{4,6},{5,7},{6,4},{7,5},{8,10},{9,11},{10,... | collective-permute-start | bytes 786440 | tf_op jit(solution)/shard_map/ppermute | solution.py:208
  3.5 0.0 collective-permute-start.5
  3.5 2.1 %collective-permute-start.2 = (bf16[512,128]{1,0:T(8,128)(2,1)}, bf16[512,128]{1,0:T(8,128)(2,1)S(1)}, u32[]{:S(2)}, u32[]{:S(2)}) collective-permute-start(bf16[512,128]{1,0:T(8,128)(2,1)} %bitcast.5), channel_id=1, source_target_pairs={{0,4},{1,5},{2,6},{3,7},{4,0},{5,1},{6,2},{7,3},{8,12},{9,13},{10,... | collective-permute-start | bytes 393224 | tf_op jit(solution)/shard_map/ppermute | solution.py:208
  5.6 0.0 collective-permute-done.refs_5_.refs_4_
  5.6 2.6 %collective-permute-start.3 = (bf16[512,128]{1,0:T(8,128)(2,1)}, bf16[512,128]{1,0:T(8,128)(2,1)S(1)}, u32[]{:S(2)}, u32[]{:S(2)}) collective-permute-start(bf16[512,128]{1,0:T(8,128)(2,1)} %bitcast.6), channel_id=1, source_target_pairs={{0,8},{1,9},{2,10},{3,11},{4,12},{5,13},{6,14},{7,15},{8,0},{9,1},... | collective-permute-start | bytes 393224 | tf_op jit(solution)/shard_map/ppermute | solution.py:208
  8.8 0.0 copy-start.1
  8.8 0.0 collective-permute-done.1.refs_6_.refs_5_
  8.9 0.7 %copy-done.1 = s32[512]{0:T(512)S(1)} copy-done((s32[512]{0:T(512)S(1)}, s32[512]{0:T(512)}, u32[]{:S(2)}) %copy-start.1) | copy-done | bytes 2072
  9.5 2.7 %shard_map.55 = (f32[1,512]{1,0:T(1,128)S(1)}, f32[1,512]{1,0:T(1,128)S(1)}, f32[128,512]{1,0:T(8,128)S(1)}, s32[4,512]{1,0:T(4,128)S(1)}, bf16[1024,128]{1,0:T(8,128)(2,1)S(1)}, /*index=5*/bf16[1024,128]{1,0:T(8,128)(2,1)S(1)}) custom-call(s32[4,128]{1,0:T(4,128)S(1)} %bitcast.9, s32[1,1]{1,0:T(1,128)} %bitcast.4.refs_1_, bf16[512,128]{1,0:T(8,128)(2,1)} %bitcast.7, ...), custom_call_target="tpu_custom_call" | custom-call | tf_op jit(solution)/shard_map/pallas_call | solution.py:272
  12.2 0.0 collective-permute-done.2.refs_1_
  12.2 1.5 %shard_map.56 = (f32[1,512]{1,0:T(1,128)S(1)}, f32[1,512]{1,0:T(1,128)S(1)}, f32[128,512]{1,0:T(8,128)S(1)}) custom-call(s32[4,512]{1,0:T(4,128)S(1)} %get-tuple-element.88.refs_0_, bf16[512,128]{1,0:T(8,128)(2,1)S(1)} %collective-permute-done.2.refs_1_, bf16[1024,128]{1,0:T(8,128)(2,1)S(1)} %get-tuple-element.57.refs_2_, ...), custom_call_target="tpu_custom_call" | custom-call | tf_op jit(solution)/shard_map/pallas_call | solution.py:272
  13.8 0.4 collective-permute-done.3.refs_1_
  14.1 0.0 collective-permute-done.4.refs_2_.refs_6_
  14.1 1.5 %shard_map.57 = (f32[1,512]{1,0:T(1,128)S(1)}, f32[1,512]{1,0:T(1,128)S(1)}, f32[128,512]{1,0:T(8,128)S(1)}) custom-call(s32[4,512]{1,0:T(4,128)S(1)} %get-tuple-element.88.refs_0_, bf16[512,128]{1,0:T(8,128)(2,1)S(1)} %collective-permute-done.3.refs_1_, bf16[1024,128]{1,0:T(8,128)(2,1)S(1)} %get-tuple-element.57.refs_2_, ...), custom_call_target="tpu_custom_call" | custom-call | tf_op jit(solution)/shard_map/pallas_call | solution.py:272
  15.7 0.2 collective-permute-done.5.refs_3_.refs_7_
  15.8 0.0 collective-permute-start.7
  15.8 0.5 %collective-permute-start.6 = (bf16[1024,128]{1,0:T(8,128)(2,1)S(1)}, bf16[1024,128]{1,0:T(8,128)(2,1)S(1)}, u32[]{:S(2)}, u32[]{:S(2)}) collective-permute-start(bf16[1024,128]{1,0:T(8,128)(2,1)S(1)} %collective-permute-done.4.refs_2_.refs_6_), channel_id=1, source_target_pairs={{0,1},{1,0},{2,3},{3,2},{4,5},{5,4},{6,7},{7,6},{8,9},{9,8},{10,11... | collective-permute-start | bytes 786440 | tf_op jit(solution)/shard_map/ppermute | solution.py:208
  16.3 1.8 %collective-permute-start.8 = (bf16[512,128]{1,0:T(8,128)(2,1)S(1)}, bf16[512,128]{1,0:T(8,128)(2,1)S(1)}, u32[]{:S(2)}, u32[]{:S(2)}) collective-permute-start(bf16[512,128]{1,0:T(8,128)(2,1)S(1)} %collective-permute-done.3.refs_1_), channel_id=1, source_target_pairs={{0,4},{1,5},{2,6},{3,7},{4,0},{5,1},{6,2},{7,3},{8,12},{9,13},{10,... | collective-permute-start | bytes 393224 | tf_op jit(solution)/shard_map/ppermute | solution.py:208
  18.1 0.9 %shard_map.58 = (f32[1,512]{1,0:T(1,128)S(1)}, f32[1,512]{1,0:T(1,128)S(1)}, f32[128,512]{1,0:T(8,128)S(1)}) custom-call(s32[4,512]{1,0:T(4,128)S(1)} %get-tuple-element.88.refs_0_, bf16[512,128]{1,0:T(8,128)(2,1)S(1)} %collective-permute-done.3.refs_1_, bf16[1024,128]{1,0:T(8,128)(2,1)S(1)} %collective-permute-done.4.refs_2_.refs_6_, ...), custom_call_target="tpu_custom_call" | custom-call | tf_op jit(solution)/shard_map/pallas_call | solution.py:272
  19.1 0.0 collective-permute-done.7.refs_3_.refs_9_.refs_5_
  19.1 0.0 collective-permute-done.6.refs_2_.refs_8_.refs_4_
  19.1 1.0 %shard_map.59 = bf16[136,512]{1,0:T(8,128)(2,1)S(1)} custom-call(s32[4,512]{1,0:T(4,128)S(1)} %get-tuple-element.88.refs_0_, bf16[512,128]{1,0:T(8,128)(2,1)S(1)} %collective-permute-done.3.refs_1_, bf16[1024,128]{1,0:T(8,128)(2,1)S(1)} %collective-permute-done.6.refs_2_.refs_8_.refs_4_, ...), custom_call_target="tpu_custom_call" | custom-call | tf_op jit(solution)/shard_map/pallas_call | solution.py:272
  20.1 1.7 %collective-permute-done.8.refs_1_ = bf16[512,128]{1,0:T(8,128)(2,1)S(1)} collective-permute-done((bf16[512,128]{1,0:T(8,128)(2,1)S(1)}, bf16[512,128]{1,0:T(8,128)(2,1)S(1)}, u32[]{:S(2)}, u32[]{:S(2)}) %collective-permute-start.8) | collective-permute-done | bytes 131104 | tf_op jit(solution)/shard_map/ppermute | solution.py:208
  21.8 2.9 %shard_map.60 = bf16[136,512]{1,0:T(8,128)(2,1)S(1)} custom-call(s32[4,512]{1,0:T(4,128)S(1)} %get-tuple-element.88.refs_0_, bf16[512,128]{1,0:T(8,128)(2,1)S(1)} %collective-permute-done.8.refs_1_, bf16[1024,128]{1,0:T(8,128)(2,1)S(1)} %get-tuple-element.57.refs_2_, bf16[1024,128]{1,0:T(8,128)(2,1)S(1)} %get-tuple-element.58.refs_3_, ...), custom_call_target="tpu_custom_call" | custom-call | tf_op jit(solution)/shard_map/pallas_call | solution.py:272
  24.7 0.0 copy-start
  24.7 1.6 %shard_map.61 = bf16[136,512]{1,0:T(8,128)(2,1)S(1)} custom-call(s32[4,512]{1,0:T(4,128)S(1)} %get-tuple-element.88.refs_0_, bf16[512,128]{1,0:T(8,128)(2,1)S(1)} %collective-permute-done.2.refs_1_, bf16[1024,128]{1,0:T(8,128)(2,1)S(1)} %collective-permute-done.4.refs_2_.refs_6_, bf16[1024,128]{1,0:T(8,128)(2,1)S(1)} %collective-permute-done.5.refs_3_.refs_7_, ...), custom_call_target="tpu_custom_call" | custom-call | tf_op jit(solution)/shard_map/pallas_call | solution.py:272
  26.3 1.8 %collective-permute-start.11 = (bf16[136,512]{1,0:T(8,128)(2,1)S(1)}, bf16[136,512]{1,0:T(8,128)(2,1)S(1)}, u32[]{:S(2)}, u32[]{:S(2)}) collective-permute-start(bf16[136,512]{1,0:T(8,128)(2,1)S(1)} %shard_map.61), channel_id=1, source_target_pairs={{0,4},{1,5},{2,6},{3,7},{4,0},{5,1},{6,2},{7,3},{8,12},{9,13},{10,... | collective-permute-start | bytes 417800 | tf_op jit(solution)/shard_map/ppermute | solution.py:208
  28.1 2.5 %collective-permute-start.10 = (bf16[136,512]{1,0:T(8,128)(2,1)S(1)}, bf16[136,512]{1,0:T(8,128)(2,1)S(1)}, u32[]{:S(2)}, u32[]{:S(2)}) collective-permute-start(bf16[136,512]{1,0:T(8,128)(2,1)S(1)} %shard_map.60), channel_id=1, source_target_pairs={{0,12},{1,13},{2,14},{3,15},{4,8},{5,9},{6,10},{7,11},{8,4},{9,5},... | collective-permute-start | bytes 417800 | tf_op jit(solution)/shard_map/ppermute | solution.py:208
  30.6 0.1 collective-permute-start.9
  30.7 0.0 copy-done
  30.7 1.5 %shard_map.62 = (f32[128,512]{1,0:T(8,128)S(1)}, f32[1,512]{1,0:T(1,128)S(1)}) custom-call(s32[4,512]{1,0:T(4,128)S(1)} %get-tuple-element.88.refs_0_, bf16[512,128]{1,0:T(8,128)(2,1)S(1)} %bitcast.8, bf16[1024,128]{1,0:T(8,128)(2,1)S(1)} %collective-permute-done.4.refs_2_.refs_6_, bf16[1024,128]{1,0:T(8,128)(2,1)S(1)} %collective-permute-done.5.refs_3_.refs_7_, ...), custom_call_target="tpu_custom_call" | custom-call | tf_op jit(solution)/shard_map/pallas_call | solution.py:272
  32.2 0.0 collective-permute-done.11.refs_4_
  32.2 5.5 %collective-permute-done.10.refs_3_ = bf16[136,512]{1,0:T(8,128)(2,1)S(1)} collective-permute-done((bf16[136,512]{1,0:T(8,128)(2,1)S(1)}, bf16[136,512]{1,0:T(8,128)(2,1)S(1)}, u32[]{:S(2)}, u32[]{:S(2)}) %collective-permute-start.10) | collective-permute-done | bytes 139296 | tf_op jit(solution)/shard_map/ppermute | solution.py:208
  37.7 4.6 %collective-permute-done.9.refs_2_ = bf16[136,512]{1,0:T(8,128)(2,1)S(1)} collective-permute-done((bf16[136,512]{1,0:T(8,128)(2,1)S(1)}, bf16[136,512]{1,0:T(8,128)(2,1)S(1)}, u32[]{:S(2)}, u32[]{:S(2)}) %collective-permute-start.9) | collective-permute-done | bytes 139296 | tf_op jit(solution)/shard_map/ppermute | solution.py:208
  42.3 1.0 %merge.1 = bf16[512,128]{1,0:T(8,128)(2,1)} custom-call(f32[128,512]{1,0:T(8,128)S(1)} %get-tuple-element.94.refs_0_, f32[1,512]{1,0:T(1,128)S(1)} %get-tuple-element.95.refs_1_, bf16[136,512]{1,0:T(8,128)(2,1)S(1)} %collective-permute-done.9.refs_2_, bf16[136,512]{1,0:T(8,128)(2,1)S(1)} %collective-permute-done.10.refs_3_, ...), custom_call_target="tpu_custom_call" | custom-call | tf_op jit(solution)/shard_map/merge/pallas_call | solution.py:343
Async XLA Ops:
  0.0 5.6 %collective-permute-start = (bf16[1024,128]{1,0:T(8,128)(2,1)}, bf16[1024,128]{1,0:T(8,128)(2,1)S(1)}, u32[]{:S(2)}, u32[]{:S(2)}) collective-permute-start(bf16[1024,128]{1,0:T(8,128)(2,1)} %refs_3_.1), channel_id=1, source_target_pairs={{0,1},{1,0},{2,3},{3,2},{4,5},{5,4},{6,7},{7,6},{8,9},{9,8},{10,11... | collective-permute-start | bytes 786440 | tf_op jit(solution)/shard_map/ppermute | solution.py:208
  0.5 8.4 %collective-permute-start.1 = (bf16[1024,128]{1,0:T(8,128)(2,1)}, bf16[1024,128]{1,0:T(8,128)(2,1)S(1)}, u32[]{:S(2)}, u32[]{:S(2)}) collective-permute-start(bf16[1024,128]{1,0:T(8,128)(2,1)} %refs_4_.1), channel_id=1, source_target_pairs={{0,1},{1,0},{2,3},{3,2},{4,5},{5,4},{6,7},{7,6},{8,9},{9,8},{10,11... | collective-permute-start | bytes 786440 | tf_op jit(solution)/shard_map/ppermute | solution.py:208
  0.5 13.6 %collective-permute-start.4 = (bf16[1024,128]{1,0:T(8,128)(2,1)}, bf16[1024,128]{1,0:T(8,128)(2,1)S(1)}, u32[]{:S(2)}, u32[]{:S(2)}) collective-permute-start(bf16[1024,128]{1,0:T(8,128)(2,1)} %refs_3_.1), channel_id=1, source_target_pairs={{0,2},{1,3},{2,0},{3,1},{4,6},{5,7},{6,4},{7,5},{8,10},{9,11},{10,... | collective-permute-start | bytes 786440 | tf_op jit(solution)/shard_map/ppermute | solution.py:208
  3.5 12.3 %collective-permute-start.5 = (bf16[1024,128]{1,0:T(8,128)(2,1)}, bf16[1024,128]{1,0:T(8,128)(2,1)S(1)}, u32[]{:S(2)}, u32[]{:S(2)}) collective-permute-start(bf16[1024,128]{1,0:T(8,128)(2,1)} %refs_4_.1), channel_id=1, source_target_pairs={{0,2},{1,3},{2,0},{3,1},{4,6},{5,7},{6,4},{7,5},{8,10},{9,11},{10,... | collective-permute-start | bytes 786440 | tf_op jit(solution)/shard_map/ppermute | solution.py:208
  3.5 8.7 %collective-permute-start.2 = (bf16[512,128]{1,0:T(8,128)(2,1)}, bf16[512,128]{1,0:T(8,128)(2,1)S(1)}, u32[]{:S(2)}, u32[]{:S(2)}) collective-permute-start(bf16[512,128]{1,0:T(8,128)(2,1)} %bitcast.5), channel_id=1, source_target_pairs={{0,4},{1,5},{2,6},{3,7},{4,0},{5,1},{6,2},{7,3},{8,12},{9,13},{10,... | collective-permute-start | bytes 393224 | tf_op jit(solution)/shard_map/ppermute | solution.py:208
  5.6 8.5 %collective-permute-start.3 = (bf16[512,128]{1,0:T(8,128)(2,1)}, bf16[512,128]{1,0:T(8,128)(2,1)S(1)}, u32[]{:S(2)}, u32[]{:S(2)}) collective-permute-start(bf16[512,128]{1,0:T(8,128)(2,1)} %bitcast.6), channel_id=1, source_target_pairs={{0,8},{1,9},{2,10},{3,11},{4,12},{5,13},{6,14},{7,15},{8,0},{9,1},... | collective-permute-start | bytes 393224 | tf_op jit(solution)/shard_map/ppermute | solution.py:208
  8.8 0.7 %copy-start.1 = (s32[512]{0:T(512)S(1)}, s32[512]{0:T(512)}, u32[]{:S(2)}) copy-start(s32[512]{0:T(512)} %param.9) | copy-start | bytes 6148
  15.8 3.3 %collective-permute-start.7 = (bf16[1024,128]{1,0:T(8,128)(2,1)S(1)}, bf16[1024,128]{1,0:T(8,128)(2,1)S(1)}, u32[]{:S(2)}, u32[]{:S(2)}) collective-permute-start(bf16[1024,128]{1,0:T(8,128)(2,1)S(1)} %collective-permute-done.5.refs_3_.refs_7_), channel_id=1, source_target_pairs={{0,1},{1,0},{2,3},{3,2},{4,5},{5,4},{6,7},{7,6},{8,9},{9,8},{10,11... | collective-permute-start | bytes 786440 | tf_op jit(solution)/shard_map/ppermute | solution.py:208
  15.8 3.3 %collective-permute-start.6 = (bf16[1024,128]{1,0:T(8,128)(2,1)S(1)}, bf16[1024,128]{1,0:T(8,128)(2,1)S(1)}, u32[]{:S(2)}, u32[]{:S(2)}) collective-permute-start(bf16[1024,128]{1,0:T(8,128)(2,1)S(1)} %collective-permute-done.4.refs_2_.refs_6_), channel_id=1, source_target_pairs={{0,1},{1,0},{2,3},{3,2},{4,5},{5,4},{6,7},{7,6},{8,9},{9,8},{10,11... | collective-permute-start | bytes 786440 | tf_op jit(solution)/shard_map/ppermute | solution.py:208
  16.3 5.5 %collective-permute-start.8 = (bf16[512,128]{1,0:T(8,128)(2,1)S(1)}, bf16[512,128]{1,0:T(8,128)(2,1)S(1)}, u32[]{:S(2)}, u32[]{:S(2)}) collective-permute-start(bf16[512,128]{1,0:T(8,128)(2,1)S(1)} %collective-permute-done.3.refs_1_), channel_id=1, source_target_pairs={{0,4},{1,5},{2,6},{3,7},{4,0},{5,1},{6,2},{7,3},{8,12},{9,13},{10,... | collective-permute-start | bytes 393224 | tf_op jit(solution)/shard_map/ppermute | solution.py:208
  24.7 6.0 %copy-start = (bf16[32,16,128]{2,1,0:T(8,128)(2,1)S(1)}, bf16[32,16,128]{2,1,0:T(8,128)(2,1)}, u32[]{:S(2)}) copy-start(bf16[32,16,128]{2,1,0:T(8,128)(2,1)} %param.5) | copy-start | bytes 393220
  26.3 5.9 %collective-permute-start.11 = (bf16[136,512]{1,0:T(8,128)(2,1)S(1)}, bf16[136,512]{1,0:T(8,128)(2,1)S(1)}, u32[]{:S(2)}, u32[]{:S(2)}) collective-permute-start(bf16[136,512]{1,0:T(8,128)(2,1)S(1)} %shard_map.61), channel_id=1, source_target_pairs={{0,4},{1,5},{2,6},{3,7},{4,0},{5,1},{6,2},{7,3},{8,12},{9,13},{10,... | collective-permute-start | bytes 417800 | tf_op jit(solution)/shard_map/ppermute | solution.py:208
  28.1 9.7 %collective-permute-start.10 = (bf16[136,512]{1,0:T(8,128)(2,1)S(1)}, bf16[136,512]{1,0:T(8,128)(2,1)S(1)}, u32[]{:S(2)}, u32[]{:S(2)}) collective-permute-start(bf16[136,512]{1,0:T(8,128)(2,1)S(1)} %shard_map.60), channel_id=1, source_target_pairs={{0,12},{1,13},{2,14},{3,15},{4,8},{5,9},{6,10},{7,11},{8,4},{9,5},... | collective-permute-start | bytes 417800 | tf_op jit(solution)/shard_map/ppermute | solution.py:208
  30.6 11.8 %collective-permute-start.9 = (bf16[136,512]{1,0:T(8,128)(2,1)S(1)}, bf16[136,512]{1,0:T(8,128)(2,1)S(1)}, u32[]{:S(2)}, u32[]{:S(2)}) collective-permute-start(bf16[136,512]{1,0:T(8,128)(2,1)S(1)} %shard_map.59), channel_id=1, source_target_pairs={{0,8},{1,9},{2,10},{3,11},{4,12},{5,13},{6,14},{7,15},{8,0},{9,1},... | collective-permute-start | bytes 417800 | tf_op jit(solution)/shard_map/ppermute | solution.py:208

commit v4 on v3

--- a/solution.py
+++ b/solution.py
@@ -181,6 +181,13 @@
     return value, top + jnp.log2(total)
 
 
+def combine_kernel(value_ref, level_ref, part_ref, out_ref):
+    width, lanes = value_ref.shape
+    value, level = decode(part_ref[:width, :], part_ref[width:, :])
+    value, level = combine([value_ref[...], value], [level_ref[...], level])
+    write_partial([out_ref], "code", slice(0, lanes), value, level)
+
+
 def merge_kernel(groups, *refs):
     own_ref, own_level_ref = refs[:2]
     parts, out_ref = refs[2:-1], refs[-1]
@@ -327,10 +334,28 @@
 
     coded = [packed_shape(stage_rows)]
     attend(last - 1, [2])
-    send(last - 1, attend(last - 1, [3], whole_plan, coded)[0])
-    send(last, attend(last, [0, 1, 2, 3], whole_plan, coded)[0])
-    for index in range(last - 2, 0, -1):
-        send(index, attend(index, [2, 3], whole_plan, coded)[0])
+    if outer == 4:
+        (packed,) = attend(2, [3], whole_plan, coded)
+        handed = swap(packed, inner)
+        (packed,) = attend(1, [2, 3], whole_plan, coded)
+        parts.append(swap(packed, inner))
+        value, level = attend(3, [0, 1, 2, 3], own_plan, float_shapes(stage_rows))
+        (handed,) = hold(handed)
+        joined = pl.pallas_call(
+            combine_kernel,
+            in_specs=[vmem] * 3,
+            out_specs=vmem,
+            out_shape=coded[0],
+            compiler_params=params,
+            name="combine",
+        )(value, level, handed)
+        (joined,) = hold(joined)
+        parts.append(swap(joined, 3 * inner))
+    else:
+        send(last - 1, attend(last - 1, [3], whole_plan, coded)[0])
+        send(last, attend(last, [0, 1, 2, 3], whole_plan, coded)[0])
+        for index in range(last - 2, 0, -1):
+            send(index, attend(index, [2, 3], whole_plan, coded)[0])
     if per_stage == 1:
         own = attend(0, [2, 3], own_plan, float_shapes(rows))
     else:

time: 43.5 us -> 41.5 us (0.954)
  waiting for transfers between devices: 12.3 us -> 9.79 us
    ppermute x12, waiting for transfers between devices: 12.3 us -> 9.79 us  [swap(): return lax.ppermute(array, 'ctx', [(i, i ^ step) for i in range(size)])]
  transfers between devices with their start and end apart: 12 -> 12, of which waited for: 5 -> 6; matrix products, arithmetic and copies ran while one was open for 0% -> 0% of each run, Pallas kernels for 21% -> 31%
where the time goes in v4:
time: 41.5 us; the launch traced here: 41.3 us
  starting transfers between devices  15.1 us (36%)
  Pallas kernels  15 us (36%)
  waiting for transfers between devices  9.79 us (24%)
  between operations  0.77 us (2%)
  local copies, waits for them, and re-layouts  0.67 us (2%)
    ppermute x12, starting transfers between devices, swap(): return lax.ppermute(array, 'ctx', [(i, i ^ step) for i in range(size)])  15.1 us
    pallas_call x8, Pallas kernels, attend(): pl.pallas_call(functools.partial(attend_kernel, scale, index, blocks, sta...  13.8 us
    ppermute x12, waiting for transfers between devices, swap(): return lax.ppermute(array, 'ctx', [(i, i ^ step) for i in range(size)])  9.79 us
    pallas_call x1, Pallas kernels, local(): pl.pallas_call(functools.partial(merge_kernel, groups), in_specs=[vmem] *...  0.94 us
  transfers between devices with their start and end apart: 12, of which 6 were waited for; matrix products, arithmetic and copies ran while one was open for 0% of the time, Pallas kernels for 31%

profile of v4, /device:TPU:0, one launch (start us, length us, event | category | flops | bytes accessed | tf_op | source)
XLA Modules:
  0.0 41.3 jit_solution(10396451211201186119)
XLA Ops:
  0.0 0.5 %collective-permute-start = (bf16[1024,128]{1,0:T(8,128)(2,1)}, bf16[1024,128]{1,0:T(8,128)(2,1)S(1)}, u32[]{:S(2)}, u32[]{:S(2)}) collective-permute-start(bf16[1024,128]{1,0:T(8,128)(2,1)} %refs_3_.1), channel_id=1, source_target_pairs={{0,1},{1,0},{2,3},{3,2},{4,5},{5,4},{6,7},{7,6},{8,9},{9,8},{10,11... | collective-permute-start | bytes 786440 | tf_op jit(solution)/shard_map/ppermute | solution.py:215
  0.5 0.0 collective-permute-start.1
  0.5 3.0 %collective-permute-start.4 = (bf16[1024,128]{1,0:T(8,128)(2,1)}, bf16[1024,128]{1,0:T(8,128)(2,1)S(1)}, u32[]{:S(2)}, u32[]{:S(2)}) collective-permute-start(bf16[1024,128]{1,0:T(8,128)(2,1)} %refs_3_.1), channel_id=1, source_target_pairs={{0,2},{1,3},{2,0},{3,1},{4,6},{5,7},{6,4},{7,5},{8,10},{9,11},{10,... | collective-permute-start | bytes 786440 | tf_op jit(solution)/shard_map/ppermute | solution.py:215
  3.5 0.0 collective-permute-start.5
  3.5 2.1 %collective-permute-start.2 = (bf16[512,128]{1,0:T(8,128)(2,1)}, bf16[512,128]{1,0:T(8,128)(2,1)S(1)}, u32[]{:S(2)}, u32[]{:S(2)}) collective-permute-start(bf16[512,128]{1,0:T(8,128)(2,1)} %bitcast.5), channel_id=1, source_target_pairs={{0,4},{1,5},{2,6},{3,7},{4,0},{5,1},{6,2},{7,3},{8,12},{9,13},{10,... | collective-permute-start | bytes 393224 | tf_op jit(solution)/shard_map/ppermute | solution.py:215
  5.6 0.0 collective-permute-done.refs_5_.refs_4_
  5.6 2.6 %collective-permute-start.3 = (bf16[512,128]{1,0:T(8,128)(2,1)}, bf16[512,128]{1,0:T(8,128)(2,1)S(1)}, u32[]{:S(2)}, u32[]{:S(2)}) collective-permute-start(bf16[512,128]{1,0:T(8,128)(2,1)} %bitcast.6), channel_id=1, source_target_pairs={{0,8},{1,9},{2,10},{3,11},{4,12},{5,13},{6,14},{7,15},{8,0},{9,1},... | collective-permute-start | bytes 393224 | tf_op jit(solution)/shard_map/ppermute | solution.py:215
  8.8 0.0 copy-start.1
  8.8 0.0 collective-permute-done.1.refs_6_.refs_5_
  8.9 0.7 %copy-done.1 = s32[512]{0:T(512)S(1)} copy-done((s32[512]{0:T(512)S(1)}, s32[512]{0:T(512)}, u32[]{:S(2)}) %copy-start.1) | copy-done | bytes 2072
  9.5 2.7 %shard_map.55 = (f32[1,512]{1,0:T(1,128)S(1)}, f32[1,512]{1,0:T(1,128)S(1)}, f32[128,512]{1,0:T(8,128)S(1)}, s32[4,512]{1,0:T(4,128)S(1)}, bf16[1024,128]{1,0:T(8,128)(2,1)S(1)}, /*index=5*/bf16[1024,128]{1,0:T(8,128)(2,1)S(1)}) custom-call(s32[4,128]{1,0:T(4,128)S(1)} %bitcast.9, s32[1,1]{1,0:T(1,128)} %bitcast.4.refs_1_, bf16[512,128]{1,0:T(8,128)(2,1)} %bitcast.7, ...), custom_call_target="tpu_custom_call" | custom-call | tf_op jit(solution)/shard_map/pallas_call | solution.py:279
  12.3 0.0 collective-permute-done.2.refs_1_
  12.3 1.5 %shard_map.56 = (f32[1,512]{1,0:T(1,128)S(1)}, f32[1,512]{1,0:T(1,128)S(1)}, f32[128,512]{1,0:T(8,128)S(1)}) custom-call(s32[4,512]{1,0:T(4,128)S(1)} %get-tuple-element.103.refs_0_, bf16[512,128]{1,0:T(8,128)(2,1)S(1)} %collective-permute-done.2.refs_1_, bf16[1024,128]{1,0:T(8,128)(2,1)S(1)} %get-tuple-element.64.refs_2_, ...), custom_call_target="tpu_custom_call" | custom-call | tf_op jit(solution)/shard_map/pallas_call | solution.py:279
  13.8 0.3 collective-permute-done.3.refs_1_
  14.1 0.0 collective-permute-done.4.refs_2_.refs_6_
  14.1 1.5 %shard_map.57 = (f32[1,512]{1,0:T(1,128)S(1)}, f32[1,512]{1,0:T(1,128)S(1)}, f32[128,512]{1,0:T(8,128)S(1)}) custom-call(s32[4,512]{1,0:T(4,128)S(1)} %get-tuple-element.103.refs_0_, bf16[512,128]{1,0:T(8,128)(2,1)S(1)} %collective-permute-done.3.refs_1_, bf16[1024,128]{1,0:T(8,128)(2,1)S(1)} %get-tuple-element.64.refs_2_, ...), custom_call_target="tpu_custom_call" | custom-call | tf_op jit(solution)/shard_map/pallas_call | solution.py:279
  15.7 0.1 collective-permute-done.5.refs_3_.refs_7_
  15.8 0.0 collective-permute-start.7
  15.8 0.5 %collective-permute-start.6 = (bf16[1024,128]{1,0:T(8,128)(2,1)S(1)}, bf16[1024,128]{1,0:T(8,128)(2,1)S(1)}, u32[]{:S(2)}, u32[]{:S(2)}) collective-permute-start(bf16[1024,128]{1,0:T(8,128)(2,1)S(1)} %collective-permute-done.4.refs_2_.refs_6_), channel_id=1, source_target_pairs={{0,1},{1,0},{2,3},{3,2},{4,5},{5,4},{6,7},{7,6},{8,9},{9,8},{10,11... | collective-permute-start | bytes 786440 | tf_op jit(solution)/shard_map/ppermute | solution.py:215
  16.3 0.9 %shard_map.58 = (f32[1,512]{1,0:T(1,128)S(1)}, f32[1,512]{1,0:T(1,128)S(1)}, f32[128,512]{1,0:T(8,128)S(1)}) custom-call(s32[4,512]{1,0:T(4,128)S(1)} %get-tuple-element.103.refs_0_, bf16[512,128]{1,0:T(8,128)(2,1)S(1)} %collective-permute-done.3.refs_1_, bf16[1024,128]{1,0:T(8,128)(2,1)S(1)} %collective-permute-done.4.refs_2_.refs_6_, ...), custom_call_target="tpu_custom_call" | custom-call | tf_op jit(solution)/shard_map/pallas_call | solution.py:279
  17.3 0.1 collective-permute-done.7.refs_3_.refs_5_.refs_9_
  17.3 0.4 collective-permute-done.6.refs_2_.refs_4_.refs_8_
  17.7 1.0 %shard_map.59 = bf16[136,512]{1,0:T(8,128)(2,1)S(1)} custom-call(s32[4,512]{1,0:T(4,128)S(1)} %get-tuple-element.103.refs_0_, bf16[512,128]{1,0:T(8,128)(2,1)S(1)} %collective-permute-done.3.refs_1_, bf16[1024,128]{1,0:T(8,128)(2,1)S(1)} %collective-permute-done.6.refs_2_.refs_4_.refs_8_, ...), custom_call_target="tpu_custom_call" | custom-call | tf_op jit(solution)/shard_map/pallas_call | solution.py:279
  18.7 1.9 %collective-permute-start.9 = (bf16[136,512]{1,0:T(8,128)(2,1)S(1)}, bf16[136,512]{1,0:T(8,128)(2,1)S(1)}, u32[]{:S(2)}, u32[]{:S(2)}) collective-permute-start(bf16[136,512]{1,0:T(8,128)(2,1)S(1)} %shard_map.59), channel_id=1, source_target_pairs={{0,4},{1,5},{2,6},{3,7},{4,0},{5,1},{6,2},{7,3},{8,12},{9,13},{10,... | collective-permute-start | bytes 417800 | tf_op jit(solution)/shard_map/ppermute | solution.py:215
  20.6 0.2 collective-permute-start.8
  20.8 1.6 %shard_map.60 = bf16[136,512]{1,0:T(8,128)(2,1)S(1)} custom-call(s32[4,512]{1,0:T(4,128)S(1)} %get-tuple-element.103.refs_0_, bf16[512,128]{1,0:T(8,128)(2,1)S(1)} %collective-permute-done.2.refs_1_, bf16[1024,128]{1,0:T(8,128)(2,1)S(1)} %collective-permute-done.4.refs_2_.refs_6_, bf16[1024,128]{1,0:T(8,128)(2,1)S(1)} %collective-permute-done.5.refs_3_.refs_7_, ...), custom_call_target="tpu_custom_call" | custom-call | tf_op jit(solution)/shard_map/pallas_call | solution.py:279
  22.5 4.9 %collective-permute-done.8.refs_1_ = bf16[512,128]{1,0:T(8,128)(2,1)S(1)} collective-permute-done((bf16[512,128]{1,0:T(8,128)(2,1)S(1)}, bf16[512,128]{1,0:T(8,128)(2,1)S(1)}, u32[]{:S(2)}, u32[]{:S(2)}) %collective-permute-start.8) | collective-permute-done | bytes 131104 | tf_op jit(solution)/shard_map/ppermute | solution.py:215
  27.4 2.9 %shard_map.61 = (f32[128,512]{1,0:T(8,128)S(1)}, f32[1,512]{1,0:T(1,128)S(1)}) custom-call(s32[4,512]{1,0:T(4,128)S(1)} %get-tuple-element.103.refs_0_, bf16[512,128]{1,0:T(8,128)(2,1)S(1)} %collective-permute-done.8.refs_1_, bf16[1024,128]{1,0:T(8,128)(2,1)S(1)} %get-tuple-element.64.refs_2_, bf16[1024,128]{1,0:T(8,128)(2,1)S(1)} %get-tuple-element.65.refs_3_, ...), custom_call_target="tpu_custom_call" | custom-call | tf_op jit(solution)/shard_map/pallas_call | solution.py:279
  30.3 0.0 copy-start
  30.3 1.8 %collective-permute-start.10 = (bf16[136,512]{1,0:T(8,128)(2,1)S(1)}, bf16[136,512]{1,0:T(8,128)(2,1)S(1)}, u32[]{:S(2)}, u32[]{:S(2)}) collective-permute-start(bf16[136,512]{1,0:T(8,128)(2,1)S(1)} %shard_map.60), channel_id=1, source_target_pairs={{0,4},{1,5},{2,6},{3,7},{4,0},{5,1},{6,2},{7,3},{8,12},{9,13},{10,... | collective-permute-start | bytes 417800 | tf_op jit(solution)/shard_map/ppermute | solution.py:215
  32.1 0.0 collective-permute-done.9.part_ref
  32.1 0.3 combine.1
  32.3 2.5 %collective-permute-start.11 = (bf16[136,512]{1,0:T(8,128)(2,1)S(1)}, bf16[136,512]{1,0:T(8,128)(2,1)S(1)}, u32[]{:S(2)}, u32[]{:S(2)}) collective-permute-start(bf16[136,512]{1,0:T(8,128)(2,1)S(1)} %combine.1), channel_id=1, source_target_pairs={{0,12},{1,13},{2,14},{3,15},{4,8},{5,9},{6,10},{7,11},{8,4},{9,5},... | collective-permute-start | bytes 417800 | tf_op jit(solution)/shard_map/ppermute | solution.py:215
  34.9 0.0 copy-done
  34.9 1.5 %shard_map.62 = (f32[128,512]{1,0:T(8,128)S(1)}, f32[1,512]{1,0:T(1,128)S(1)}) custom-call(s32[4,512]{1,0:T(4,128)S(1)} %get-tuple-element.103.refs_0_, bf16[512,128]{1,0:T(8,128)(2,1)S(1)} %bitcast.8, bf16[1024,128]{1,0:T(8,128)(2,1)S(1)} %collective-permute-done.4.refs_2_.refs_6_, bf16[1024,128]{1,0:T(8,128)(2,1)S(1)} %collective-permute-done.5.refs_3_.refs_7_, ...), custom_call_target="tpu_custom_call" | custom-call | tf_op jit(solution)/shard_map/pallas_call | solution.py:279
  36.4 0.0 collective-permute-done.10.refs_2_
  36.4 3.9 %collective-permute-done.11.refs_3_ = bf16[136,512]{1,0:T(8,128)(2,1)S(1)} collective-permute-done((bf16[136,512]{1,0:T(8,128)(2,1)S(1)}, bf16[136,512]{1,0:T(8,128)(2,1)S(1)}, u32[]{:S(2)}, u32[]{:S(2)}) %collective-permute-start.11) | collective-permute-done | bytes 139296 | tf_op jit(solution)/shard_map/ppermute | solution.py:215
  40.4 0.9 %merge.1 = bf16[512,128]{1,0:T(8,128)(2,1)} custom-call(f32[128,512]{1,0:T(8,128)S(1)} %get-tuple-element.109.refs_0_, f32[1,512]{1,0:T(1,128)S(1)} %get-tuple-element.110.refs_1_, bf16[136,512]{1,0:T(8,128)(2,1)S(1)} %collective-permute-done.10.refs_2_, bf16[136,512]{1,0:T(8,128)(2,1)S(1)} %collective-permute-done.11.refs_3_), custom_call_target="tpu_custom_call" | custom-call | tf_op jit(solution)/shard_map/merge/pallas_call | solution.py:368
Async XLA Ops:
  0.0 5.6 %collective-permute-start = (bf16[1024,128]{1,0:T(8,128)(2,1)}, bf16[1024,128]{1,0:T(8,128)(2,1)S(1)}, u32[]{:S(2)}, u32[]{:S(2)}) collective-permute-start(bf16[1024,128]{1,0:T(8,128)(2,1)} %refs_3_.1), channel_id=1, source_target_pairs={{0,1},{1,0},{2,3},{3,2},{4,5},{5,4},{6,7},{7,6},{8,9},{9,8},{10,11... | collective-permute-start | bytes 786440 | tf_op jit(solution)/shard_map/ppermute | solution.py:215
  0.5 8.4 %collective-permute-start.1 = (bf16[1024,128]{1,0:T(8,128)(2,1)}, bf16[1024,128]{1,0:T(8,128)(2,1)S(1)}, u32[]{:S(2)}, u32[]{:S(2)}) collective-permute-start(bf16[1024,128]{1,0:T(8,128)(2,1)} %refs_4_.1), channel_id=1, source_target_pairs={{0,1},{1,0},{2,3},{3,2},{4,5},{5,4},{6,7},{7,6},{8,9},{9,8},{10,11... | collective-permute-start | bytes 786440 | tf_op jit(solution)/shard_map/ppermute | solution.py:215
  0.5 13.6 %collective-permute-start.4 = (bf16[1024,128]{1,0:T(8,128)(2,1)}, bf16[1024,128]{1,0:T(8,128)(2,1)S(1)}, u32[]{:S(2)}, u32[]{:S(2)}) collective-permute-start(bf16[1024,128]{1,0:T(8,128)(2,1)} %refs_3_.1), channel_id=1, source_target_pairs={{0,2},{1,3},{2,0},{3,1},{4,6},{5,7},{6,4},{7,5},{8,10},{9,11},{10,... | collective-permute-start | bytes 786440 | tf_op jit(solution)/shard_map/ppermute | solution.py:215
  3.5 12.3 %collective-permute-start.5 = (bf16[1024,128]{1,0:T(8,128)(2,1)}, bf16[1024,128]{1,0:T(8,128)(2,1)S(1)}, u32[]{:S(2)}, u32[]{:S(2)}) collective-permute-start(bf16[1024,128]{1,0:T(8,128)(2,1)} %refs_4_.1), channel_id=1, source_target_pairs={{0,2},{1,3},{2,0},{3,1},{4,6},{5,7},{6,4},{7,5},{8,10},{9,11},{10,... | collective-permute-start | bytes 786440 | tf_op jit(solution)/shard_map/ppermute | solution.py:215
  3.5 8.7 %collective-permute-start.2 = (bf16[512,128]{1,0:T(8,128)(2,1)}, bf16[512,128]{1,0:T(8,128)(2,1)S(1)}, u32[]{:S(2)}, u32[]{:S(2)}) collective-permute-start(bf16[512,128]{1,0:T(8,128)(2,1)} %bitcast.5), channel_id=1, source_target_pairs={{0,4},{1,5},{2,6},{3,7},{4,0},{5,1},{6,2},{7,3},{8,12},{9,13},{10,... | collective-permute-start | bytes 393224 | tf_op jit(solution)/shard_map/ppermute | solution.py:215
  5.6 8.5 %collective-permute-start.3 = (bf16[512,128]{1,0:T(8,128)(2,1)}, bf16[512,128]{1,0:T(8,128)(2,1)S(1)}, u32[]{:S(2)}, u32[]{:S(2)}) collective-permute-start(bf16[512,128]{1,0:T(8,128)(2,1)} %bitcast.6), channel_id=1, source_target_pairs={{0,8},{1,9},{2,10},{3,11},{4,12},{5,13},{6,14},{7,15},{8,0},{9,1},... | collective-permute-start | bytes 393224 | tf_op jit(solution)/shard_map/ppermute | solution.py:215
  8.8 0.7 %copy-start.1 = (s32[512]{0:T(512)S(1)}, s32[512]{0:T(512)}, u32[]{:S(2)}) copy-start(s32[512]{0:T(512)} %param.9) | copy-start | bytes 6148
  15.8 1.5 %collective-permute-start.7 = (bf16[1024,128]{1,0:T(8,128)(2,1)S(1)}, bf16[1024,128]{1,0:T(8,128)(2,1)S(1)}, u32[]{:S(2)}, u32[]{:S(2)}) collective-permute-start(bf16[1024,128]{1,0:T(8,128)(2,1)S(1)} %collective-permute-done.5.refs_3_.refs_7_), channel_id=1, source_target_pairs={{0,1},{1,0},{2,3},{3,2},{4,5},{5,4},{6,7},{7,6},{8,9},{9,8},{10,11... | collective-permute-start | bytes 786440 | tf_op jit(solution)/shard_map/ppermute | solution.py:215
  15.8 1.9 %collective-permute-start.6 = (bf16[1024,128]{1,0:T(8,128)(2,1)S(1)}, bf16[1024,128]{1,0:T(8,128)(2,1)S(1)}, u32[]{:S(2)}, u32[]{:S(2)}) collective-permute-start(bf16[1024,128]{1,0:T(8,128)(2,1)S(1)} %collective-permute-done.4.refs_2_.refs_6_), channel_id=1, source_target_pairs={{0,1},{1,0},{2,3},{3,2},{4,5},{5,4},{6,7},{7,6},{8,9},{9,8},{10,11... | collective-permute-start | bytes 786440 | tf_op jit(solution)/shard_map/ppermute | solution.py:215
  18.7 13.3 %collective-permute-start.9 = (bf16[136,512]{1,0:T(8,128)(2,1)S(1)}, bf16[136,512]{1,0:T(8,128)(2,1)S(1)}, u32[]{:S(2)}, u32[]{:S(2)}) collective-permute-start(bf16[136,512]{1,0:T(8,128)(2,1)S(1)} %shard_map.59), channel_id=1, source_target_pairs={{0,4},{1,5},{2,6},{3,7},{4,0},{5,1},{6,2},{7,3},{8,12},{9,13},{10,... | collective-permute-start | bytes 417800 | tf_op jit(solution)/shard_map/ppermute | solution.py:215
  20.6 6.8 %collective-permute-start.8 = (bf16[512,128]{1,0:T(8,128)(2,1)S(1)}, bf16[512,128]{1,0:T(8,128)(2,1)S(1)}, u32[]{:S(2)}, u32[]{:S(2)}) collective-permute-start(bf16[512,128]{1,0:T(8,128)(2,1)S(1)} %collective-permute-done.3.refs_1_), channel_id=1, source_target_pairs={{0,4},{1,5},{2,6},{3,7},{4,0},{5,1},{6,2},{7,3},{8,12},{9,13},{10,... | collective-permute-start | bytes 393224 | tf_op jit(solution)/shard_map/ppermute | solution.py:215
  30.3 4.6 %copy-start = (bf16[32,16,128]{2,1,0:T(8,128)(2,1)S(1)}, bf16[32,16,128]{2,1,0:T(8,128)(2,1)}, u32[]{:S(2)}) copy-start(bf16[32,16,128]{2,1,0:T(8,128)(2,1)} %param.5) | copy-start | bytes 393220
  30.3 6.2 %collective-permute-start.10 = (bf16[136,512]{1,0:T(8,128)(2,1)S(1)}, bf16[136,512]{1,0:T(8,128)(2,1)S(1)}, u32[]{:S(2)}, u32[]{:S(2)}) collective-permute-start(bf16[136,512]{1,0:T(8,128)(2,1)S(1)} %shard_map.60), channel_id=1, source_target_pairs={{0,4},{1,5},{2,6},{3,7},{4,0},{5,1},{6,2},{7,3},{8,12},{9,13},{10,... | collective-permute-start | bytes 417800 | tf_op jit(solution)/shard_map/ppermute | solution.py:215
  32.3 8.0 %collective-permute-start.11 = (bf16[136,512]{1,0:T(8,128)(2,1)S(1)}, bf16[136,512]{1,0:T(8,128)(2,1)S(1)}, u32[]{:S(2)}, u32[]{:S(2)}) collective-permute-start(bf16[136,512]{1,0:T(8,128)(2,1)S(1)} %combine.1), channel_id=1, source_target_pairs={{0,12},{1,13},{2,14},{3,15},{4,8},{5,9},{6,10},{7,11},{8,4},{9,5},... | collective-permute-start | bytes 417800 | tf_op jit(solution)/shard_map/ppermute | solution.py:215

commit v5 on v4

--- a/solution.py
+++ b/solution.py
@@ -17,65 +17,113 @@
 code_low = -120.0
 
 
-def attend_tiles(scale, query, keys, values, limits, states, scores_ref, weights_ref, values_ref):
-    rows, width = query.shape
-    shard_keys = keys[0].shape[0]
-    tile = scores_ref.shape[2]
-    chunk = min(512, shard_keys)
-    chunks = shard_keys // chunk
+def split_query(query, scale):
     scaled = query.astype(jnp.float32) * scale
     high = scaled.astype(jnp.bfloat16)
     low = (scaled - high.astype(jnp.float32)).astype(jnp.bfloat16)
-    query_pair = jnp.concatenate([high, low], axis=1)
+    return jnp.concatenate([high, low], axis=1)
+
+
+def transpose_values(values, values_ref):
     for b, value in enumerate(values):
+        shard_keys, width = value.shape
         values_ref[b, :width, :] = value[...].T
         values_ref[b, width:, :] = jnp.ones((extra_rows, shard_keys), jnp.bfloat16)
+
+
+def score_chunk(key, query_pair, limit, start, scores_ref, slot):
+    chunk, tile = key.shape[0], query_pair.shape[0]
+    scores = lax.dot_general(
+        jnp.concatenate([key, key], axis=1), query_pair, (((1,), (1,)), ((), ())), preferred_element_type=jnp.float32
+    ).reshape(chunk // 8, 8, tile)
+    position = lax.broadcasted_iota(jnp.int32, scores.shape, 0) * 8 + start
     sublane = lax.broadcasted_iota(jnp.int32, (8, tile), 0)
+    scores = jnp.where(position <= (limit - sublane)[None], scores, masked_floor)
+    scores_ref[slot, start : start + chunk, :] = scores.reshape(chunk, tile)
+    return jnp.max(scores, axis=0)
+
+
+def add_block(state, values_t, weights, shard_max):
+    width = values_t.shape[0] - extra_rows
+    sums = lax.dot_general(values_t, weights, (((1,), (0,)), ((), ())), preferred_element_type=jnp.float32)
+    num, den = sums[:width], sums[width : width + 1]
+    if state is None:
+        return shard_max, den, num
+    top, run_den, run_num = state
+    new_top = jnp.maximum(top, shard_max)
+    keep, fresh = jnp.exp2(top - new_top), jnp.exp2(shard_max - new_top)
+    return new_top, run_den * keep + den * fresh, run_num * keep + num * fresh
+
+
+def sweep_tiles(rows, tile, query_pair, keys, limits, scores_ref, put_weights, finish):
+    shard_keys = keys[0].shape[0]
+    chunk = min(512, shard_keys)
+    chunks = shard_keys // chunk
     tiles = [(b, h) for b in range(len(keys)) for h in range(rows // tile)]
     count = len(tiles)
     running, tops = [None] * count, [None] * count
-    states = list(states)
     for step in range(count + 2):
         for c in range(chunks):
             span = slice(c * chunk, (c + 1) * chunk)
             if step < count:
                 b, h = tiles[step]
                 lanes = slice(h * tile, (h + 1) * tile)
-                key = keys[b][span, :]
-                scores = lax.dot_general(
-                    jnp.concatenate([key, key], axis=1),
-                    query_pair[lanes],
-                    (((1,), (1,)), ((), ())),
-                    preferred_element_type=jnp.float32,
-                ).reshape(chunk // 8, 8, tile)
-                position = lax.broadcasted_iota(jnp.int32, scores.shape, 0) * 8 + c * chunk
-                scores = jnp.where(position <= (limits[b][:, lanes] - sublane)[None], scores, masked_floor)
-                peak = jnp.max(scores, axis=0)
+                peak = score_chunk(
+                    keys[b][span, :], query_pair[lanes], limits[b][:, lanes], c * chunk, scores_ref, step % 2
+                )
                 running[step] = peak if c == 0 else jnp.maximum(running[step], peak)
-                scores_ref[step % 2, span, :] = scores.reshape(chunk, tile)
             if 1 <= step <= count:
                 t = step - 1
                 if c == 0:
                     tops[t] = jnp.max(running[t], axis=0, keepdims=True)
-                weights_ref[t % 2, span, :] = jnp.exp2(scores_ref[t % 2, span, :] - tops[t]).astype(jnp.bfloat16)
+                put_weights(t, *tiles[t], span, jnp.exp2(scores_ref[t % 2, span, :] - tops[t]).astype(jnp.bfloat16))
             if step >= 2 and c == min(1, chunks - 1):
-                b, h = tiles[step - 2]
-                shard_max = tops[step - 2]
-                sums = lax.dot_general(
-                    values_ref[b],
-                    weights_ref[step % 2],
-                    (((1,), (0,)), ((), ())),
-                    preferred_element_type=jnp.float32,
-                )
-                num, den = sums[:width], sums[width : width + 1]
-                if states[h] is None:
-                    states[h] = (shard_max, den, num)
-                else:
-                    top, run_den, run_num = states[h]
-                    new_top = jnp.maximum(top, shard_max)
-                    keep, fresh = jnp.exp2(top - new_top), jnp.exp2(shard_max - new_top)
-                    states[h] = (new_top, run_den * keep + den * fresh, run_num * keep + num * fresh)
+                finish(step - 2, *tiles[step - 2], tops[step - 2])
+
+
+def attend_tiles(scale, query, keys, values, limits, states, scores_ref, weights_ref, values_ref):
+    states = list(states)
+    query_pair = split_query(query, scale)
+    transpose_values(values, values_ref)
+
+    def put_weights(t, b, h, span, weights):
+        weights_ref[t % 2, span, :] = weights
+
+    def finish(t, b, h, shard_max):
+        states[h] = add_block(states[h], values_ref[b], weights_ref[t % 2], shard_max)
+
+    sweep_tiles(query.shape[0], scores_ref.shape[2], query_pair, keys, limits, scores_ref, put_weights, finish)
     return states
+
+
+def weigh_kernel(scale, index, blocks, limits_ref, q_ref, *refs):
+    me = lax.axis_index("ctx")
+    count = len(blocks)
+    keys, weights, tops, scores_ref = refs[:count], refs[count : 2 * count], refs[2 * count : 3 * count], refs[-1]
+    tile = scores_ref.shape[2]
+    limits = [limits_ref[index : index + 1, :] - (me ^ b) * keys[0].shape[0] for b in blocks]
+
+    def put_weights(t, b, h, span, value):
+        weights[b][span, h * tile : (h + 1) * tile] = value
+
+    def finish(t, b, h, shard_max):
+        tops[b][:, h * tile : (h + 1) * tile] = shard_max
+
+    query_pair = split_query(q_ref[...], scale)
+    sweep_tiles(q_ref.shape[0], tile, query_pair, keys, limits, scores_ref, put_weights, finish)
+
+
+def finish_kernel(count, plan, *refs):
+    values, weights, tops = refs[:count], refs[count : 2 * count], refs[2 * count : 3 * count]
+    state_refs, outs, values_ref = refs[3 * count : 3 * count + 3], refs[3 * count + 3 : -1], refs[-1]
+    transpose_values(values, values_ref)
+    for at, form, out, offset, lanes in plan:
+        span = slice(at * lanes, (at + 1) * lanes)
+        state = tuple(ref[:, span] for ref in state_refs)
+        for b in range(count):
+            state = add_block(state, values_ref[b], weights[b][:, span], tops[b][:, span])
+        top, den, num = state
+        write_partial(outs[out:], form, slice(offset, offset + lanes), num * (1.0 / den), top + jnp.log2(den))
 
 
 def encode(values, level):
@@ -310,7 +358,7 @@
     for index in range(len(stages) - 1):
         gather(index)
         ready(index)
-    attend(0, [0, 1])
+    attend(0, [0])
     for index in range(1, last - 1):
         attend(index, [0, 1])
     source = stages[last][0] ^ (stages[last][0] & -stages[last][0])
@@ -320,9 +368,31 @@
     far_pair[0], = hold(far_pair[0])
     across_keys = swap(far_pair[0], 1)
     attend(last - 1, [0, 1])
+    ahead = stage_query[last - 1]
+    block = jax.ShapeDtypeStruct((shard_keys, stage_rows), jnp.bfloat16)
+    weighed = pl.pallas_call(
+        functools.partial(weigh_kernel, scale, last - 1, [2, 3]),
+        in_specs=[vmem] * 4,
+        out_specs=[vmem] * 4,
+        out_shape=[block, block, stat, stat],
+        scratch_shapes=[pltpu.VMEM((2, shard_keys, tile), jnp.float32)],
+        compiler_params=params,
+        name="weigh",
+    )(chain[0], ahead, far_pair[0], across_keys)
+    weighed = hold(*weighed)
     far_pair[1], = hold(far_pair[1])
     across_values = swap(far_pair[1], 1)
     pairs += [far_pair, [across_keys, across_values]]
+    packed = pl.pallas_call(
+        functools.partial(finish_kernel, 2, whole_plan),
+        in_specs=[vmem] * 9,
+        out_specs=vmem,
+        out_shape=packed_shape(stage_rows),
+        scratch_shapes=[pltpu.VMEM((2, head_width + extra_rows, shard_keys), jnp.bfloat16)],
+        compiler_params=params,
+        name="finish",
+    )(far_pair[1], across_values, *weighed, *states[last - 1])
+    (packed,) = hold(packed)
     own_plan = [(at, "float", 0, at * tile, tile) for at in tiles]
     parts = []
 
@@ -333,9 +403,7 @@
                 parts.append(swap(piece, inner * k))
 
     coded = [packed_shape(stage_rows)]
-    attend(last - 1, [2])
     if outer == 4:
-        (packed,) = attend(2, [3], whole_plan, coded)
         handed = swap(packed, inner)
         (packed,) = attend(1, [2, 3], whole_plan, coded)
         parts.append(swap(packed, inner))
@@ -352,16 +420,16 @@
         (joined,) = hold(joined)
         parts.append(swap(joined, 3 * inner))
     else:
-        send(last - 1, attend(last - 1, [3], whole_plan, coded)[0])
+        send(last - 1, packed)
         send(last, attend(last, [0, 1, 2, 3], whole_plan, coded)[0])
         for index in range(last - 2, 0, -1):
             send(index, attend(index, [2, 3], whole_plan, coded)[0])
     if per_stage == 1:
-        own = attend(0, [2, 3], own_plan, float_shapes(rows))
+        own = attend(0, [1, 2, 3], own_plan, float_shapes(rows))
     else:
         own_plan = [(0, "float", 1, 0, rows)]
         packed, *own = attend(
-            0, [2, 3], whole_plan + own_plan, [packed_shape(stage_rows)] + float_shapes(rows)
+            0, [1, 2, 3], whole_plan + own_plan, [packed_shape(stage_rows)] + float_shapes(rows)
         )
         send(0, packed)
     groups = [(slice(0, rows), [(at, 0) for at in range(len(parts))])]

time: 41.5 us -> 46.4 us (1.12)
  waiting for transfers between devices: 9.79 us -> 16.5 us
  starting transfers between devices: 15.1 us -> 13.2 us
    ppermute x12, waiting for transfers between devices: 9.79 us -> 16.5 us  [swap(): return lax.ppermute(array, 'ctx', [(i, i ^ step) for i in range(size)])]
    pallas_call x0 -> x2, Pallas kernels: none -> 1.93 us  [the longest x1 1.33 us: local(): pl.pallas_call(functools.partial(weigh_kernel, scale, last - 1, [2, 3]),...]
    ppermute x12, starting transfers between devices: 15.1 us -> 13.2 us  [swap(): return lax.ppermute(array, 'ctx', [(i, i ^ step) for i in range(size)])]
    pallas_call x8 -> x6, Pallas kernels: 13.8 us -> 11.9 us  [attend(): pl.pallas_call(functools.partial(attend_kernel, scale, index, blocks, sta...]
  transfers between devices with their start and end apart: 12 -> 12, of which waited for: 6 -> 6; matrix products, arithmetic and copies ran while one was open for 0% -> 0% of each run, Pallas kernels for 31% -> 29%
where the time goes in v5:
time: 46.4 us; the launch traced here: 46.2 us
  waiting for transfers between devices  16.5 us (36%)
  Pallas kernels  15 us (32%)
  starting transfers between devices  13.2 us (28%)
  between operations  0.79 us (2%)
  local copies, waits for them, and re-layouts  0.69 us (1%)
    ppermute x12, waiting for transfers between devices, swap(): return lax.ppermute(array, 'ctx', [(i, i ^ step) for i in range(size)])  16.5 us
    ppermute x12, starting transfers between devices, swap(): return lax.ppermute(array, 'ctx', [(i, i ^ step) for i in range(size)])  13.2 us
    pallas_call x6, Pallas kernels, attend(): pl.pallas_call(functools.partial(attend_kernel, scale, index, blocks, sta...  11.9 us
    pallas_call x1, Pallas kernels, local(): pl.pallas_call(functools.partial(weigh_kernel, scale, last - 1, [2, 3]),...  1.33 us
    pallas_call x1, Pallas kernels, local(): pl.pallas_call(functools.partial(merge_kernel, groups), in_specs=[vmem] *...  0.94 us
  transfers between devices with their start and end apart: 12, of which 6 were waited for; matrix products, arithmetic and copies ran while one was open for 0% of the time, Pallas kernels for 29%

profile of v5, /device:TPU:0, one launch (start us, length us, event | category | flops | bytes accessed | tf_op | source)
XLA Modules:
  0.0 46.2 jit_solution(2722996835788386859)
XLA Ops:
  0.0 0.5 %collective-permute-start.1 = (bf16[1024,128]{1,0:T(8,128)(2,1)}, bf16[1024,128]{1,0:T(8,128)(2,1)S(1)}, u32[]{:S(2)}, u32[]{:S(2)}) collective-permute-start(bf16[1024,128]{1,0:T(8,128)(2,1)} %refs_3_.1), channel_id=1, source_target_pairs={{0,1},{1,0},{2,3},{3,2},{4,5},{5,4},{6,7},{7,6},{8,9},{9,8},{10,11... | collective-permute-start | bytes 786440 | tf_op jit(solution)/shard_map/ppermute | solution.py:263
  0.5 0.0 collective-permute-start.2
  0.5 3.0 %collective-permute-start.4 = (bf16[1024,128]{1,0:T(8,128)(2,1)}, bf16[1024,128]{1,0:T(8,128)(2,1)S(1)}, u32[]{:S(2)}, u32[]{:S(2)}) collective-permute-start(bf16[1024,128]{1,0:T(8,128)(2,1)} %refs_3_.1), channel_id=1, source_target_pairs={{0,2},{1,3},{2,0},{3,1},{4,6},{5,7},{6,4},{7,5},{8,10},{9,11},{10,... | collective-permute-start | bytes 786440 | tf_op jit(solution)/shard_map/ppermute | solution.py:263
  3.5 1.6 %collective-permute-start = (bf16[512,128]{1,0:T(8,128)(2,1)}, bf16[512,128]{1,0:T(8,128)(2,1)S(1)}, u32[]{:S(2)}, u32[]{:S(2)}) collective-permute-start(bf16[512,128]{1,0:T(8,128)(2,1)} %bitcast.5), channel_id=1, source_target_pairs={{0,4},{1,5},{2,6},{3,7},{4,0},{5,1},{6,2},{7,3},{8,12},{9,13},{10,... | collective-permute-start | bytes 393224 | tf_op jit(solution)/shard_map/ppermute | solution.py:263
  5.1 2.6 %collective-permute-start.3 = (bf16[512,128]{1,0:T(8,128)(2,1)}, bf16[512,128]{1,0:T(8,128)(2,1)S(1)}, u32[]{:S(2)}, u32[]{:S(2)}) collective-permute-start(bf16[512,128]{1,0:T(8,128)(2,1)} %bitcast.6), channel_id=1, source_target_pairs={{0,8},{1,9},{2,10},{3,11},{4,12},{5,13},{6,14},{7,15},{8,0},{9,1},... | collective-permute-start | bytes 393224 | tf_op jit(solution)/shard_map/ppermute | solution.py:263
  8.3 0.0 copy-start.1
  8.3 0.7 %copy-done.1 = s32[512]{0:T(512)S(1)} copy-done((s32[512]{0:T(512)S(1)}, s32[512]{0:T(512)}, u32[]{:S(2)}) %copy-start.1) | copy-done | bytes 2072
  9.0 2.1 %shard_map.55 = (f32[1,512]{1,0:T(1,128)S(1)}, f32[1,512]{1,0:T(1,128)S(1)}, f32[128,512]{1,0:T(8,128)S(1)}, s32[4,512]{1,0:T(4,128)S(1)}, bf16[1024,128]{1,0:T(8,128)(2,1)S(1)}, /*index=5*/bf16[1024,128]{1,0:T(8,128)(2,1)S(1)}) custom-call(s32[4,128]{1,0:T(4,128)S(1)} %bitcast.9, s32[1,1]{1,0:T(1,128)} %bitcast.4.refs_1_, bf16[512,128]{1,0:T(8,128)(2,1)} %bitcast.7, ...), custom_call_target="tpu_custom_call" | custom-call | tf_op jit(solution)/shard_map/pallas_call | solution.py:327
  11.1 0.0 collective-permute-done.refs_1_
  11.1 0.0 collective-permute-done.1.refs_4_.refs_2_
  11.2 0.0 collective-permute-done.2.refs_5_.refs_3_
  11.2 0.0 copy-start.2
  11.2 1.5 %shard_map.56 = (f32[1,512]{1,0:T(1,128)S(1)}, f32[1,512]{1,0:T(1,128)S(1)}, f32[128,512]{1,0:T(8,128)S(1)}) custom-call(s32[4,512]{1,0:T(4,128)S(1)} %get-tuple-element.107.refs_0_.limits_ref, bf16[512,128]{1,0:T(8,128)(2,1)S(1)} %collective-permute-done.refs_1_, bf16[1024,128]{1,0:T(8,128)(2,1)S(1)} %get-tuple-element.66.refs_2_, ...), custom_call_target="tpu_custom_call" | custom-call | tf_op jit(solution)/shard_map/pallas_call | solution.py:327
  12.7 1.2 %collective-permute-done.3.refs_1_.q_ref = bf16[512,128]{1,0:T(8,128)(2,1)S(1)} collective-permute-done((bf16[512,128]{1,0:T(8,128)(2,1)}, bf16[512,128]{1,0:T(8,128)(2,1)S(1)}, u32[]{:S(2)}, u32[]{:S(2)}) %collective-permute-start.3) | collective-permute-done | bytes 131104 | tf_op jit(solution)/shard_map/ppermute | solution.py:263
  13.9 0.0 collective-permute-done.4.refs_0_.refs_2_.refs_6_.refs_4_
  13.9 0.0 collective-permute-start.5
  13.9 0.0 copy-done.2
  13.9 0.6 %collective-permute-start.6 = (bf16[1024,128]{1,0:T(8,128)(2,1)S(1)}, bf16[1024,128]{1,0:T(8,128)(2,1)S(1)}, u32[]{:S(2)}, u32[]{:S(2)}) collective-permute-start(bf16[1024,128]{1,0:T(8,128)(2,1)S(1)} %copy-done.2), channel_id=1, source_target_pairs={{0,2},{1,3},{2,0},{3,1},{4,6},{5,7},{6,4},{7,5},{8,10},{9,11},{10,... | collective-permute-start | bytes 786440 | tf_op jit(solution)/shard_map/ppermute | solution.py:263
  14.5 1.5 %shard_map.57 = (f32[1,512]{1,0:T(1,128)S(1)}, f32[1,512]{1,0:T(1,128)S(1)}, f32[128,512]{1,0:T(8,128)S(1)}) custom-call(s32[4,512]{1,0:T(4,128)S(1)} %get-tuple-element.107.refs_0_.limits_ref, bf16[512,128]{1,0:T(8,128)(2,1)S(1)} %collective-permute-done.3.refs_1_.q_ref, bf16[1024,128]{1,0:T(8,128)(2,1)S(1)} %get-tuple-element.66.refs_2_, ...), custom_call_target="tpu_custom_call" | custom-call | tf_op jit(solution)/shard_map/pallas_call | solution.py:327
  16.0 0.0 collective-permute-done.5.refs_1_.refs_4_.refs_8_.refs_6_
  16.0 1.3 %weigh.1 = (bf16[1024,512]{1,0:T(8,128)(2,1)S(1)}, bf16[1024,512]{1,0:T(8,128)(2,1)S(1)}, f32[1,512]{1,0:T(1,128)S(1)}, f32[1,512]{1,0:T(1,128)S(1)}) custom-call(s32[4,512]{1,0:T(4,128)S(1)} %get-tuple-element.107.refs_0_.limits_ref, bf16[512,128]{1,0:T(8,128)(2,1)S(1)} %collective-permute-done.3.refs_1_.q_ref, ...), custom_call_target="tpu_custom_call" | custom-call | tf_op jit(solution)/shard_map/weigh/pallas_call | solution.py:373
  17.4 5.3 %collective-permute-done.6.refs_0_.refs_3_.refs_7_.refs_5_ = bf16[1024,128]{1,0:T(8,128)(2,1)S(1)} collective-permute-done((bf16[1024,128]{1,0:T(8,128)(2,1)S(1)}, bf16[1024,128]{1,0:T(8,128)(2,1)S(1)}, u32[]{:S(2)}, u32[]{:S(2)}) %collective-permute-start.6) | collective-permute-done | bytes 262176 | tf_op jit(solution)/shard_map/ppermute | solution.py:263
  22.6 0.0 collective-permute-start.7
  22.6 1.5 %collective-permute-done.7.refs_1_.refs_5_.refs_9_.refs_7_ = bf16[1024,128]{1,0:T(8,128)(2,1)S(1)} collective-permute-done((bf16[1024,128]{1,0:T(8,128)(2,1)S(1)}, bf16[1024,128]{1,0:T(8,128)(2,1)S(1)}, u32[]{:S(2)}, u32[]{:S(2)}) %collective-permute-start.7) | collective-permute-done | bytes 262176 | tf_op jit(solution)/shard_map/ppermute | solution.py:263
  24.2 0.6 %finish.1 = bf16[136,512]{1,0:T(8,128)(2,1)S(1)} custom-call(bf16[1024,128]{1,0:T(8,128)(2,1)S(1)} %collective-permute-done.6.refs_0_.refs_3_.refs_7_.refs_5_, bf16[1024,128]{1,0:T(8,128)(2,1)S(1)} %collective-permute-done.7.refs_1_.refs_5_.refs_9_.refs_7_, bf16[1024,512]{1,0:T(8,128)(2,1)S(1)} %get-tuple-element.86.refs_2_, ...), custom_call_target="tpu_custom_call" | custom-call | tf_op jit(solution)/shard_map/finish/pallas_call | solution.py:386
  24.8 0.5 %collective-permute-start.9 = (bf16[136,512]{1,0:T(8,128)(2,1)S(1)}, bf16[136,512]{1,0:T(8,128)(2,1)S(1)}, u32[]{:S(2)}, u32[]{:S(2)}) collective-permute-start(bf16[136,512]{1,0:T(8,128)(2,1)S(1)} %finish.1), channel_id=1, source_target_pairs={{0,4},{1,5},{2,6},{3,7},{4,0},{5,1},{6,2},{7,3},{8,12},{9,13},{10,... | collective-permute-start | bytes 417800 | tf_op jit(solution)/shard_map/ppermute | solution.py:263
  25.3 1.6 %collective-permute-start.8 = (bf16[512,128]{1,0:T(8,128)(2,1)S(1)}, bf16[512,128]{1,0:T(8,128)(2,1)S(1)}, u32[]{:S(2)}, u32[]{:S(2)}) collective-permute-start(bf16[512,128]{1,0:T(8,128)(2,1)S(1)} %collective-permute-done.3.refs_1_.q_ref), channel_id=1, source_target_pairs={{0,4},{1,5},{2,6},{3,7},{4,0},{5,1},{6,2},{7,3},{8,12},{9,13},{10,... | collective-permute-start | bytes 393224 | tf_op jit(solution)/shard_map/ppermute | solution.py:263
  26.9 1.6 %shard_map.58 = bf16[136,512]{1,0:T(8,128)(2,1)S(1)} custom-call(s32[4,512]{1,0:T(4,128)S(1)} %get-tuple-element.107.refs_0_.limits_ref, bf16[512,128]{1,0:T(8,128)(2,1)S(1)} %collective-permute-done.refs_1_, bf16[1024,128]{1,0:T(8,128)(2,1)S(1)} %collective-permute-done.4.refs_0_.refs_2_.refs_6_.refs_4_, ...), custom_call_target="tpu_custom_call" | custom-call | tf_op jit(solution)/shard_map/pallas_call | solution.py:327
  28.5 4.9 %collective-permute-done.8.refs_1_ = bf16[512,128]{1,0:T(8,128)(2,1)S(1)} collective-permute-done((bf16[512,128]{1,0:T(8,128)(2,1)S(1)}, bf16[512,128]{1,0:T(8,128)(2,1)S(1)}, u32[]{:S(2)}, u32[]{:S(2)}) %collective-permute-start.8) | collective-permute-done | bytes 131104 | tf_op jit(solution)/shard_map/ppermute | solution.py:263
  33.4 2.9 %shard_map.59 = (f32[128,512]{1,0:T(8,128)S(1)}, f32[1,512]{1,0:T(1,128)S(1)}) custom-call(s32[4,512]{1,0:T(4,128)S(1)} %get-tuple-element.107.refs_0_.limits_ref, bf16[512,128]{1,0:T(8,128)(2,1)S(1)} %collective-permute-done.8.refs_1_, bf16[1024,128]{1,0:T(8,128)(2,1)S(1)} %get-tuple-element.66.refs_2_, bf16[1024,128]{1,0:T(8,128)(2,1)S(1)} %get-tuple-element.67.refs_3_, ...), custom_call_target="tpu_custom_call" | custom-call | tf_op jit(solution)/shard_map/pallas_call | solution.py:327
  36.2 0.0 copy-start
  36.2 0.5 %collective-permute-start.10 = (bf16[136,512]{1,0:T(8,128)(2,1)S(1)}, bf16[136,512]{1,0:T(8,128)(2,1)S(1)}, u32[]{:S(2)}, u32[]{:S(2)}) collective-permute-start(bf16[136,512]{1,0:T(8,128)(2,1)S(1)} %shard_map.58), channel_id=1, source_target_pairs={{0,4},{1,5},{2,6},{3,7},{4,0},{5,1},{6,2},{7,3},{8,12},{9,13},{10,... | collective-permute-start | bytes 417800 | tf_op jit(solution)/shard_map/ppermute | solution.py:263
  36.7 0.0 collective-permute-done.9.part_ref
  36.7 0.3 combine.1
  37.0 2.4 %collective-permute-start.11 = (bf16[136,512]{1,0:T(8,128)(2,1)S(1)}, bf16[136,512]{1,0:T(8,128)(2,1)S(1)}, u32[]{:S(2)}, u32[]{:S(2)}) collective-permute-start(bf16[136,512]{1,0:T(8,128)(2,1)S(1)} %combine.1), channel_id=1, source_target_pairs={{0,12},{1,13},{2,14},{3,15},{4,8},{5,9},{6,10},{7,11},{8,4},{9,5},... | collective-permute-start | bytes 417800 | tf_op jit(solution)/shard_map/ppermute | solution.py:263
  39.4 0.0 copy-done
  39.4 2.2 %shard_map.60 = (f32[128,512]{1,0:T(8,128)S(1)}, f32[1,512]{1,0:T(1,128)S(1)}) custom-call(s32[4,512]{1,0:T(4,128)S(1)} %get-tuple-element.107.refs_0_.limits_ref, bf16[512,128]{1,0:T(8,128)(2,1)S(1)} %bitcast.8, bf16[1024,128]{1,0:T(8,128)(2,1)S(1)} %collective-permute-done.1.refs_4_.refs_2_, bf16[1024,128]{1,0:T(8,128)(2,1)S(1)} %collective-permute-done.2.refs_5_.refs_3_, ...), custom_call_target="tpu_custom_call" | custom-call | tf_op jit(solution)/shard_map/pallas_call | solution.py:327
  41.6 0.4 collective-permute-done.10.refs_2_
  42.0 3.3 %collective-permute-done.11.refs_3_ = bf16[136,512]{1,0:T(8,128)(2,1)S(1)} collective-permute-done((bf16[136,512]{1,0:T(8,128)(2,1)S(1)}, bf16[136,512]{1,0:T(8,128)(2,1)S(1)}, u32[]{:S(2)}, u32[]{:S(2)}) %collective-permute-start.11) | collective-permute-done | bytes 139296 | tf_op jit(solution)/shard_map/ppermute | solution.py:263
  45.2 0.9 %merge.1 = bf16[512,128]{1,0:T(8,128)(2,1)} custom-call(f32[128,512]{1,0:T(8,128)S(1)} %get-tuple-element.113.refs_0_, f32[1,512]{1,0:T(1,128)S(1)} %get-tuple-element.114.refs_1_, bf16[136,512]{1,0:T(8,128)(2,1)S(1)} %collective-permute-done.10.refs_2_, bf16[136,512]{1,0:T(8,128)(2,1)S(1)} %collective-permute-done.11.refs_3_), custom_call_target="tpu_custom_call" | custom-call | tf_op jit(solution)/shard_map/merge/pallas_call | solution.py:436
Async XLA Ops:
  0.0 11.1 %collective-permute-start.1 = (bf16[1024,128]{1,0:T(8,128)(2,1)}, bf16[1024,128]{1,0:T(8,128)(2,1)S(1)}, u32[]{:S(2)}, u32[]{:S(2)}) collective-permute-start(bf16[1024,128]{1,0:T(8,128)(2,1)} %refs_3_.1), channel_id=1, source_target_pairs={{0,1},{1,0},{2,3},{3,2},{4,5},{5,4},{6,7},{7,6},{8,9},{9,8},{10,11... | collective-permute-start | bytes 786440 | tf_op jit(solution)/shard_map/ppermute | solution.py:263
  0.5 10.7 %collective-permute-start.2 = (bf16[1024,128]{1,0:T(8,128)(2,1)}, bf16[1024,128]{1,0:T(8,128)(2,1)S(1)}, u32[]{:S(2)}, u32[]{:S(2)}) collective-permute-start(bf16[1024,128]{1,0:T(8,128)(2,1)} %refs_4_.1), channel_id=1, source_target_pairs={{0,1},{1,0},{2,3},{3,2},{4,5},{5,4},{6,7},{7,6},{8,9},{9,8},{10,11... | collective-permute-start | bytes 786440 | tf_op jit(solution)/shard_map/ppermute | solution.py:263
  0.5 13.4 %collective-permute-start.4 = (bf16[1024,128]{1,0:T(8,128)(2,1)}, bf16[1024,128]{1,0:T(8,128)(2,1)S(1)}, u32[]{:S(2)}, u32[]{:S(2)}) collective-permute-start(bf16[1024,128]{1,0:T(8,128)(2,1)} %refs_3_.1), channel_id=1, source_target_pairs={{0,2},{1,3},{2,0},{3,1},{4,6},{5,7},{6,4},{7,5},{8,10},{9,11},{10,... | collective-permute-start | bytes 786440 | tf_op jit(solution)/shard_map/ppermute | solution.py:263
  3.5 7.6 %collective-permute-start = (bf16[512,128]{1,0:T(8,128)(2,1)}, bf16[512,128]{1,0:T(8,128)(2,1)S(1)}, u32[]{:S(2)}, u32[]{:S(2)}) collective-permute-start(bf16[512,128]{1,0:T(8,128)(2,1)} %bitcast.5), channel_id=1, source_target_pairs={{0,4},{1,5},{2,6},{3,7},{4,0},{5,1},{6,2},{7,3},{8,12},{9,13},{10,... | collective-permute-start | bytes 393224 | tf_op jit(solution)/shard_map/ppermute | solution.py:263
  5.1 8.8 %collective-permute-start.3 = (bf16[512,128]{1,0:T(8,128)(2,1)}, bf16[512,128]{1,0:T(8,128)(2,1)S(1)}, u32[]{:S(2)}, u32[]{:S(2)}) collective-permute-start(bf16[512,128]{1,0:T(8,128)(2,1)} %bitcast.6), channel_id=1, source_target_pairs={{0,8},{1,9},{2,10},{3,11},{4,12},{5,13},{6,14},{7,15},{8,0},{9,1},... | collective-permute-start | bytes 393224 | tf_op jit(solution)/shard_map/ppermute | solution.py:263
  8.3 0.7 %copy-start.1 = (s32[512]{0:T(512)S(1)}, s32[512]{0:T(512)}, u32[]{:S(2)}) copy-start(s32[512]{0:T(512)} %param.9) | copy-start | bytes 6148
  11.2 2.8 %copy-start.2 = (bf16[1024,128]{1,0:T(8,128)(2,1)S(1)}, bf16[1024,128]{1,0:T(8,128)(2,1)}, u32[]{:S(2)}) copy-start(bf16[1024,128]{1,0:T(8,128)(2,1)} %refs_4_.1) | copy-start | bytes 786436
  13.9 2.1 %collective-permute-start.5 = (bf16[1024,128]{1,0:T(8,128)(2,1)S(1)}, bf16[1024,128]{1,0:T(8,128)(2,1)S(1)}, u32[]{:S(2)}, u32[]{:S(2)}) collective-permute-start(bf16[1024,128]{1,0:T(8,128)(2,1)S(1)} %collective-permute-done.4.refs_0_.refs_2_.refs_6_.refs_4_), channel_id=1, source_target_pairs={{0,1},{1,0},{2,3},{3,2},{4,5},{5,4},{6,7},{7,6},{8,9},{9,8},{10,11... | collective-permute-start | bytes 786440 | tf_op jit(solution)/shard_map/ppermute | solution.py:263
  13.9 8.7 %collective-permute-start.6 = (bf16[1024,128]{1,0:T(8,128)(2,1)S(1)}, bf16[1024,128]{1,0:T(8,128)(2,1)S(1)}, u32[]{:S(2)}, u32[]{:S(2)}) collective-permute-start(bf16[1024,128]{1,0:T(8,128)(2,1)S(1)} %copy-done.2), channel_id=1, source_target_pairs={{0,2},{1,3},{2,0},{3,1},{4,6},{5,7},{6,4},{7,5},{8,10},{9,11},{10,... | collective-permute-start | bytes 786440 | tf_op jit(solution)/shard_map/ppermute | solution.py:263
  22.6 1.5 %collective-permute-start.7 = (bf16[1024,128]{1,0:T(8,128)(2,1)S(1)}, bf16[1024,128]{1,0:T(8,128)(2,1)S(1)}, u32[]{:S(2)}, u32[]{:S(2)}) collective-permute-start(bf16[1024,128]{1,0:T(8,128)(2,1)S(1)} %collective-permute-done.6.refs_0_.refs_3_.refs_7_.refs_5_), channel_id=1, source_target_pairs={{0,1},{1,0},{2,3},{3,2},{4,5},{5,4},{6,7},{7,6},{8,9},{9,8},{10,11... | collective-permute-start | bytes 786440 | tf_op jit(solution)/shard_map/ppermute | solution.py:263
  24.8 12.0 %collective-permute-start.9 = (bf16[136,512]{1,0:T(8,128)(2,1)S(1)}, bf16[136,512]{1,0:T(8,128)(2,1)S(1)}, u32[]{:S(2)}, u32[]{:S(2)}) collective-permute-start(bf16[136,512]{1,0:T(8,128)(2,1)S(1)} %finish.1), channel_id=1, source_target_pairs={{0,4},{1,5},{2,6},{3,7},{4,0},{5,1},{6,2},{7,3},{8,12},{9,13},{10,... | collective-permute-start | bytes 417800 | tf_op jit(solution)/shard_map/ppermute | solution.py:263
  25.3 8.1 %collective-permute-start.8 = (bf16[512,128]{1,0:T(8,128)(2,1)S(1)}, bf16[512,128]{1,0:T(8,128)(2,1)S(1)}, u32[]{:S(2)}, u32[]{:S(2)}) collective-permute-start(bf16[512,128]{1,0:T(8,128)(2,1)S(1)} %collective-permute-done.3.refs_1_.q_ref), channel_id=1, source_target_pairs={{0,4},{1,5},{2,6},{3,7},{4,0},{5,1},{6,2},{7,3},{8,12},{9,13},{10,... | collective-permute-start | bytes 393224 | tf_op jit(solution)/shard_map/ppermute | solution.py:263
  36.2 3.1 %copy-start = (bf16[32,16,128]{2,1,0:T(8,128)(2,1)S(1)}, bf16[32,16,128]{2,1,0:T(8,128)(2,1)}, u32[]{:S(2)}) copy-start(bf16[32,16,128]{2,1,0:T(8,128)(2,1)} %param.5) | copy-start | bytes 393220
  36.2 5.7 %collective-permute-start.10 = (bf16[136,512]{1,0:T(8,128)(2,1)S(1)}, bf16[136,512]{1,0:T(8,128)(2,1)S(1)}, u32[]{:S(2)}, u32[]{:S(2)}) collective-permute-start(bf16[136,512]{1,0:T(8,128)(2,1)S(1)} %shard_map.58), channel_id=1, source_target_pairs={{0,4},{1,5},{2,6},{3,7},{4,0},{5,1},{6,2},{7,3},{8,12},{9,13},{10,... | collective-permute-start | bytes 417800 | tf_op jit(solution)/shard_map/ppermute | solution.py:263
  37.0 8.2 %collective-permute-start.11 = (bf16[136,512]{1,0:T(8,128)(2,1)S(1)}, bf16[136,512]{1,0:T(8,128)(2,1)S(1)}, u32[]{:S(2)}, u32[]{:S(2)}) collective-permute-start(bf16[136,512]{1,0:T(8,128)(2,1)S(1)} %combine.1), channel_id=1, source_target_pairs={{0,12},{1,13},{2,14},{3,15},{4,8},{5,9},{6,10},{7,11},{8,4},{9,5},... | collective-permute-start | bytes 417800 | tf_op jit(solution)/shard_map/ppermute | solution.py:263

commit v6 on v5

--- a/solution.py
+++ b/solution.py
@@ -117,6 +117,13 @@
     values, weights, tops = refs[:count], refs[count : 2 * count], refs[2 * count : 3 * count]
     state_refs, outs, values_ref = refs[3 * count : 3 * count + 3], refs[3 * count + 3 : -1], refs[-1]
     transpose_values(values, values_ref)
+    if plan is None:
+        state = tuple(ref[...] for ref in state_refs)
+        for b in range(count):
+            state = add_block(state, values_ref[b], weights[b][...], tops[b][...])
+        for ref, value in zip(outs, state):
+            ref[...] = value
+        return
     for at, form, out, offset, lanes in plan:
         span = slice(at * lanes, (at + 1) * lanes)
         state = tuple(ref[:, span] for ref in state_refs)
@@ -229,11 +236,11 @@
     return value, top + jnp.log2(total)
 
 
-def combine_kernel(value_ref, level_ref, part_ref, out_ref):
+def combine_kernel(form, value_ref, level_ref, part_ref, *out_refs):
     width, lanes = value_ref.shape
     value, level = decode(part_ref[:width, :], part_ref[width:, :])
     value, level = combine([value_ref[...], value], [level_ref[...], level])
-    write_partial([out_ref], "code", slice(0, lanes), value, level)
+    write_partial(out_refs, form, slice(0, lanes), value, level)
 
 
 def merge_kernel(groups, *refs):
@@ -361,13 +368,13 @@
     attend(0, [0])
     for index in range(1, last - 1):
         attend(index, [0, 1])
+    far_pair[0], = hold(far_pair[0])
+    across_keys = swap(far_pair[0], 1)
+    attend(last - 1, [0, 1])
     source = stages[last][0] ^ (stages[last][0] & -stages[last][0])
     (got[source],) = hold(got[source])
     gather(last)
     ready(last)
-    far_pair[0], = hold(far_pair[0])
-    across_keys = swap(far_pair[0], 1)
-    attend(last - 1, [0, 1])
     ahead = stage_query[last - 1]
     block = jax.ShapeDtypeStruct((shard_keys, stage_rows), jnp.bfloat16)
     weighed = pl.pallas_call(
@@ -383,16 +390,24 @@
     far_pair[1], = hold(far_pair[1])
     across_values = swap(far_pair[1], 1)
     pairs += [far_pair, [across_keys, across_values]]
-    packed = pl.pallas_call(
-        functools.partial(finish_kernel, 2, whole_plan),
-        in_specs=[vmem] * 9,
-        out_specs=vmem,
-        out_shape=packed_shape(stage_rows),
-        scratch_shapes=[pltpu.VMEM((2, head_width + extra_rows, shard_keys), jnp.bfloat16)],
-        compiler_params=params,
-        name="finish",
-    )(far_pair[1], across_values, *weighed, *states[last - 1])
-    (packed,) = hold(packed)
+
+    def finish(values, weights, top, plan, shapes):
+        results = pl.pallas_call(
+            functools.partial(finish_kernel, 1, plan),
+            in_specs=[vmem] * 6,
+            out_specs=[vmem] * len(shapes),
+            out_shape=shapes,
+            scratch_shapes=[pltpu.VMEM((1, head_width + extra_rows, shard_keys), jnp.bfloat16)],
+            compiler_params=params,
+        )(values, weights, top, *states[last - 1])
+        return hold(*results)
+
+    states[last - 1] = finish(far_pair[1], weighed[0], weighed[2], None, state_shapes)
+    if outer == 4:
+        attend(1, [2])
+    (across_values,) = hold(across_values)
+    pairs[3] = [across_keys, across_values]
+    (packed,) = finish(across_values, weighed[1], weighed[3], whole_plan, [packed_shape(stage_rows)])
     own_plan = [(at, "float", 0, at * tile, tile) for at in tiles]
     parts = []
 
@@ -403,20 +418,23 @@
                 parts.append(swap(piece, inner * k))
 
     coded = [packed_shape(stage_rows)]
+
+    def fold(form, value, level, part, shapes):
+        return pl.pallas_call(
+            functools.partial(combine_kernel, form),
+            in_specs=[vmem] * 3,
+            out_specs=[vmem] * len(shapes),
+            out_shape=shapes,
+            compiler_params=params,
+        )(value, level, part)
+
     if outer == 4:
         handed = swap(packed, inner)
-        (packed,) = attend(1, [2, 3], whole_plan, coded)
+        (packed,) = attend(1, [3], whole_plan, coded)
         parts.append(swap(packed, inner))
         value, level = attend(3, [0, 1, 2, 3], own_plan, float_shapes(stage_rows))
         (handed,) = hold(handed)
-        joined = pl.pallas_call(
-            combine_kernel,
-            in_specs=[vmem] * 3,
-            out_specs=vmem,
-            out_shape=coded[0],
-            compiler_params=params,
-            name="combine",
-        )(value, level, handed)
+        (joined,) = fold("code", value, level, handed, coded)
         (joined,) = hold(joined)
         parts.append(swap(joined, 3 * inner))
     else:
@@ -426,6 +444,8 @@
             send(index, attend(index, [2, 3], whole_plan, coded)[0])
     if per_stage == 1:
         own = attend(0, [1, 2, 3], own_plan, float_shapes(rows))
+        if outer == 4:
+            own = fold("float", *own, parts.pop(0), float_shapes(rows))
     else:
         own_plan = [(0, "float", 1, 0, rows)]
         packed, *own = attend(

time: 46.4 us -> 49 us (1.056)
  starting transfers between devices: 13.2 us -> 15.3 us
    ppermute x12, starting transfers between devices: 13.2 us -> 15.3 us  [swap(): return lax.ppermute(array, 'ctx', [(i, i ^ step) for i in range(size)])]
    pallas_call x2 -> x4, Pallas kernels: 0.85 us -> 1.21 us  [the longest x2 0.85 us: finish(): pl.pallas_call(functools.partial(finish_kernel, 1, plan), in_specs=[vmem]...]
    pallas_call x6 -> x7, Pallas kernels: 11.9 us -> 12.1 us  [attend(): pl.pallas_call(functools.partial(attend_kernel, scale, index, blocks, sta...]
  transfers between devices with their start and end apart: 12 -> 12, of which waited for: 6 -> 5; matrix products, arithmetic and copies ran while one was open for 0% -> 0% of each run, Pallas kernels for 29% -> 29%
where the time goes in v6:
time: 49 us; the launch traced here: 48.8 us
  waiting for transfers between devices  16.6 us (34%)
  Pallas kernels  15.4 us (31%)
  starting transfers between devices  15.3 us (31%)
  between operations  0.82 us (2%)
  local copies, waits for them, and re-layouts  0.68 us (1%)
    ppermute x12, waiting for transfers between devices, swap(): return lax.ppermute(array, 'ctx', [(i, i ^ step) for i in range(size)])  16.6 us
    ppermute x12, starting transfers between devices, swap(): return lax.ppermute(array, 'ctx', [(i, i ^ step) for i in range(size)])  15.3 us
    pallas_call x7, Pallas kernels, attend(): pl.pallas_call(functools.partial(attend_kernel, scale, index, blocks, sta...  12.1 us
    pallas_call x1, Pallas kernels, local(): pl.pallas_call(functools.partial(weigh_kernel, scale, last - 1, [2, 3]),...  1.32 us
  transfers between devices with their start and end apart: 12, of which 5 were waited for; matrix products, arithmetic and copies ran while one was open for 0% of the time, Pallas kernels for 29%

profile of v6, /device:TPU:0, one launch (start us, length us, event | category | flops | bytes accessed | tf_op | source)
XLA Modules:
  0.0 48.8 jit_solution(2869335131242726935)
XLA Ops:
  0.0 0.5 %collective-permute-start.1 = (bf16[1024,128]{1,0:T(8,128)(2,1)}, bf16[1024,128]{1,0:T(8,128)(2,1)S(1)}, u32[]{:S(2)}, u32[]{:S(2)}) collective-permute-start(bf16[1024,128]{1,0:T(8,128)(2,1)} %refs_3_.1), channel_id=1, source_target_pairs={{0,1},{1,0},{2,3},{3,2},{4,5},{5,4},{6,7},{7,6},{8,9},{9,8},{10,11... | collective-permute-start | bytes 786440 | tf_op jit(solution)/shard_map/ppermute | solution.py:270
  0.5 0.0 collective-permute-start.2
  0.5 3.0 %collective-permute-start.3 = (bf16[1024,128]{1,0:T(8,128)(2,1)}, bf16[1024,128]{1,0:T(8,128)(2,1)S(1)}, u32[]{:S(2)}, u32[]{:S(2)}) collective-permute-start(bf16[1024,128]{1,0:T(8,128)(2,1)} %refs_3_.1), channel_id=1, source_target_pairs={{0,2},{1,3},{2,0},{3,1},{4,6},{5,7},{6,4},{7,5},{8,10},{9,11},{10,... | collective-permute-start | bytes 786440 | tf_op jit(solution)/shard_map/ppermute | solution.py:270
  3.5 1.6 %collective-permute-start = (bf16[512,128]{1,0:T(8,128)(2,1)}, bf16[512,128]{1,0:T(8,128)(2,1)S(1)}, u32[]{:S(2)}, u32[]{:S(2)}) collective-permute-start(bf16[512,128]{1,0:T(8,128)(2,1)} %bitcast.5), channel_id=1, source_target_pairs={{0,4},{1,5},{2,6},{3,7},{4,0},{5,1},{6,2},{7,3},{8,12},{9,13},{10,... | collective-permute-start | bytes 393224 | tf_op jit(solution)/shard_map/ppermute | solution.py:270
  5.7 0.0 copy-start.1
  5.7 0.7 %copy-done.1 = s32[512]{0:T(512)S(1)} copy-done((s32[512]{0:T(512)S(1)}, s32[512]{0:T(512)}, u32[]{:S(2)}) %copy-start.1) | copy-done | bytes 2072
  6.4 2.1 %shard_map.55 = (f32[1,512]{1,0:T(1,128)S(1)}, f32[1,512]{1,0:T(1,128)S(1)}, f32[128,512]{1,0:T(8,128)S(1)}, s32[4,512]{1,0:T(4,128)S(1)}, bf16[1024,128]{1,0:T(8,128)(2,1)S(1)}, /*index=5*/bf16[1024,128]{1,0:T(8,128)(2,1)S(1)}) custom-call(s32[4,128]{1,0:T(4,128)S(1)} %bitcast.9, s32[1,1]{1,0:T(1,128)} %bitcast.4.refs_1_, bf16[512,128]{1,0:T(8,128)(2,1)} %bitcast.6, ...), custom_call_target="tpu_custom_call" | custom-call | tf_op jit(solution)/shard_map/pallas_call | solution.py:334
  8.5 0.3 collective-permute-done.refs_1_
  8.8 0.0 collective-permute-done.1.refs_4_.refs_2_
  8.8 0.0 collective-permute-done.2.refs_5_.refs_3_
  8.8 0.0 copy-start.2
  8.9 0.0 copy-start
  8.9 1.5 %shard_map.56 = (f32[1,512]{1,0:T(1,128)S(1)}, f32[1,512]{1,0:T(1,128)S(1)}, f32[128,512]{1,0:T(8,128)S(1)}) custom-call(s32[4,512]{1,0:T(4,128)S(1)} %get-tuple-element.141.refs_0_.limits_ref, bf16[512,128]{1,0:T(8,128)(2,1)S(1)} %collective-permute-done.refs_1_, bf16[1024,128]{1,0:T(8,128)(2,1)S(1)} %get-tuple-element.84.refs_2_, ...), custom_call_target="tpu_custom_call" | custom-call | tf_op jit(solution)/shard_map/pallas_call | solution.py:334
  10.4 0.0 collective-permute-done.3.refs_0_.refs_2_.refs_6_.refs_4_
  10.4 0.1 collective-permute-start.5
  10.5 0.0 copy-done.2
  10.5 1.5 %collective-permute-start.6 = (bf16[1024,128]{1,0:T(8,128)(2,1)S(1)}, bf16[1024,128]{1,0:T(8,128)(2,1)S(1)}, u32[]{:S(2)}, u32[]{:S(2)}) collective-permute-start(bf16[1024,128]{1,0:T(8,128)(2,1)S(1)} %copy-done.2), channel_id=1, source_target_pairs={{0,2},{1,3},{2,0},{3,1},{4,6},{5,7},{6,4},{7,5},{8,10},{9,11},{10,... | collective-permute-start | bytes 786440 | tf_op jit(solution)/shard_map/ppermute | solution.py:270
  11.9 0.0 copy-done
  11.9 2.6 %collective-permute-start.4 = (bf16[512,128]{1,0:T(8,128)(2,1)S(1)}, bf16[512,128]{1,0:T(8,128)(2,1)S(1)}, u32[]{:S(2)}, u32[]{:S(2)}) collective-permute-start(bf16[512,128]{1,0:T(8,128)(2,1)S(1)} %bitcast.7), channel_id=1, source_target_pairs={{0,8},{1,9},{2,10},{3,11},{4,12},{5,13},{6,14},{7,15},{8,0},{9,1},... | collective-permute-start | bytes 393224 | tf_op jit(solution)/shard_map/ppermute | solution.py:270
  14.5 6.7 %collective-permute-done.4.refs_1_.q_ref = bf16[512,128]{1,0:T(8,128)(2,1)S(1)} collective-permute-done((bf16[512,128]{1,0:T(8,128)(2,1)S(1)}, bf16[512,128]{1,0:T(8,128)(2,1)S(1)}, u32[]{:S(2)}, u32[]{:S(2)}) %collective-permute-start.4) | collective-permute-done | bytes 131104 | tf_op jit(solution)/shard_map/ppermute | solution.py:270
  21.3 1.5 %shard_map.57 = (f32[1,512]{1,0:T(1,128)S(1)}, f32[1,512]{1,0:T(1,128)S(1)}, f32[128,512]{1,0:T(8,128)S(1)}) custom-call(s32[4,512]{1,0:T(4,128)S(1)} %get-tuple-element.141.refs_0_.limits_ref, bf16[512,128]{1,0:T(8,128)(2,1)S(1)} %collective-permute-done.4.refs_1_.q_ref, bf16[1024,128]{1,0:T(8,128)(2,1)S(1)} %get-tuple-element.84.refs_2_, ...), custom_call_target="tpu_custom_call" | custom-call | tf_op jit(solution)/shard_map/pallas_call | solution.py:334
  22.8 0.0 collective-permute-done.5.refs_1_.refs_2_.refs_8_.refs_6_
  22.8 1.3 %weigh.1 = (bf16[1024,512]{1,0:T(8,128)(2,1)S(1)}, bf16[1024,512]{1,0:T(8,128)(2,1)S(1)}, f32[1,512]{1,0:T(1,128)S(1)}, f32[1,512]{1,0:T(1,128)S(1)}) custom-call(s32[4,512]{1,0:T(4,128)S(1)} %get-tuple-element.141.refs_0_.limits_ref, bf16[512,128]{1,0:T(8,128)(2,1)S(1)} %collective-permute-done.4.refs_1_.q_ref, ...), custom_call_target="tpu_custom_call" | custom-call | tf_op jit(solution)/shard_map/weigh/pallas_call | solution.py:380
  24.1 0.0 collective-permute-done.6.refs_0_.refs_3_.refs_7_.refs_5_
  24.1 0.1 collective-permute-start.7
  24.2 0.4 shard_map.58
  24.6 0.9 %shard_map.59 = (f32[1,512]{1,0:T(1,128)S(1)}, f32[1,512]{1,0:T(1,128)S(1)}, f32[128,512]{1,0:T(8,128)S(1)}) custom-call(s32[4,512]{1,0:T(4,128)S(1)} %get-tuple-element.141.refs_0_.limits_ref, bf16[512,128]{1,0:T(8,128)(2,1)S(1)} %collective-permute-done.refs_1_, bf16[1024,128]{1,0:T(8,128)(2,1)S(1)} %collective-permute-done.3.refs_0_.refs_2_.refs_6_.refs_4_, ...), custom_call_target="tpu_custom_call" | custom-call | tf_op jit(solution)/shard_map/pallas_call | solution.py:334
  25.5 0.2 collective-permute-done.7.refs_0_.refs_3_.refs_9_.refs_7_
  25.7 0.5 %shard_map.60 = bf16[136,512]{1,0:T(8,128)(2,1)S(1)} custom-call(bf16[1024,128]{1,0:T(8,128)(2,1)S(1)} %collective-permute-done.7.refs_0_.refs_3_.refs_9_.refs_7_, bf16[1024,512]{1,0:T(8,128)(2,1)S(1)} %get-tuple-element.122.refs_1_, f32[1,512]{1,0:T(1,128)S(1)} %get-tuple-element.123.refs_2_, f32[1,512]{1,0:T(1,128)S(1)} %get-tuple-element.124.refs_3_, ...), custom_call_target="tpu_custom_call" | custom-call | tf_op jit(solution)/shard_map/pallas_call | solution.py:395
  26.2 0.7 %collective-permute-start.9 = (bf16[136,512]{1,0:T(8,128)(2,1)S(1)}, bf16[136,512]{1,0:T(8,128)(2,1)S(1)}, u32[]{:S(2)}, u32[]{:S(2)}) collective-permute-start(bf16[136,512]{1,0:T(8,128)(2,1)S(1)} %shard_map.60), channel_id=1, source_target_pairs={{0,4},{1,5},{2,6},{3,7},{4,0},{5,1},{6,2},{7,3},{8,12},{9,13},{10,... | collective-permute-start | bytes 417800 | tf_op jit(solution)/shard_map/ppermute | solution.py:270
  27.0 1.4 %collective-permute-start.8 = (bf16[512,128]{1,0:T(8,128)(2,1)S(1)}, bf16[512,128]{1,0:T(8,128)(2,1)S(1)}, u32[]{:S(2)}, u32[]{:S(2)}) collective-permute-start(bf16[512,128]{1,0:T(8,128)(2,1)S(1)} %collective-permute-done.4.refs_1_.q_ref), channel_id=1, source_target_pairs={{0,4},{1,5},{2,6},{3,7},{4,0},{5,1},{6,2},{7,3},{8,12},{9,13},{10,... | collective-permute-start | bytes 393224 | tf_op jit(solution)/shard_map/ppermute | solution.py:270
  28.3 1.0 %shard_map.61 = bf16[136,512]{1,0:T(8,128)(2,1)S(1)} custom-call(s32[4,512]{1,0:T(4,128)S(1)} %get-tuple-element.141.refs_0_.limits_ref, bf16[512,128]{1,0:T(8,128)(2,1)S(1)} %collective-permute-done.refs_1_, bf16[1024,128]{1,0:T(8,128)(2,1)S(1)} %collective-permute-done.5.refs_1_.refs_2_.refs_8_.refs_6_, ...), custom_call_target="tpu_custom_call" | custom-call | tf_op jit(solution)/shard_map/pallas_call | solution.py:334
  29.4 5.6 %collective-permute-done.8.refs_1_ = bf16[512,128]{1,0:T(8,128)(2,1)S(1)} collective-permute-done((bf16[512,128]{1,0:T(8,128)(2,1)S(1)}, bf16[512,128]{1,0:T(8,128)(2,1)S(1)}, u32[]{:S(2)}, u32[]{:S(2)}) %collective-permute-start.8) | collective-permute-done | bytes 131104 | tf_op jit(solution)/shard_map/ppermute | solution.py:270
  35.0 2.8 %shard_map.62 = (f32[128,512]{1,0:T(8,128)S(1)}, f32[1,512]{1,0:T(1,128)S(1)}) custom-call(s32[4,512]{1,0:T(4,128)S(1)} %get-tuple-element.141.refs_0_.limits_ref, bf16[512,128]{1,0:T(8,128)(2,1)S(1)} %collective-permute-done.8.refs_1_, bf16[1024,128]{1,0:T(8,128)(2,1)S(1)} %get-tuple-element.84.refs_2_, bf16[1024,128]{1,0:T(8,128)(2,1)S(1)} %get-tuple-element.85.refs_3_, ...), custom_call_target="tpu_custom_call" | custom-call | tf_op jit(solution)/shard_map/pallas_call | solution.py:334
  37.8 0.7 %collective-permute-start.10 = (bf16[136,512]{1,0:T(8,128)(2,1)S(1)}, bf16[136,512]{1,0:T(8,128)(2,1)S(1)}, u32[]{:S(2)}, u32[]{:S(2)}) collective-permute-start(bf16[136,512]{1,0:T(8,128)(2,1)S(1)} %shard_map.61), channel_id=1, source_target_pairs={{0,4},{1,5},{2,6},{3,7},{4,0},{5,1},{6,2},{7,3},{8,12},{9,13},{10,... | collective-permute-start | bytes 417800 | tf_op jit(solution)/shard_map/ppermute | solution.py:270
  38.5 0.0 collective-permute-done.9.part_ref
  38.5 0.3 shard_map.63
  38.8 3.2 %collective-permute-start.11 = (bf16[136,512]{1,0:T(8,128)(2,1)S(1)}, bf16[136,512]{1,0:T(8,128)(2,1)S(1)}, u32[]{:S(2)}, u32[]{:S(2)}) collective-permute-start(bf16[136,512]{1,0:T(8,128)(2,1)S(1)} %shard_map.63), channel_id=1, source_target_pairs={{0,12},{1,13},{2,14},{3,15},{4,8},{5,9},{6,10},{7,11},{8,4},{9,5},... | collective-permute-start | bytes 417800 | tf_op jit(solution)/shard_map/ppermute | solution.py:270
  42.0 2.2 %shard_map.64 = (f32[128,512]{1,0:T(8,128)S(1)}, f32[1,512]{1,0:T(1,128)S(1)}) custom-call(s32[4,512]{1,0:T(4,128)S(1)} %get-tuple-element.141.refs_0_.limits_ref, bf16[512,128]{1,0:T(8,128)(2,1)S(1)} %bitcast.8, bf16[1024,128]{1,0:T(8,128)(2,1)S(1)} %collective-permute-done.1.refs_4_.refs_2_, bf16[1024,128]{1,0:T(8,128)(2,1)S(1)} %collective-permute-done.2.refs_5_.refs_3_, ...), custom_call_target="tpu_custom_call" | custom-call | tf_op jit(solution)/shard_map/pallas_call | solution.py:334
  44.2 0.0 collective-permute-done.10.part_ref
  44.2 0.1 shard_map.65
  44.3 3.7 %collective-permute-done.11.refs_2_ = bf16[136,512]{1,0:T(8,128)(2,1)S(1)} collective-permute-done((bf16[136,512]{1,0:T(8,128)(2,1)S(1)}, bf16[136,512]{1,0:T(8,128)(2,1)S(1)}, u32[]{:S(2)}, u32[]{:S(2)}) %collective-permute-start.11) | collective-permute-done | bytes 139296 | tf_op jit(solution)/shard_map/ppermute | solution.py:270
  48.0 0.8 %merge.1 = bf16[512,128]{1,0:T(8,128)(2,1)} custom-call(f32[128,512]{1,0:T(8,128)S(1)} %get-tuple-element.150.refs_0_, f32[1,512]{1,0:T(1,128)S(1)} %get-tuple-element.151.refs_1_, bf16[136,512]{1,0:T(8,128)(2,1)S(1)} %collective-permute-done.11.refs_2_), custom_call_target="tpu_custom_call" | custom-call | tf_op jit(solution)/shard_map/merge/pallas_call | solution.py:456
Async XLA Ops:
  0.0 8.8 %collective-permute-start.1 = (bf16[1024,128]{1,0:T(8,128)(2,1)}, bf16[1024,128]{1,0:T(8,128)(2,1)S(1)}, u32[]{:S(2)}, u32[]{:S(2)}) collective-permute-start(bf16[1024,128]{1,0:T(8,128)(2,1)} %refs_3_.1), channel_id=1, source_target_pairs={{0,1},{1,0},{2,3},{3,2},{4,5},{5,4},{6,7},{7,6},{8,9},{9,8},{10,11... | collective-permute-start | bytes 786440 | tf_op jit(solution)/shard_map/ppermute | solution.py:270
  0.5 8.4 %collective-permute-start.2 = (bf16[1024,128]{1,0:T(8,128)(2,1)}, bf16[1024,128]{1,0:T(8,128)(2,1)S(1)}, u32[]{:S(2)}, u32[]{:S(2)}) collective-permute-start(bf16[1024,128]{1,0:T(8,128)(2,1)} %refs_4_.1), channel_id=1, source_target_pairs={{0,1},{1,0},{2,3},{3,2},{4,5},{5,4},{6,7},{7,6},{8,9},{9,8},{10,11... | collective-permute-start | bytes 786440 | tf_op jit(solution)/shard_map/ppermute | solution.py:270
  0.5 9.9 %collective-permute-start.3 = (bf16[1024,128]{1,0:T(8,128)(2,1)}, bf16[1024,128]{1,0:T(8,128)(2,1)S(1)}, u32[]{:S(2)}, u32[]{:S(2)}) collective-permute-start(bf16[1024,128]{1,0:T(8,128)(2,1)} %refs_3_.1), channel_id=1, source_target_pairs={{0,2},{1,3},{2,0},{3,1},{4,6},{5,7},{6,4},{7,5},{8,10},{9,11},{10,... | collective-permute-start | bytes 786440 | tf_op jit(solution)/shard_map/ppermute | solution.py:270
  3.5 5.3 %collective-permute-start = (bf16[512,128]{1,0:T(8,128)(2,1)}, bf16[512,128]{1,0:T(8,128)(2,1)S(1)}, u32[]{:S(2)}, u32[]{:S(2)}) collective-permute-start(bf16[512,128]{1,0:T(8,128)(2,1)} %bitcast.5), channel_id=1, source_target_pairs={{0,4},{1,5},{2,6},{3,7},{4,0},{5,1},{6,2},{7,3},{8,12},{9,13},{10,... | collective-permute-start | bytes 393224 | tf_op jit(solution)/shard_map/ppermute | solution.py:270
  5.7 0.7 %copy-start.1 = (s32[512]{0:T(512)S(1)}, s32[512]{0:T(512)}, u32[]{:S(2)}) copy-start(s32[512]{0:T(512)} %param.9) | copy-start | bytes 6148
  8.8 1.6 %copy-start.2 = (bf16[1024,128]{1,0:T(8,128)(2,1)S(1)}, bf16[1024,128]{1,0:T(8,128)(2,1)}, u32[]{:S(2)}) copy-start(bf16[1024,128]{1,0:T(8,128)(2,1)} %refs_4_.1) | copy-start | bytes 786436
  8.9 3.1 %copy-start = (bf16[32,16,128]{2,1,0:T(8,128)(2,1)S(1)}, bf16[32,16,128]{2,1,0:T(8,128)(2,1)}, u32[]{:S(2)}) copy-start(bf16[32,16,128]{2,1,0:T(8,128)(2,1)} %param.5) | copy-start | bytes 393220
  10.4 12.4 %collective-permute-start.5 = (bf16[1024,128]{1,0:T(8,128)(2,1)S(1)}, bf16[1024,128]{1,0:T(8,128)(2,1)S(1)}, u32[]{:S(2)}, u32[]{:S(2)}) collective-permute-start(bf16[1024,128]{1,0:T(8,128)(2,1)S(1)} %collective-permute-done.3.refs_0_.refs_2_.refs_6_.refs_4_), channel_id=1, source_target_pairs={{0,1},{1,0},{2,3},{3,2},{4,5},{5,4},{6,7},{7,6},{8,9},{9,8},{10,11... | collective-permute-start | bytes 786440 | tf_op jit(solution)/shard_map/ppermute | solution.py:270
  10.5 13.7 %collective-permute-start.6 = (bf16[1024,128]{1,0:T(8,128)(2,1)S(1)}, bf16[1024,128]{1,0:T(8,128)(2,1)S(1)}, u32[]{:S(2)}, u32[]{:S(2)}) collective-permute-start(bf16[1024,128]{1,0:T(8,128)(2,1)S(1)} %copy-done.2), channel_id=1, source_target_pairs={{0,2},{1,3},{2,0},{3,1},{4,6},{5,7},{6,4},{7,5},{8,10},{9,11},{10,... | collective-permute-start | bytes 786440 | tf_op jit(solution)/shard_map/ppermute | solution.py:270
  11.9 9.3 %collective-permute-start.4 = (bf16[512,128]{1,0:T(8,128)(2,1)S(1)}, bf16[512,128]{1,0:T(8,128)(2,1)S(1)}, u32[]{:S(2)}, u32[]{:S(2)}) collective-permute-start(bf16[512,128]{1,0:T(8,128)(2,1)S(1)} %bitcast.7), channel_id=1, source_target_pairs={{0,8},{1,9},{2,10},{3,11},{4,12},{5,13},{6,14},{7,15},{8,0},{9,1},... | collective-permute-start | bytes 393224 | tf_op jit(solution)/shard_map/ppermute | solution.py:270
  24.1 1.6 %collective-permute-start.7 = (bf16[1024,128]{1,0:T(8,128)(2,1)S(1)}, bf16[1024,128]{1,0:T(8,128)(2,1)S(1)}, u32[]{:S(2)}, u32[]{:S(2)}) collective-permute-start(bf16[1024,128]{1,0:T(8,128)(2,1)S(1)} %collective-permute-done.6.refs_0_.refs_3_.refs_7_.refs_5_), channel_id=1, source_target_pairs={{0,1},{1,0},{2,3},{3,2},{4,5},{5,4},{6,7},{7,6},{8,9},{9,8},{10,11... | collective-permute-start | bytes 786440 | tf_op jit(solution)/shard_map/ppermute | solution.py:270
  26.2 12.3 %collective-permute-start.9 = (bf16[136,512]{1,0:T(8,128)(2,1)S(1)}, bf16[136,512]{1,0:T(8,128)(2,1)S(1)}, u32[]{:S(2)}, u32[]{:S(2)}) collective-permute-start(bf16[136,512]{1,0:T(8,128)(2,1)S(1)} %shard_map.60), channel_id=1, source_target_pairs={{0,4},{1,5},{2,6},{3,7},{4,0},{5,1},{6,2},{7,3},{8,12},{9,13},{10,... | collective-permute-start | bytes 417800 | tf_op jit(solution)/shard_map/ppermute | solution.py:270
  27.0 8.0 %collective-permute-start.8 = (bf16[512,128]{1,0:T(8,128)(2,1)S(1)}, bf16[512,128]{1,0:T(8,128)(2,1)S(1)}, u32[]{:S(2)}, u32[]{:S(2)}) collective-permute-start(bf16[512,128]{1,0:T(8,128)(2,1)S(1)} %collective-permute-done.4.refs_1_.q_ref), channel_id=1, source_target_pairs={{0,4},{1,5},{2,6},{3,7},{4,0},{5,1},{6,2},{7,3},{8,12},{9,13},{10,... | collective-permute-start | bytes 393224 | tf_op jit(solution)/shard_map/ppermute | solution.py:270
  37.8 6.3 %collective-permute-start.10 = (bf16[136,512]{1,0:T(8,128)(2,1)S(1)}, bf16[136,512]{1,0:T(8,128)(2,1)S(1)}, u32[]{:S(2)}, u32[]{:S(2)}) collective-permute-start(bf16[136,512]{1,0:T(8,128)(2,1)S(1)} %shard_map.61), channel_id=1, source_target_pairs={{0,4},{1,5},{2,6},{3,7},{4,0},{5,1},{6,2},{7,3},{8,12},{9,13},{10,... | collective-permute-start | bytes 417800 | tf_op jit(solution)/shard_map/ppermute | solution.py:270
  38.8 9.2 %collective-permute-start.11 = (bf16[136,512]{1,0:T(8,128)(2,1)S(1)}, bf16[136,512]{1,0:T(8,128)(2,1)S(1)}, u32[]{:S(2)}, u32[]{:S(2)}) collective-permute-start(bf16[136,512]{1,0:T(8,128)(2,1)S(1)} %shard_map.63), channel_id=1, source_target_pairs={{0,12},{1,13},{2,14},{3,15},{4,8},{5,9},{6,10},{7,11},{8,4},{9,5},... | collective-permute-start | bytes 417800 | tf_op jit(solution)/shard_map/ppermute | solution.py:270

commit v7 on v6

--- a/solution.py
+++ b/solution.py
@@ -25,9 +25,11 @@
 
 
 def transpose_values(values, values_ref):
-    for b, value in enumerate(values):
-        shard_keys, width = value.shape
-        values_ref[b, :width, :] = value[...].T
+    shard_keys = values_ref.shape[2]
+    for b, pieces in enumerate(values):
+        for at, piece in enumerate(pieces):
+            count, width = piece.shape
+            values_ref[b, :width, at * count : (at + 1) * count] = piece[...].T
         values_ref[b, width:, :] = jnp.ones((extra_rows, shard_keys), jnp.bfloat16)
 
 
@@ -113,23 +115,20 @@
     sweep_tiles(q_ref.shape[0], tile, query_pair, keys, limits, scores_ref, put_weights, finish)
 
 
-def finish_kernel(count, plan, *refs):
-    values, weights, tops = refs[:count], refs[count : 2 * count], refs[2 * count : 3 * count]
-    state_refs, outs, values_ref = refs[3 * count : 3 * count + 3], refs[3 * count + 3 : -1], refs[-1]
-    transpose_values(values, values_ref)
+def finish_kernel(pieces, plan, weights_ref, peaks_ref, top_ref, den_ref, num_ref, *refs):
+    state_refs = (top_ref, den_ref, num_ref)
+    values, outs, values_ref = refs[:pieces], refs[pieces:-1], refs[-1]
+    transpose_values([values], values_ref)
     if plan is None:
         state = tuple(ref[...] for ref in state_refs)
-        for b in range(count):
-            state = add_block(state, values_ref[b], weights[b][...], tops[b][...])
+        state = add_block(state, values_ref[0], weights_ref[...], peaks_ref[...])
         for ref, value in zip(outs, state):
             ref[...] = value
         return
     for at, form, out, offset, lanes in plan:
         span = slice(at * lanes, (at + 1) * lanes)
         state = tuple(ref[:, span] for ref in state_refs)
-        for b in range(count):
-            state = add_block(state, values_ref[b], weights[b][:, span], tops[b][:, span])
-        top, den, num = state
+        top, den, num = add_block(state, values_ref[0], weights_ref[:, span], peaks_ref[:, span])
         write_partial(outs[out:], form, slice(offset, offset + lanes), num * (1.0 / den), top + jnp.log2(den))
 
 
@@ -175,7 +174,7 @@
         limits_ref[k : k + 1, :] = wide[2 * k : 2 * k + 1] * 256 + wide[2 * k + 1 : 2 * k + 2] + span_ref[...]
 
 
-def attend_kernel(scale, index, blocks, has_state, plan, setup, *refs):
+def attend_kernel(scale, index, blocks, pieces, has_state, plan, setup, *refs):
     me = lax.axis_index("ctx")
     refs = list(refs)
     if setup:
@@ -194,9 +193,11 @@
     else:
         scratch = [refs.pop() for _ in range(3)][::-1]
         limits_ref, q_ref = refs[:2]
-    keys = refs[2 : 2 + 2 * len(blocks) : 2]
-    values = refs[3 : 3 + 2 * len(blocks) : 2]
-    rest = list(refs[2 + 2 * len(blocks) :])
+    rest = list(refs[2:])
+    keys, values = [], []
+    for count in pieces:
+        keys.append(rest.pop(0))
+        values.append([rest.pop(0) for _ in range(count)])
     rows, _ = q_ref.shape
     tile = scratch[0].shape[2]
     spans = [slice(at, at + tile) for at in range(0, rows, tile)]
@@ -274,7 +275,9 @@
     stages = [list(range(s, s + per_stage)) for s in range(0, outer, per_stage)]
     last = len(stages) - 1
 
-    far_pair = [swap(cache_keys, 2), swap(cache_values, 2)]
+    half = shard_keys // 2
+    far_keys = swap(cache_keys, 2)
+    far_values = [swap(cache_values[at * half : (at + 1) * half], 2) for at in range(2)]
     near_pair = [swap(cache_keys, 1), swap(cache_values, 1)]
     got = [query] + [None] * (outer - 1)
 
@@ -333,7 +336,14 @@
             specs, extra = [], []
         results = pl.pallas_call(
             functools.partial(
-                attend_kernel, scale, index, blocks, states[index] is not None, plan, setup
+                attend_kernel,
+                scale,
+                index,
+                blocks,
+                [len(pairs[b]) - 1 for b in blocks],
+                states[index] is not None,
+                plan,
+                setup,
             ),
             in_specs=specs + [vmem] * (len(operands) - len(specs)),
             out_specs=[vmem] * len(shapes),
@@ -368,13 +378,20 @@
     attend(0, [0])
     for index in range(1, last - 1):
         attend(index, [0, 1])
-    far_pair[0], = hold(far_pair[0])
-    across_keys = swap(far_pair[0], 1)
+    (far_keys,) = hold(far_keys)
+    across_keys = swap(far_keys, 1)
     attend(last - 1, [0, 1])
     source = stages[last][0] ^ (stages[last][0] & -stages[last][0])
     (got[source],) = hold(got[source])
     gather(last)
     ready(last)
+    across_values = [None, None]
+
+    def pass_values(at):
+        (far_values[at],) = hold(far_values[at])
+        across_values[at] = swap(far_values[at], 1)
+
+    pass_values(0)
     ahead = stage_query[last - 1]
     block = jax.ShapeDtypeStruct((shard_keys, stage_rows), jnp.bfloat16)
     weighed = pl.pallas_call(
@@ -385,28 +402,24 @@
         scratch_shapes=[pltpu.VMEM((2, shard_keys, tile), jnp.float32)],
         compiler_params=params,
         name="weigh",
-    )(chain[0], ahead, far_pair[0], across_keys)
+    )(chain[0], ahead, far_keys, across_keys)
     weighed = hold(*weighed)
-    far_pair[1], = hold(far_pair[1])
-    across_values = swap(far_pair[1], 1)
-    pairs += [far_pair, [across_keys, across_values]]
-
-    def finish(values, weights, top, plan, shapes):
+    pass_values(1)
+
+    def finish(values, weights, peaks, plan, shapes):
         results = pl.pallas_call(
-            functools.partial(finish_kernel, 1, plan),
-            in_specs=[vmem] * 6,
+            functools.partial(finish_kernel, len(values), plan),
+            in_specs=[vmem] * (5 + len(values)),
             out_specs=[vmem] * len(shapes),
             out_shape=shapes,
             scratch_shapes=[pltpu.VMEM((1, head_width + extra_rows, shard_keys), jnp.bfloat16)],
             compiler_params=params,
-        )(values, weights, top, *states[last - 1])
+        )(weights, peaks, *states[last - 1], *values)
         return hold(*results)
 
-    states[last - 1] = finish(far_pair[1], weighed[0], weighed[2], None, state_shapes)
-    if outer == 4:
-        attend(1, [2])
-    (across_values,) = hold(across_values)
-    pairs[3] = [across_keys, across_values]
+    states[last - 1] = finish(far_values, weighed[0], weighed[2], None, state_shapes)
+    across_values = hold(*across_values)
+    pairs += [[far_keys, *far_values], [across_keys, *across_values]]
     (packed,) = finish(across_values, weighed[1], weighed[3], whole_plan, [packed_shape(stage_rows)])
     own_plan = [(at, "float", 0, at * tile, tile) for at in tiles]
     parts = []
@@ -430,7 +443,7 @@
 
     if outer == 4:
         handed = swap(packed, inner)
-        (packed,) = attend(1, [3], whole_plan, coded)
+        (packed,) = attend(1, [2, 3], whole_plan, coded)
         parts.append(swap(packed, inner))
         value, level = attend(3, [0, 1, 2, 3], own_plan, float_shapes(stage_rows))
         (handed,) = hold(handed)

time: 49 us -> 45.1 us (0.920)
  waiting for transfers between devices: 16.6 us -> 13.1 us
    ppermute x12 -> x14, waiting for transfers between devices: 16.6 us -> 13.1 us  [swap(): return lax.ppermute(array, 'ctx', [(i, i ^ step) for i in range(size)])]
    pallas_call x9 -> x8, Pallas kernels: 12.9 us -> 12.5 us  [the longest x6 11.7 us: attend(): pl.pallas_call(functools.partial(attend_kernel, scale, index, blocks, [le...]
    ppermute x12 -> x14, starting transfers between devices: 15.3 us -> 15.2 us  [swap(): return lax.ppermute(array, 'ctx', [(i, i ^ step) for i in range(size)])]
  transfers between devices with their start and end apart: 12 -> 14, of which waited for: 5 -> 5; matrix products, arithmetic and copies ran while one was open for 0% -> 0% of each run, Pallas kernels for 29% -> 31%
where the time goes in v7:
time: 45.1 us; the launch traced here: 44.9 us
  starting transfers between devices  15.2 us (34%)
  Pallas kernels  15 us (33%)
  waiting for transfers between devices  13.1 us (29%)
  between operations  0.84 us (2%)
  local copies, waits for them, and re-layouts  0.71 us (2%)
    ppermute x14, starting transfers between devices, swap(): return lax.ppermute(array, 'ctx', [(i, i ^ step) for i in range(size)])  15.2 us
    ppermute x14, waiting for transfers between devices, swap(): return lax.ppermute(array, 'ctx', [(i, i ^ step) for i in range(size)])  13.1 us
    pallas_call x6, Pallas kernels, attend(): pl.pallas_call(functools.partial(attend_kernel, scale, index, blocks, [le...  11.7 us
    pallas_call x1, Pallas kernels, local(): pl.pallas_call(functools.partial(weigh_kernel, scale, last - 1, [2, 3]),...  1.34 us
  transfers between devices with their start and end apart: 14, of which 5 were waited for; matrix products, arithmetic and copies ran while one was open for 0% of the time, Pallas kernels for 31%

profile of v7, /device:TPU:0, one launch (start us, length us, event | category | flops | bytes accessed | tf_op | source)
XLA Modules:
  0.0 44.9 jit_solution(8439116064985694308)
XLA Ops:
  0.0 0.5 %collective-permute-start.1 = (bf16[1024,128]{1,0:T(8,128)(2,1)}, bf16[1024,128]{1,0:T(8,128)(2,1)S(1)}, u32[]{:S(2)}, u32[]{:S(2)}) collective-permute-start(bf16[1024,128]{1,0:T(8,128)(2,1)} %refs_3_.1), channel_id=1, source_target_pairs={{0,1},{1,0},{2,3},{3,2},{4,5},{5,4},{6,7},{7,6},{8,9},{9,8},{10,11... | collective-permute-start | bytes 786440 | tf_op jit(solution)/shard_map/ppermute | solution.py:271
  0.5 0.0 collective-permute-start.2
  0.5 3.0 %collective-permute-start.3 = (bf16[1024,128]{1,0:T(8,128)(2,1)}, bf16[1024,128]{1,0:T(8,128)(2,1)S(1)}, u32[]{:S(2)}, u32[]{:S(2)}) collective-permute-start(bf16[1024,128]{1,0:T(8,128)(2,1)} %refs_3_.1), channel_id=1, source_target_pairs={{0,2},{1,3},{2,0},{3,1},{4,6},{5,7},{6,4},{7,5},{8,10},{9,11},{10,... | collective-permute-start | bytes 786440 | tf_op jit(solution)/shard_map/ppermute | solution.py:271
  3.5 1.6 %collective-permute-start = (bf16[512,128]{1,0:T(8,128)(2,1)}, bf16[512,128]{1,0:T(8,128)(2,1)S(1)}, u32[]{:S(2)}, u32[]{:S(2)}) collective-permute-start(bf16[512,128]{1,0:T(8,128)(2,1)} %bitcast.5), channel_id=1, source_target_pairs={{0,4},{1,5},{2,6},{3,7},{4,0},{5,1},{6,2},{7,3},{8,12},{9,13},{10,... | collective-permute-start | bytes 393224 | tf_op jit(solution)/shard_map/ppermute | solution.py:271
  5.1 2.6 %collective-permute-start.4 = (bf16[512,128]{1,0:T(8,128)(2,1)}, bf16[512,128]{1,0:T(8,128)(2,1)S(1)}, u32[]{:S(2)}, u32[]{:S(2)}) collective-permute-start(bf16[512,128]{1,0:T(8,128)(2,1)} %bitcast.6), channel_id=1, source_target_pairs={{0,8},{1,9},{2,10},{3,11},{4,12},{5,13},{6,14},{7,15},{8,0},{9,1},... | collective-permute-start | bytes 393224 | tf_op jit(solution)/shard_map/ppermute | solution.py:271
  8.3 0.0 copy-start.1
  8.3 0.7 %copy-done.1 = s32[512]{0:T(512)S(1)} copy-done((s32[512]{0:T(512)S(1)}, s32[512]{0:T(512)}, u32[]{:S(2)}) %copy-start.1) | copy-done | bytes 2072
  9.0 2.1 %shard_map.55 = (f32[1,512]{1,0:T(1,128)S(1)}, f32[1,512]{1,0:T(1,128)S(1)}, f32[128,512]{1,0:T(8,128)S(1)}, s32[4,512]{1,0:T(4,128)S(1)}, bf16[1024,128]{1,0:T(8,128)(2,1)S(1)}, /*index=5*/bf16[1024,128]{1,0:T(8,128)(2,1)S(1)}) custom-call(s32[4,128]{1,0:T(4,128)S(1)} %bitcast.9, s32[1,1]{1,0:T(1,128)} %bitcast.4.refs_1_, bf16[512,128]{1,0:T(8,128)(2,1)} %bitcast.7, ...), custom_call_target="tpu_custom_call" | custom-call | tf_op jit(solution)/shard_map/pallas_call | solution.py:337
  11.1 0.0 collective-permute-done.refs_1_
  11.1 0.0 collective-permute-done.1.refs_4_.refs_2_
  11.1 0.0 collective-permute-done.2.refs_5_.refs_3_
  11.2 0.0 copy-start.2
  11.2 1.5 %shard_map.56 = (f32[1,512]{1,0:T(1,128)S(1)}, f32[1,512]{1,0:T(1,128)S(1)}, f32[128,512]{1,0:T(8,128)S(1)}) custom-call(s32[4,512]{1,0:T(4,128)S(1)} %get-tuple-element.133.refs_0_.limits_ref, bf16[512,128]{1,0:T(8,128)(2,1)S(1)} %collective-permute-done.refs_1_, bf16[1024,128]{1,0:T(8,128)(2,1)S(1)} %get-tuple-element.80.refs_2_, ...), custom_call_target="tpu_custom_call" | custom-call | tf_op jit(solution)/shard_map/pallas_call | solution.py:337
  12.7 0.0 collective-permute-done.3.refs_0_.refs_2_.refs_6_.refs_4_
  12.7 0.1 collective-permute-start.6
  12.8 0.0 copy-done.2
  12.8 0.6 %collective-permute-start.5 = (bf16[512,128]{1,0:T(8,128)(2,1)S(1)}, bf16[512,128]{1,0:T(8,128)(2,1)S(1)}, u32[]{:S(2)}, u32[]{:S(2)}) collective-permute-start(bf16[512,128]{1,0:T(8,128)(2,1)S(1)} %get-tuple-element.146), channel_id=1, source_target_pairs={{0,2},{1,3},{2,0},{3,1},{4,6},{5,7},{6,4},{7,5},{8,10},{9,11},{10,... | collective-permute-start | bytes 393224 | tf_op jit(solution)/shard_map/ppermute | solution.py:271
  13.4 1.5 %collective-permute-start.7 = (bf16[512,128]{1,0:T(8,128)(2,1)S(1)}, bf16[512,128]{1,0:T(8,128)(2,1)S(1)}, u32[]{:S(2)}, u32[]{:S(2)}) collective-permute-start(bf16[512,128]{1,0:T(8,128)(2,1)S(1)} %get-tuple-element.145), channel_id=1, source_target_pairs={{0,2},{1,3},{2,0},{3,1},{4,6},{5,7},{6,4},{7,5},{8,10},{9,11},{10,... | collective-permute-start | bytes 393224 | tf_op jit(solution)/shard_map/ppermute | solution.py:271
  14.9 0.0 collective-permute-done.4.refs_1_.q_ref
  14.9 1.5 %shard_map.57 = (f32[1,512]{1,0:T(1,128)S(1)}, f32[1,512]{1,0:T(1,128)S(1)}, f32[128,512]{1,0:T(8,128)S(1)}) custom-call(s32[4,512]{1,0:T(4,128)S(1)} %get-tuple-element.133.refs_0_.limits_ref, bf16[512,128]{1,0:T(8,128)(2,1)S(1)} %collective-permute-done.4.refs_1_.q_ref, bf16[1024,128]{1,0:T(8,128)(2,1)S(1)} %get-tuple-element.80.refs_2_, ...), custom_call_target="tpu_custom_call" | custom-call | tf_op jit(solution)/shard_map/pallas_call | solution.py:337
  16.4 2.8 %collective-permute-done.5.refs_0_.refs_3_.refs_7_.refs_5_ = bf16[512,128]{1,0:T(8,128)(2,1)S(1)} collective-permute-done((bf16[512,128]{1,0:T(8,128)(2,1)S(1)}, bf16[512,128]{1,0:T(8,128)(2,1)S(1)}, u32[]{:S(2)}, u32[]{:S(2)}) %collective-permute-start.5) | collective-permute-done | bytes 131104 | tf_op jit(solution)/shard_map/ppermute | solution.py:271
  19.2 0.0 collective-permute-start.8
  19.2 0.0 collective-permute-done.6.refs_1_.refs_5_.refs_9_.refs_7_
  19.2 1.3 %weigh.1 = (bf16[1024,512]{1,0:T(8,128)(2,1)S(1)}, bf16[1024,512]{1,0:T(8,128)(2,1)S(1)}, f32[1,512]{1,0:T(1,128)S(1)}, f32[1,512]{1,0:T(1,128)S(1)}) custom-call(s32[4,512]{1,0:T(4,128)S(1)} %get-tuple-element.133.refs_0_.limits_ref, bf16[512,128]{1,0:T(8,128)(2,1)S(1)} %collective-permute-done.4.refs_1_.q_ref, ...), custom_call_target="tpu_custom_call" | custom-call | tf_op jit(solution)/shard_map/weigh/pallas_call | solution.py:397
  20.6 1.0 %collective-permute-done.7.refs_1_.refs_4_.refs_8_.refs_6_ = bf16[512,128]{1,0:T(8,128)(2,1)S(1)} collective-permute-done((bf16[512,128]{1,0:T(8,128)(2,1)S(1)}, bf16[512,128]{1,0:T(8,128)(2,1)S(1)}, u32[]{:S(2)}, u32[]{:S(2)}) %collective-permute-start.7) | collective-permute-done | bytes 131104 | tf_op jit(solution)/shard_map/ppermute | solution.py:271
  21.6 0.0 collective-permute-start.9
  21.6 0.3 shard_map.58
  21.9 0.0 collective-permute-done.8.refs_0_.refs_6_.refs_10_.refs_8_
  21.9 1.0 %collective-permute-done.9.refs_1_.refs_7_.refs_11_.refs_9_ = bf16[512,128]{1,0:T(8,128)(2,1)S(1)} collective-permute-done((bf16[512,128]{1,0:T(8,128)(2,1)S(1)}, bf16[512,128]{1,0:T(8,128)(2,1)S(1)}, u32[]{:S(2)}, u32[]{:S(2)}) %collective-permute-start.9) | collective-permute-done | bytes 131104 | tf_op jit(solution)/shard_map/ppermute | solution.py:271
  22.9 0.5 %shard_map.59 = bf16[136,512]{1,0:T(8,128)(2,1)S(1)} custom-call(bf16[1024,512]{1,0:T(8,128)(2,1)S(1)} %get-tuple-element.112.weights_ref, f32[1,512]{1,0:T(1,128)S(1)} %get-tuple-element.113.peaks_ref, f32[1,512]{1,0:T(1,128)S(1)} %get-tuple-element.114.top_ref, f32[1,512]{1,0:T(1,128)S(1)} %get-tuple-element.115.den_ref, ...), custom_call_target="tpu_custom_call" | custom-call | tf_op jit(solution)/shard_map/pallas_call | solution.py:410
  23.4 0.5 %collective-permute-start.11 = (bf16[136,512]{1,0:T(8,128)(2,1)S(1)}, bf16[136,512]{1,0:T(8,128)(2,1)S(1)}, u32[]{:S(2)}, u32[]{:S(2)}) collective-permute-start(bf16[136,512]{1,0:T(8,128)(2,1)S(1)} %shard_map.59), channel_id=1, source_target_pairs={{0,4},{1,5},{2,6},{3,7},{4,0},{5,1},{6,2},{7,3},{8,12},{9,13},{10,... | collective-permute-start | bytes 417800 | tf_op jit(solution)/shard_map/ppermute | solution.py:271
  23.9 1.6 %collective-permute-start.10 = (bf16[512,128]{1,0:T(8,128)(2,1)S(1)}, bf16[512,128]{1,0:T(8,128)(2,1)S(1)}, u32[]{:S(2)}, u32[]{:S(2)}) collective-permute-start(bf16[512,128]{1,0:T(8,128)(2,1)S(1)} %collective-permute-done.4.refs_1_.q_ref), channel_id=1, source_target_pairs={{0,4},{1,5},{2,6},{3,7},{4,0},{5,1},{6,2},{7,3},{8,12},{9,13},{10,... | collective-permute-start | bytes 393224 | tf_op jit(solution)/shard_map/ppermute | solution.py:271
  25.5 1.6 %shard_map.60 = bf16[136,512]{1,0:T(8,128)(2,1)S(1)} custom-call(s32[4,512]{1,0:T(4,128)S(1)} %get-tuple-element.133.refs_0_.limits_ref, bf16[512,128]{1,0:T(8,128)(2,1)S(1)} %collective-permute-done.refs_1_, bf16[1024,128]{1,0:T(8,128)(2,1)S(1)} %collective-permute-done.3.refs_0_.refs_2_.refs_6_.refs_4_, ...), custom_call_target="tpu_custom_call" | custom-call | tf_op jit(solution)/shard_map/pallas_call | solution.py:337
  27.1 4.9 %collective-permute-done.10.refs_1_ = bf16[512,128]{1,0:T(8,128)(2,1)S(1)} collective-permute-done((bf16[512,128]{1,0:T(8,128)(2,1)S(1)}, bf16[512,128]{1,0:T(8,128)(2,1)S(1)}, u32[]{:S(2)}, u32[]{:S(2)}) %collective-permute-start.10) | collective-permute-done | bytes 131104 | tf_op jit(solution)/shard_map/ppermute | solution.py:271
  32.0 2.8 %shard_map.61 = (f32[128,512]{1,0:T(8,128)S(1)}, f32[1,512]{1,0:T(1,128)S(1)}) custom-call(s32[4,512]{1,0:T(4,128)S(1)} %get-tuple-element.133.refs_0_.limits_ref, bf16[512,128]{1,0:T(8,128)(2,1)S(1)} %collective-permute-done.10.refs_1_, bf16[1024,128]{1,0:T(8,128)(2,1)S(1)} %get-tuple-element.80.refs_2_, bf16[1024,128]{1,0:T(8,128)(2,1)S(1)} %get-tuple-element.81.refs_3_, ...), custom_call_target="tpu_custom_call" | custom-call | tf_op jit(solution)/shard_map/pallas_call | solution.py:337
  34.8 0.0 copy-start
  34.8 0.5 %collective-permute-start.12 = (bf16[136,512]{1,0:T(8,128)(2,1)S(1)}, bf16[136,512]{1,0:T(8,128)(2,1)S(1)}, u32[]{:S(2)}, u32[]{:S(2)}) collective-permute-start(bf16[136,512]{1,0:T(8,128)(2,1)S(1)} %shard_map.60), channel_id=1, source_target_pairs={{0,4},{1,5},{2,6},{3,7},{4,0},{5,1},{6,2},{7,3},{8,12},{9,13},{10,... | collective-permute-start | bytes 417800 | tf_op jit(solution)/shard_map/ppermute | solution.py:271
  35.4 0.0 collective-permute-done.11.part_ref
  35.4 0.3 shard_map.62
  35.6 2.8 %collective-permute-start.13 = (bf16[136,512]{1,0:T(8,128)(2,1)S(1)}, bf16[136,512]{1,0:T(8,128)(2,1)S(1)}, u32[]{:S(2)}, u32[]{:S(2)}) collective-permute-start(bf16[136,512]{1,0:T(8,128)(2,1)S(1)} %shard_map.62), channel_id=1, source_target_pairs={{0,12},{1,13},{2,14},{3,15},{4,8},{5,9},{6,10},{7,11},{8,4},{9,5},... | collective-permute-start | bytes 417800 | tf_op jit(solution)/shard_map/ppermute | solution.py:271
  38.4 0.0 copy-done
  38.4 2.2 %shard_map.63 = (f32[128,512]{1,0:T(8,128)S(1)}, f32[1,512]{1,0:T(1,128)S(1)}) custom-call(s32[4,512]{1,0:T(4,128)S(1)} %get-tuple-element.133.refs_0_.limits_ref, bf16[512,128]{1,0:T(8,128)(2,1)S(1)} %bitcast.8, bf16[1024,128]{1,0:T(8,128)(2,1)S(1)} %collective-permute-done.1.refs_4_.refs_2_, bf16[1024,128]{1,0:T(8,128)(2,1)S(1)} %collective-permute-done.2.refs_5_.refs_3_, ...), custom_call_target="tpu_custom_call" | custom-call | tf_op jit(solution)/shard_map/pallas_call | solution.py:337
  40.6 0.0 collective-permute-done.12.part_ref
  40.6 0.1 shard_map.64
  40.7 3.4 %collective-permute-done.13.refs_2_ = bf16[136,512]{1,0:T(8,128)(2,1)S(1)} collective-permute-done((bf16[136,512]{1,0:T(8,128)(2,1)S(1)}, bf16[136,512]{1,0:T(8,128)(2,1)S(1)}, u32[]{:S(2)}, u32[]{:S(2)}) %collective-permute-start.13) | collective-permute-done | bytes 139296 | tf_op jit(solution)/shard_map/ppermute | solution.py:271
  44.1 0.8 %merge.1 = bf16[512,128]{1,0:T(8,128)(2,1)} custom-call(f32[128,512]{1,0:T(8,128)S(1)} %get-tuple-element.142.refs_0_, f32[1,512]{1,0:T(1,128)S(1)} %get-tuple-element.143.refs_1_, bf16[136,512]{1,0:T(8,128)(2,1)S(1)} %collective-permute-done.13.refs_2_), custom_call_target="tpu_custom_call" | custom-call | tf_op jit(solution)/shard_map/merge/pallas_call | solution.py:469
  (1 shorter events, 0.0 us)
Async XLA Ops:
  0.0 11.1 %collective-permute-start.1 = (bf16[1024,128]{1,0:T(8,128)(2,1)}, bf16[1024,128]{1,0:T(8,128)(2,1)S(1)}, u32[]{:S(2)}, u32[]{:S(2)}) collective-permute-start(bf16[1024,128]{1,0:T(8,128)(2,1)} %refs_3_.1), channel_id=1, source_target_pairs={{0,1},{1,0},{2,3},{3,2},{4,5},{5,4},{6,7},{7,6},{8,9},{9,8},{10,11... | collective-permute-start | bytes 786440 | tf_op jit(solution)/shard_map/ppermute | solution.py:271
  0.5 10.7 %collective-permute-start.2 = (bf16[1024,128]{1,0:T(8,128)(2,1)}, bf16[1024,128]{1,0:T(8,128)(2,1)S(1)}, u32[]{:S(2)}, u32[]{:S(2)}) collective-permute-start(bf16[1024,128]{1,0:T(8,128)(2,1)} %refs_4_.1), channel_id=1, source_target_pairs={{0,1},{1,0},{2,3},{3,2},{4,5},{5,4},{6,7},{7,6},{8,9},{9,8},{10,11... | collective-permute-start | bytes 786440 | tf_op jit(solution)/shard_map/ppermute | solution.py:271
  0.5 12.2 %collective-permute-start.3 = (bf16[1024,128]{1,0:T(8,128)(2,1)}, bf16[1024,128]{1,0:T(8,128)(2,1)S(1)}, u32[]{:S(2)}, u32[]{:S(2)}) collective-permute-start(bf16[1024,128]{1,0:T(8,128)(2,1)} %refs_3_.1), channel_id=1, source_target_pairs={{0,2},{1,3},{2,0},{3,1},{4,6},{5,7},{6,4},{7,5},{8,10},{9,11},{10,... | collective-permute-start | bytes 786440 | tf_op jit(solution)/shard_map/ppermute | solution.py:271
  3.5 7.6 %collective-permute-start = (bf16[512,128]{1,0:T(8,128)(2,1)}, bf16[512,128]{1,0:T(8,128)(2,1)S(1)}, u32[]{:S(2)}, u32[]{:S(2)}) collective-permute-start(bf16[512,128]{1,0:T(8,128)(2,1)} %bitcast.5), channel_id=1, source_target_pairs={{0,4},{1,5},{2,6},{3,7},{4,0},{5,1},{6,2},{7,3},{8,12},{9,13},{10,... | collective-permute-start | bytes 393224 | tf_op jit(solution)/shard_map/ppermute | solution.py:271
  5.1 9.8 %collective-permute-start.4 = (bf16[512,128]{1,0:T(8,128)(2,1)}, bf16[512,128]{1,0:T(8,128)(2,1)S(1)}, u32[]{:S(2)}, u32[]{:S(2)}) collective-permute-start(bf16[512,128]{1,0:T(8,128)(2,1)} %bitcast.6), channel_id=1, source_target_pairs={{0,8},{1,9},{2,10},{3,11},{4,12},{5,13},{6,14},{7,15},{8,0},{9,1},... | collective-permute-start | bytes 393224 | tf_op jit(solution)/shard_map/ppermute | solution.py:271
  8.3 0.7 %copy-start.1 = (s32[512]{0:T(512)S(1)}, s32[512]{0:T(512)}, u32[]{:S(2)}) copy-start(s32[512]{0:T(512)} %param.9) | copy-start | bytes 6148
  11.2 1.6 %copy-start.2 = (bf16[1024,128]{1,0:T(8,128)(2,1)S(1)}, bf16[1024,128]{1,0:T(8,128)(2,1)}, u32[]{:S(2)}) copy-start(bf16[1024,128]{1,0:T(8,128)(2,1)} %refs_4_.1) | copy-start | bytes 786436
  12.7 6.6 %collective-permute-start.6 = (bf16[1024,128]{1,0:T(8,128)(2,1)S(1)}, bf16[1024,128]{1,0:T(8,128)(2,1)S(1)}, u32[]{:S(2)}, u32[]{:S(2)}) collective-permute-start(bf16[1024,128]{1,0:T(8,128)(2,1)S(1)} %collective-permute-done.3.refs_0_.refs_2_.refs_6_.refs_4_), channel_id=1, source_target_pairs={{0,1},{1,0},{2,3},{3,2},{4,5},{5,4},{6,7},{7,6},{8,9},{9,8},{10,11... | collective-permute-start | bytes 786440 | tf_op jit(solution)/shard_map/ppermute | solution.py:271
  12.8 6.4 %collective-permute-start.5 = (bf16[512,128]{1,0:T(8,128)(2,1)S(1)}, bf16[512,128]{1,0:T(8,128)(2,1)S(1)}, u32[]{:S(2)}, u32[]{:S(2)}) collective-permute-start(bf16[512,128]{1,0:T(8,128)(2,1)S(1)} %get-tuple-element.146), channel_id=1, source_target_pairs={{0,2},{1,3},{2,0},{3,1},{4,6},{5,7},{6,4},{7,5},{8,10},{9,11},{10,... | collective-permute-start | bytes 393224 | tf_op jit(solution)/shard_map/ppermute | solution.py:271
  13.4 8.2 %collective-permute-start.7 = (bf16[512,128]{1,0:T(8,128)(2,1)S(1)}, bf16[512,128]{1,0:T(8,128)(2,1)S(1)}, u32[]{:S(2)}, u32[]{:S(2)}) collective-permute-start(bf16[512,128]{1,0:T(8,128)(2,1)S(1)} %get-tuple-element.145), channel_id=1, source_target_pairs={{0,2},{1,3},{2,0},{3,1},{4,6},{5,7},{6,4},{7,5},{8,10},{9,11},{10,... | collective-permute-start | bytes 393224 | tf_op jit(solution)/shard_map/ppermute | solution.py:271
  19.2 2.7 %collective-permute-start.8 = (bf16[512,128]{1,0:T(8,128)(2,1)S(1)}, bf16[512,128]{1,0:T(8,128)(2,1)S(1)}, u32[]{:S(2)}, u32[]{:S(2)}) collective-permute-start(bf16[512,128]{1,0:T(8,128)(2,1)S(1)} %collective-permute-done.5.refs_0_.refs_3_.refs_7_.refs_5_), channel_id=1, source_target_pairs={{0,1},{1,0},{2,3},{3,2},{4,5},{5,4},{6,7},{7,6},{8,9},{9,8},{10,11... | collective-permute-start | bytes 393224 | tf_op jit(solution)/shard_map/ppermute | solution.py:271
  21.6 1.3 %collective-permute-start.9 = (bf16[512,128]{1,0:T(8,128)(2,1)S(1)}, bf16[512,128]{1,0:T(8,128)(2,1)S(1)}, u32[]{:S(2)}, u32[]{:S(2)}) collective-permute-start(bf16[512,128]{1,0:T(8,128)(2,1)S(1)} %collective-permute-done.7.refs_1_.refs_4_.refs_8_.refs_6_), channel_id=1, source_target_pairs={{0,1},{1,0},{2,3},{3,2},{4,5},{5,4},{6,7},{7,6},{8,9},{9,8},{10,11... | collective-permute-start | bytes 393224 | tf_op jit(solution)/shard_map/ppermute | solution.py:271
  23.4 12.0 %collective-permute-start.11 = (bf16[136,512]{1,0:T(8,128)(2,1)S(1)}, bf16[136,512]{1,0:T(8,128)(2,1)S(1)}, u32[]{:S(2)}, u32[]{:S(2)}) collective-permute-start(bf16[136,512]{1,0:T(8,128)(2,1)S(1)} %shard_map.59), channel_id=1, source_target_pairs={{0,4},{1,5},{2,6},{3,7},{4,0},{5,1},{6,2},{7,3},{8,12},{9,13},{10,... | collective-permute-start | bytes 417800 | tf_op jit(solution)/shard_map/ppermute | solution.py:271
  23.9 8.1 %collective-permute-start.10 = (bf16[512,128]{1,0:T(8,128)(2,1)S(1)}, bf16[512,128]{1,0:T(8,128)(2,1)S(1)}, u32[]{:S(2)}, u32[]{:S(2)}) collective-permute-start(bf16[512,128]{1,0:T(8,128)(2,1)S(1)} %collective-permute-done.4.refs_1_.q_ref), channel_id=1, source_target_pairs={{0,4},{1,5},{2,6},{3,7},{4,0},{5,1},{6,2},{7,3},{8,12},{9,13},{10,... | collective-permute-start | bytes 393224 | tf_op jit(solution)/shard_map/ppermute | solution.py:271
  34.8 3.6 %copy-start = (bf16[32,16,128]{2,1,0:T(8,128)(2,1)S(1)}, bf16[32,16,128]{2,1,0:T(8,128)(2,1)}, u32[]{:S(2)}) copy-start(bf16[32,16,128]{2,1,0:T(8,128)(2,1)} %param.5) | copy-start | bytes 393220
  34.8 5.7 %collective-permute-start.12 = (bf16[136,512]{1,0:T(8,128)(2,1)S(1)}, bf16[136,512]{1,0:T(8,128)(2,1)S(1)}, u32[]{:S(2)}, u32[]{:S(2)}) collective-permute-start(bf16[136,512]{1,0:T(8,128)(2,1)S(1)} %shard_map.60), channel_id=1, source_target_pairs={{0,4},{1,5},{2,6},{3,7},{4,0},{5,1},{6,2},{7,3},{8,12},{9,13},{10,... | collective-permute-start | bytes 417800 | tf_op jit(solution)/shard_map/ppermute | solution.py:271
  35.6 8.4 %collective-permute-start.13 = (bf16[136,512]{1,0:T(8,128)(2,1)S(1)}, bf16[136,512]{1,0:T(8,128)(2,1)S(1)}, u32[]{:S(2)}, u32[]{:S(2)}) collective-permute-start(bf16[136,512]{1,0:T(8,128)(2,1)S(1)} %shard_map.62), channel_id=1, source_target_pairs={{0,12},{1,13},{2,14},{3,15},{4,8},{5,9},{6,10},{7,11},{8,4},{9,5},... | collective-permute-start | bytes 417800 | tf_op jit(solution)/shard_map/ppermute | solution.py:271

commit v8 on v6

--- a/solution.py
+++ b/solution.py
@@ -281,7 +281,7 @@
     def gather(index):
         for k in stages[index]:
             if k:
-                low = k & -k
+                low = k if outer == 4 else k & -k
                 got[k] = swap(got[k ^ low], inner * low)
 
     stage_rows = rows * per_stage
@@ -362,19 +362,20 @@
     def ready(index):
         stage_query[index] = join([got[k] for k in stages[index]], 0)
 
-    for index in range(len(stages) - 1):
+    for index in range(len(stages) if outer == 4 else last):
         gather(index)
         ready(index)
     attend(0, [0])
     for index in range(1, last - 1):
         attend(index, [0, 1])
+    if outer != 4:
+        source = stages[last][0] ^ (stages[last][0] & -stages[last][0])
+        (got[source],) = hold(got[source])
+        gather(last)
+        ready(last)
     far_pair[0], = hold(far_pair[0])
     across_keys = swap(far_pair[0], 1)
     attend(last - 1, [0, 1])
-    source = stages[last][0] ^ (stages[last][0] & -stages[last][0])
-    (got[source],) = hold(got[source])
-    gather(last)
-    ready(last)
     ahead = stage_query[last - 1]
     block = jax.ShapeDtypeStruct((shard_keys, stage_rows), jnp.bfloat16)
     weighed = pl.pallas_call(

time: 49 us -> 49.7 us (1.014)
  starting transfers between devices: 15.3 us -> 16.2 us
    ppermute x12, starting transfers between devices: 15.3 us -> 16.2 us  [swap(): return lax.ppermute(array, 'ctx', [(i, i ^ step) for i in range(size)])]
  transfers between devices with their start and end apart: 12 -> 12, of which waited for: 5 -> 6; matrix products, arithmetic and copies ran while one was open for 0% -> 0% of each run, Pallas kernels for 29% -> 28%
where the time goes in v8:
time: 49.7 us; the launch traced here: 49.6 us
  waiting for transfers between devices  16.4 us (33%)
  starting transfers between devices  16.2 us (33%)
  Pallas kernels  15.4 us (31%)
  between operations  0.81 us (2%)
  local copies, waits for them, and re-layouts  0.68 us (1%)
    ppermute x12, waiting for transfers between devices, swap(): return lax.ppermute(array, 'ctx', [(i, i ^ step) for i in range(size)])  16.4 us
    ppermute x12, starting transfers between devices, swap(): return lax.ppermute(array, 'ctx', [(i, i ^ step) for i in range(size)])  16.2 us
    pallas_call x7, Pallas kernels, attend(): pl.pallas_call(functools.partial(attend_kernel, scale, index, blocks, sta...  12.1 us
    pallas_call x1, Pallas kernels, local(): pl.pallas_call(functools.partial(weigh_kernel, scale, last - 1, [2, 3]),...  1.32 us
  transfers between devices with their start and end apart: 12, of which 6 were waited for; matrix products, arithmetic and copies ran while one was open for 0% of the time, Pallas kernels for 28%

profile of v8, /device:TPU:0, one launch (start us, length us, event | category | flops | bytes accessed | tf_op | source)
XLA Modules:
  0.0 49.6 jit_solution(10208753008356571406)
XLA Ops:
  0.0 0.5 collective-permute-start.1
  0.5 0.0 collective-permute-start.2
  0.5 3.0 %collective-permute-start.3 = (bf16[1024,128]{1,0:T(8,128)(2,1)}, bf16[1024,128]{1,0:T(8,128)(2,1)S(1)}, u32[]{:S(2)}, u32[]{:S(2)}) collective-permute-start(bf16[1024,128]{1,0:T(8,128)(2,1)} %refs_3_.1), channel_id=1, source_target_pairs={{0,2},{1,3},{2,0},{3,1},{4,6},{5,7},{6,4},{7,5},{8,10},{9,11},{10,... | collective-permute-start | bytes 786440 | tf_op jit(solution)/shard_map/ppermute | solution.py:270
  3.5 1.6 %collective-permute-start = (bf16[512,128]{1,0:T(8,128)(2,1)}, bf16[512,128]{1,0:T(8,128)(2,1)S(1)}, u32[]{:S(2)}, u32[]{:S(2)}) collective-permute-start(bf16[512,128]{1,0:T(8,128)(2,1)} %bitcast.5), channel_id=1, source_target_pairs={{0,4},{1,5},{2,6},{3,7},{4,0},{5,1},{6,2},{7,3},{8,12},{9,13},{10,... | collective-permute-start | bytes 393224 | tf_op jit(solution)/shard_map/ppermute | solution.py:270
  5.7 0.0 copy-start.1
  5.7 0.7 %copy-done.1 = s32[512]{0:T(512)S(1)} copy-done((s32[512]{0:T(512)S(1)}, s32[512]{0:T(512)}, u32[]{:S(2)}) %copy-start.1) | copy-done | bytes 2072
  6.4 2.1 %shard_map.55 = (f32[1,512]{1,0:T(1,128)S(1)}, f32[1,512]{1,0:T(1,128)S(1)}, f32[128,512]{1,0:T(8,128)S(1)}, s32[4,512]{1,0:T(4,128)S(1)}, bf16[1024,128]{1,0:T(8,128)(2,1)S(1)}, /*index=5*/bf16[1024,128]{1,0:T(8,128)(2,1)S(1)}) custom-call(s32[4,128]{1,0:T(4,128)S(1)} %bitcast.10, s32[1,1]{1,0:T(1,128)} %bitcast.4.refs_1_, bf16[512,128]{1,0:T(8,128)(2,1)} %bitcast.6, ...), custom_call_target="tpu_custom_call" | custom-call | tf_op jit(solution)/shard_map/pallas_call | solution.py:334
  8.5 0.3 collective-permute-done.refs_1_
  8.8 0.0 collective-permute-done.1.refs_4_.refs_2_
  8.8 0.0 collective-permute-done.2.refs_5_.refs_3_
  8.8 0.0 copy-start.2
  8.9 0.0 copy-start
  8.9 1.5 %shard_map.56 = (f32[1,512]{1,0:T(1,128)S(1)}, f32[1,512]{1,0:T(1,128)S(1)}, f32[128,512]{1,0:T(8,128)S(1)}) custom-call(s32[4,512]{1,0:T(4,128)S(1)} %get-tuple-element.137.refs_0_.limits_ref, bf16[512,128]{1,0:T(8,128)(2,1)S(1)} %collective-permute-done.refs_1_, bf16[1024,128]{1,0:T(8,128)(2,1)S(1)} %get-tuple-element.82.refs_2_, ...), custom_call_target="tpu_custom_call" | custom-call | tf_op jit(solution)/shard_map/pallas_call | solution.py:334
  10.4 0.0 collective-permute-done.3.refs_0_.refs_2_.refs_6_.refs_4_
  10.4 0.1 collective-permute-start.5
  10.5 0.0 copy-done.2
  10.5 1.5 %collective-permute-start.6 = (bf16[1024,128]{1,0:T(8,128)(2,1)S(1)}, bf16[1024,128]{1,0:T(8,128)(2,1)S(1)}, u32[]{:S(2)}, u32[]{:S(2)}) collective-permute-start(bf16[1024,128]{1,0:T(8,128)(2,1)S(1)} %copy-done.2), channel_id=1, source_target_pairs={{0,2},{1,3},{2,0},{3,1},{4,6},{5,7},{6,4},{7,5},{8,10},{9,11},{10,... | collective-permute-start | bytes 786440 | tf_op jit(solution)/shard_map/ppermute | solution.py:270
  11.9 0.0 copy-done
  11.9 2.6 %collective-permute-start.4 = (bf16[512,128]{1,0:T(8,128)(2,1)S(1)}, bf16[512,128]{1,0:T(8,128)(2,1)S(1)}, u32[]{:S(2)}, u32[]{:S(2)}) collective-permute-start(bf16[512,128]{1,0:T(8,128)(2,1)S(1)} %bitcast.7), channel_id=1, source_target_pairs={{0,8},{1,9},{2,10},{3,11},{4,12},{5,13},{6,14},{7,15},{8,0},{9,1},... | collective-permute-start | bytes 393224 | tf_op jit(solution)/shard_map/ppermute | solution.py:270
  14.5 6.7 %collective-permute-done.4.refs_1_.q_ref = bf16[512,128]{1,0:T(8,128)(2,1)S(1)} collective-permute-done((bf16[512,128]{1,0:T(8,128)(2,1)S(1)}, bf16[512,128]{1,0:T(8,128)(2,1)S(1)}, u32[]{:S(2)}, u32[]{:S(2)}) %collective-permute-start.4) | collective-permute-done | bytes 131104 | tf_op jit(solution)/shard_map/ppermute | solution.py:270
  21.3 1.5 %shard_map.57 = (f32[1,512]{1,0:T(1,128)S(1)}, f32[1,512]{1,0:T(1,128)S(1)}, f32[128,512]{1,0:T(8,128)S(1)}) custom-call(s32[4,512]{1,0:T(4,128)S(1)} %get-tuple-element.137.refs_0_.limits_ref, bf16[512,128]{1,0:T(8,128)(2,1)S(1)} %collective-permute-done.4.refs_1_.q_ref, bf16[1024,128]{1,0:T(8,128)(2,1)S(1)} %get-tuple-element.82.refs_2_, ...), custom_call_target="tpu_custom_call" | custom-call | tf_op jit(solution)/shard_map/pallas_call | solution.py:334
  22.8 0.0 collective-permute-done.5.refs_1_.refs_2_.refs_8_.refs_6_
  22.8 1.3 %weigh.1 = (bf16[1024,512]{1,0:T(8,128)(2,1)S(1)}, bf16[1024,512]{1,0:T(8,128)(2,1)S(1)}, f32[1,512]{1,0:T(1,128)S(1)}, f32[1,512]{1,0:T(1,128)S(1)}) custom-call(s32[4,512]{1,0:T(4,128)S(1)} %get-tuple-element.137.refs_0_.limits_ref, bf16[512,128]{1,0:T(8,128)(2,1)S(1)} %collective-permute-done.4.refs_1_.q_ref, ...), custom_call_target="tpu_custom_call" | custom-call | tf_op jit(solution)/shard_map/weigh/pallas_call | solution.py:381
  24.1 0.0 collective-permute-done.6.refs_0_.refs_3_.refs_7_.refs_5_
  24.1 0.1 collective-permute-start.7
  24.2 0.4 shard_map.58
  24.6 0.9 %shard_map.59 = (f32[1,512]{1,0:T(1,128)S(1)}, f32[1,512]{1,0:T(1,128)S(1)}, f32[128,512]{1,0:T(8,128)S(1)}) custom-call(s32[4,512]{1,0:T(4,128)S(1)} %get-tuple-element.137.refs_0_.limits_ref, bf16[512,128]{1,0:T(8,128)(2,1)S(1)} %collective-permute-done.refs_1_, bf16[1024,128]{1,0:T(8,128)(2,1)S(1)} %collective-permute-done.3.refs_0_.refs_2_.refs_6_.refs_4_, ...), custom_call_target="tpu_custom_call" | custom-call | tf_op jit(solution)/shard_map/pallas_call | solution.py:334
  25.5 0.2 collective-permute-done.7.refs_0_.refs_3_.refs_9_.refs_7_
  25.7 0.5 shard_map.60
  26.2 0.7 %collective-permute-start.9 = (bf16[136,512]{1,0:T(8,128)(2,1)S(1)}, bf16[136,512]{1,0:T(8,128)(2,1)S(1)}, u32[]{:S(2)}, u32[]{:S(2)}) collective-permute-start(bf16[136,512]{1,0:T(8,128)(2,1)S(1)} %shard_map.60), channel_id=1, source_target_pairs={{0,4},{1,5},{2,6},{3,7},{4,0},{5,1},{6,2},{7,3},{8,12},{9,13},{10,... | collective-permute-start | bytes 417800 | tf_op jit(solution)/shard_map/ppermute | solution.py:270
  27.0 2.9 %collective-permute-start.8 = (bf16[512,128]{1,0:T(8,128)(2,1)S(1)}, bf16[512,128]{1,0:T(8,128)(2,1)S(1)}, u32[]{:S(2)}, u32[]{:S(2)}) collective-permute-start(bf16[512,128]{1,0:T(8,128)(2,1)S(1)} %bitcast.8), channel_id=1, source_target_pairs={{0,12},{1,13},{2,14},{3,15},{4,8},{5,9},{6,10},{7,11},{8,4},{9,5},... | collective-permute-start | bytes 393224 | tf_op jit(solution)/shard_map/ppermute | solution.py:270
  29.9 1.0 %shard_map.61 = bf16[136,512]{1,0:T(8,128)(2,1)S(1)} custom-call(s32[4,512]{1,0:T(4,128)S(1)} %get-tuple-element.137.refs_0_.limits_ref, bf16[512,128]{1,0:T(8,128)(2,1)S(1)} %collective-permute-done.refs_1_, bf16[1024,128]{1,0:T(8,128)(2,1)S(1)} %collective-permute-done.5.refs_1_.refs_2_.refs_8_.refs_6_, ...), custom_call_target="tpu_custom_call" | custom-call | tf_op jit(solution)/shard_map/pallas_call | solution.py:334
  30.9 5.9 %collective-permute-done.8.refs_1_ = bf16[512,128]{1,0:T(8,128)(2,1)S(1)} collective-permute-done((bf16[512,128]{1,0:T(8,128)(2,1)S(1)}, bf16[512,128]{1,0:T(8,128)(2,1)S(1)}, u32[]{:S(2)}, u32[]{:S(2)}) %collective-permute-start.8) | collective-permute-done | bytes 131104 | tf_op jit(solution)/shard_map/ppermute | solution.py:270
  36.8 2.8 %shard_map.62 = (f32[128,512]{1,0:T(8,128)S(1)}, f32[1,512]{1,0:T(1,128)S(1)}) custom-call(s32[4,512]{1,0:T(4,128)S(1)} %get-tuple-element.137.refs_0_.limits_ref, bf16[512,128]{1,0:T(8,128)(2,1)S(1)} %collective-permute-done.8.refs_1_, bf16[1024,128]{1,0:T(8,128)(2,1)S(1)} %get-tuple-element.82.refs_2_, bf16[1024,128]{1,0:T(8,128)(2,1)S(1)} %get-tuple-element.83.refs_3_, ...), custom_call_target="tpu_custom_call" | custom-call | tf_op jit(solution)/shard_map/pallas_call | solution.py:334
  39.7 0.6 %collective-permute-start.10 = (bf16[136,512]{1,0:T(8,128)(2,1)S(1)}, bf16[136,512]{1,0:T(8,128)(2,1)S(1)}, u32[]{:S(2)}, u32[]{:S(2)}) collective-permute-start(bf16[136,512]{1,0:T(8,128)(2,1)S(1)} %shard_map.61), channel_id=1, source_target_pairs={{0,4},{1,5},{2,6},{3,7},{4,0},{5,1},{6,2},{7,3},{8,12},{9,13},{10,... | collective-permute-start | bytes 417800 | tf_op jit(solution)/shard_map/ppermute | solution.py:270
  40.3 0.0 collective-permute-done.9.part_ref
  40.3 0.3 shard_map.63
  40.5 2.7 %collective-permute-start.11 = (bf16[136,512]{1,0:T(8,128)(2,1)S(1)}, bf16[136,512]{1,0:T(8,128)(2,1)S(1)}, u32[]{:S(2)}, u32[]{:S(2)}) collective-permute-start(bf16[136,512]{1,0:T(8,128)(2,1)S(1)} %shard_map.63), channel_id=1, source_target_pairs={{0,12},{1,13},{2,14},{3,15},{4,8},{5,9},{6,10},{7,11},{8,4},{9,5},... | collective-permute-start | bytes 417800 | tf_op jit(solution)/shard_map/ppermute | solution.py:270
  43.2 2.2 %shard_map.64 = (f32[128,512]{1,0:T(8,128)S(1)}, f32[1,512]{1,0:T(1,128)S(1)}) custom-call(s32[4,512]{1,0:T(4,128)S(1)} %get-tuple-element.137.refs_0_.limits_ref, bf16[512,128]{1,0:T(8,128)(2,1)S(1)} %bitcast.9, bf16[1024,128]{1,0:T(8,128)(2,1)S(1)} %collective-permute-done.1.refs_4_.refs_2_, bf16[1024,128]{1,0:T(8,128)(2,1)S(1)} %collective-permute-done.2.refs_5_.refs_3_, ...), custom_call_target="tpu_custom_call" | custom-call | tf_op jit(solution)/shard_map/pallas_call | solution.py:334
  45.4 0.5 collective-permute-done.10.part_ref
  45.9 0.1 shard_map.65
  46.0 2.7 %collective-permute-done.11.refs_2_ = bf16[136,512]{1,0:T(8,128)(2,1)S(1)} collective-permute-done((bf16[136,512]{1,0:T(8,128)(2,1)S(1)}, bf16[136,512]{1,0:T(8,128)(2,1)S(1)}, u32[]{:S(2)}, u32[]{:S(2)}) %collective-permute-start.11) | collective-permute-done | bytes 139296 | tf_op jit(solution)/shard_map/ppermute | solution.py:270
  48.7 0.8 %merge.1 = bf16[512,128]{1,0:T(8,128)(2,1)} custom-call(f32[128,512]{1,0:T(8,128)S(1)} %get-tuple-element.146.refs_0_, f32[1,512]{1,0:T(1,128)S(1)} %get-tuple-element.147.refs_1_, bf16[136,512]{1,0:T(8,128)(2,1)S(1)} %collective-permute-done.11.refs_2_), custom_call_target="tpu_custom_call" | custom-call | tf_op jit(solution)/shard_map/merge/pallas_call | solution.py:457
Async XLA Ops:
  0.0 8.8 %collective-permute-start.1 = (bf16[1024,128]{1,0:T(8,128)(2,1)}, bf16[1024,128]{1,0:T(8,128)(2,1)S(1)}, u32[]{:S(2)}, u32[]{:S(2)}) collective-permute-start(bf16[1024,128]{1,0:T(8,128)(2,1)} %refs_3_.1), channel_id=1, source_target_pairs={{0,1},{1,0},{2,3},{3,2},{4,5},{5,4},{6,7},{7,6},{8,9},{9,8},{10,11... | collective-permute-start | bytes 786440 | tf_op jit(solution)/shard_map/ppermute | solution.py:270
  0.5 8.4 %collective-permute-start.2 = (bf16[1024,128]{1,0:T(8,128)(2,1)}, bf16[1024,128]{1,0:T(8,128)(2,1)S(1)}, u32[]{:S(2)}, u32[]{:S(2)}) collective-permute-start(bf16[1024,128]{1,0:T(8,128)(2,1)} %refs_4_.1), channel_id=1, source_target_pairs={{0,1},{1,0},{2,3},{3,2},{4,5},{5,4},{6,7},{7,6},{8,9},{9,8},{10,11... | collective-permute-start | bytes 786440 | tf_op jit(solution)/shard_map/ppermute | solution.py:270
  0.5 9.9 %collective-permute-start.3 = (bf16[1024,128]{1,0:T(8,128)(2,1)}, bf16[1024,128]{1,0:T(8,128)(2,1)S(1)}, u32[]{:S(2)}, u32[]{:S(2)}) collective-permute-start(bf16[1024,128]{1,0:T(8,128)(2,1)} %refs_3_.1), channel_id=1, source_target_pairs={{0,2},{1,3},{2,0},{3,1},{4,6},{5,7},{6,4},{7,5},{8,10},{9,11},{10,... | collective-permute-start | bytes 786440 | tf_op jit(solution)/shard_map/ppermute | solution.py:270
  3.5 5.3 %collective-permute-start = (bf16[512,128]{1,0:T(8,128)(2,1)}, bf16[512,128]{1,0:T(8,128)(2,1)S(1)}, u32[]{:S(2)}, u32[]{:S(2)}) collective-permute-start(bf16[512,128]{1,0:T(8,128)(2,1)} %bitcast.5), channel_id=1, source_target_pairs={{0,4},{1,5},{2,6},{3,7},{4,0},{5,1},{6,2},{7,3},{8,12},{9,13},{10,... | collective-permute-start | bytes 393224 | tf_op jit(solution)/shard_map/ppermute | solution.py:270
  5.7 0.7 %copy-start.1 = (s32[512]{0:T(512)S(1)}, s32[512]{0:T(512)}, u32[]{:S(2)}) copy-start(s32[512]{0:T(512)} %param.9) | copy-start | bytes 6148
  8.8 1.6 %copy-start.2 = (bf16[1024,128]{1,0:T(8,128)(2,1)S(1)}, bf16[1024,128]{1,0:T(8,128)(2,1)}, u32[]{:S(2)}) copy-start(bf16[1024,128]{1,0:T(8,128)(2,1)} %refs_4_.1) | copy-start | bytes 786436
  8.9 3.1 %copy-start = (bf16[32,16,128]{2,1,0:T(8,128)(2,1)S(1)}, bf16[32,16,128]{2,1,0:T(8,128)(2,1)}, u32[]{:S(2)}) copy-start(bf16[32,16,128]{2,1,0:T(8,128)(2,1)} %param.5) | copy-start | bytes 393220
  10.4 12.4 %collective-permute-start.5 = (bf16[1024,128]{1,0:T(8,128)(2,1)S(1)}, bf16[1024,128]{1,0:T(8,128)(2,1)S(1)}, u32[]{:S(2)}, u32[]{:S(2)}) collective-permute-start(bf16[1024,128]{1,0:T(8,128)(2,1)S(1)} %collective-permute-done.3.refs_0_.refs_2_.refs_6_.refs_4_), channel_id=1, source_target_pairs={{0,1},{1,0},{2,3},{3,2},{4,5},{5,4},{6,7},{7,6},{8,9},{9,8},{10,11... | collective-permute-start | bytes 786440 | tf_op jit(solution)/shard_map/ppermute | solution.py:270
  10.5 13.7 %collective-permute-start.6 = (bf16[1024,128]{1,0:T(8,128)(2,1)S(1)}, bf16[1024,128]{1,0:T(8,128)(2,1)S(1)}, u32[]{:S(2)}, u32[]{:S(2)}) collective-permute-start(bf16[1024,128]{1,0:T(8,128)(2,1)S(1)} %copy-done.2), channel_id=1, source_target_pairs={{0,2},{1,3},{2,0},{3,1},{4,6},{5,7},{6,4},{7,5},{8,10},{9,11},{10,... | collective-permute-start | bytes 786440 | tf_op jit(solution)/shard_map/ppermute | solution.py:270
  11.9 9.3 %collective-permute-start.4 = (bf16[512,128]{1,0:T(8,128)(2,1)S(1)}, bf16[512,128]{1,0:T(8,128)(2,1)S(1)}, u32[]{:S(2)}, u32[]{:S(2)}) collective-permute-start(bf16[512,128]{1,0:T(8,128)(2,1)S(1)} %bitcast.7), channel_id=1, source_target_pairs={{0,8},{1,9},{2,10},{3,11},{4,12},{5,13},{6,14},{7,15},{8,0},{9,1},... | collective-permute-start | bytes 393224 | tf_op jit(solution)/shard_map/ppermute | solution.py:270
  24.1 1.6 %collective-permute-start.7 = (bf16[1024,128]{1,0:T(8,128)(2,1)S(1)}, bf16[1024,128]{1,0:T(8,128)(2,1)S(1)}, u32[]{:S(2)}, u32[]{:S(2)}) collective-permute-start(bf16[1024,128]{1,0:T(8,128)(2,1)S(1)} %collective-permute-done.6.refs_0_.refs_3_.refs_7_.refs_5_), channel_id=1, source_target_pairs={{0,1},{1,0},{2,3},{3,2},{4,5},{5,4},{6,7},{7,6},{8,9},{9,8},{10,11... | collective-permute-start | bytes 786440 | tf_op jit(solution)/shard_map/ppermute | solution.py:270
  26.2 14.1 %collective-permute-start.9 = (bf16[136,512]{1,0:T(8,128)(2,1)S(1)}, bf16[136,512]{1,0:T(8,128)(2,1)S(1)}, u32[]{:S(2)}, u32[]{:S(2)}) collective-permute-start(bf16[136,512]{1,0:T(8,128)(2,1)S(1)} %shard_map.60), channel_id=1, source_target_pairs={{0,4},{1,5},{2,6},{3,7},{4,0},{5,1},{6,2},{7,3},{8,12},{9,13},{10,... | collective-permute-start | bytes 417800 | tf_op jit(solution)/shard_map/ppermute | solution.py:270
  27.0 9.9 %collective-permute-start.8 = (bf16[512,128]{1,0:T(8,128)(2,1)S(1)}, bf16[512,128]{1,0:T(8,128)(2,1)S(1)}, u32[]{:S(2)}, u32[]{:S(2)}) collective-permute-start(bf16[512,128]{1,0:T(8,128)(2,1)S(1)} %bitcast.8), channel_id=1, source_target_pairs={{0,12},{1,13},{2,14},{3,15},{4,8},{5,9},{6,10},{7,11},{8,4},{9,5},... | collective-permute-start | bytes 393224 | tf_op jit(solution)/shard_map/ppermute | solution.py:270
  39.7 6.2 %collective-permute-start.10 = (bf16[136,512]{1,0:T(8,128)(2,1)S(1)}, bf16[136,512]{1,0:T(8,128)(2,1)S(1)}, u32[]{:S(2)}, u32[]{:S(2)}) collective-permute-start(bf16[136,512]{1,0:T(8,128)(2,1)S(1)} %shard_map.61), channel_id=1, source_target_pairs={{0,4},{1,5},{2,6},{3,7},{4,0},{5,1},{6,2},{7,3},{8,12},{9,13},{10,... | collective-permute-start | bytes 417800 | tf_op jit(solution)/shard_map/ppermute | solution.py:270
  40.5 8.2 %collective-permute-start.11 = (bf16[136,512]{1,0:T(8,128)(2,1)S(1)}, bf16[136,512]{1,0:T(8,128)(2,1)S(1)}, u32[]{:S(2)}, u32[]{:S(2)}) collective-permute-start(bf16[136,512]{1,0:T(8,128)(2,1)S(1)} %shard_map.63), channel_id=1, source_target_pairs={{0,12},{1,13},{2,14},{3,15},{4,8},{5,9},{6,10},{7,11},{8,4},{9,5},... | collective-permute-start | bytes 417800 | tf_op jit(solution)/shard_map/ppermute | solution.py:270

commit v9 on v6

--- a/solution.py
+++ b/solution.py
@@ -368,25 +368,28 @@
     attend(0, [0])
     for index in range(1, last - 1):
         attend(index, [0, 1])
-    far_pair[0], = hold(far_pair[0])
-    across_keys = swap(far_pair[0], 1)
-    attend(last - 1, [0, 1])
     source = stages[last][0] ^ (stages[last][0] & -stages[last][0])
     (got[source],) = hold(got[source])
     gather(last)
     ready(last)
+    far_pair[0], = hold(far_pair[0])
+    across_keys = swap(far_pair[0], 1)
+    attend(last - 1, [0, 1])
     ahead = stage_query[last - 1]
     block = jax.ShapeDtypeStruct((shard_keys, stage_rows), jnp.bfloat16)
-    weighed = pl.pallas_call(
-        functools.partial(weigh_kernel, scale, last - 1, [2, 3]),
-        in_specs=[vmem] * 4,
-        out_specs=[vmem] * 4,
-        out_shape=[block, block, stat, stat],
-        scratch_shapes=[pltpu.VMEM((2, shard_keys, tile), jnp.float32)],
-        compiler_params=params,
-        name="weigh",
-    )(chain[0], ahead, far_pair[0], across_keys)
-    weighed = hold(*weighed)
+
+    def weigh(block_index, keys):
+        results = pl.pallas_call(
+            functools.partial(weigh_kernel, scale, last - 1, [block_index]),
+            in_specs=[vmem] * 3,
+            out_specs=[vmem] * 2,
+            out_shape=[block, stat],
+            scratch_shapes=[pltpu.VMEM((2, shard_keys, tile), jnp.float32)],
+            compiler_params=params,
+        )(chain[0], ahead, keys)
+        return hold(*results)
+
+    far_weights = weigh(2, far_pair[0])
     far_pair[1], = hold(far_pair[1])
     across_values = swap(far_pair[1], 1)
     pairs += [far_pair, [across_keys, across_values]]
@@ -402,12 +405,11 @@
         )(values, weights, top, *states[last - 1])
         return hold(*results)
 
-    states[last - 1] = finish(far_pair[1], weighed[0], weighed[2], None, state_shapes)
-    if outer == 4:
-        attend(1, [2])
+    states[last - 1] = finish(far_pair[1], *far_weights, None, state_shapes)
+    across_weights = weigh(3, across_keys)
     (across_values,) = hold(across_values)
     pairs[3] = [across_keys, across_values]
-    (packed,) = finish(across_values, weighed[1], weighed[3], whole_plan, [packed_shape(stage_rows)])
+    (packed,) = finish(across_values, *across_weights, whole_plan, [packed_shape(stage_rows)])
     own_plan = [(at, "float", 0, at * tile, tile) for at in tiles]
     parts = []
 
@@ -430,7 +432,7 @@
 
     if outer == 4:
         handed = swap(packed, inner)
-        (packed,) = attend(1, [3], whole_plan, coded)
+        (packed,) = attend(1, [2, 3], whole_plan, coded)
         parts.append(swap(packed, inner))
         value, level = attend(3, [0, 1, 2, 3], own_plan, float_shapes(stage_rows))
         (handed,) = hold(handed)

time: 49 us -> 43.7 us (0.89)
  waiting for transfers between devices: 16.6 us -> 11.7 us
  starting transfers between devices: 15.3 us -> 14.8 us
    ppermute x12, waiting for transfers between devices: 16.6 us -> 11.7 us  [swap(): return lax.ppermute(array, 'ctx', [(i, i ^ step) for i in range(size)])]
    pallas_call x1 -> x2, Pallas kernels: 1.32 us -> 1.54 us  [weigh(): pl.pallas_call(functools.partial(weigh_kernel, scale, last - 1, [block_in...]
    pallas_call x7 -> x6, Pallas kernels: 12.1 us -> 11.9 us  [attend(): pl.pallas_call(functools.partial(attend_kernel, scale, index, blocks, sta...]
  transfers between devices with their start and end apart: 12 -> 12, of which waited for: 5 -> 4; matrix products, arithmetic and copies ran while one was open for 0% -> 0% of each run, Pallas kernels for 29% -> 32%
where the time goes in v9:
time: 43.7 us; the launch traced here: 43.5 us
  Pallas kernels  15.5 us (35%)
  starting transfers between devices  14.8 us (34%)
  waiting for transfers between devices  11.7 us (27%)
  between operations  0.81 us (2%)
  local copies, waits for them, and re-layouts  0.68 us (2%)
    ppermute x12, starting transfers between devices, swap(): return lax.ppermute(array, 'ctx', [(i, i ^ step) for i in range(size)])  14.8 us
    pallas_call x6, Pallas kernels, attend(): pl.pallas_call(functools.partial(attend_kernel, scale, index, blocks, sta...  11.9 us
    ppermute x12, waiting for transfers between devices, swap(): return lax.ppermute(array, 'ctx', [(i, i ^ step) for i in range(size)])  11.7 us
    pallas_call x2, Pallas kernels, weigh(): pl.pallas_call(functools.partial(weigh_kernel, scale, last - 1, [block_in...  1.54 us
  transfers between devices with their start and end apart: 12, of which 4 were waited for; matrix products, arithmetic and copies ran while one was open for 0% of the time, Pallas kernels for 32%

profile of v9, /device:TPU:0, one launch (start us, length us, event | category | flops | bytes accessed | tf_op | source)
XLA Modules:
  0.0 43.5 jit_solution(1130358604556472765)
XLA Ops:
  0.0 0.5 %collective-permute-start.1 = (bf16[1024,128]{1,0:T(8,128)(2,1)}, bf16[1024,128]{1,0:T(8,128)(2,1)S(1)}, u32[]{:S(2)}, u32[]{:S(2)}) collective-permute-start(bf16[1024,128]{1,0:T(8,128)(2,1)} %refs_3_.1), channel_id=1, source_target_pairs={{0,1},{1,0},{2,3},{3,2},{4,5},{5,4},{6,7},{7,6},{8,9},{9,8},{10,11... | collective-permute-start | bytes 786440 | tf_op jit(solution)/shard_map/ppermute | solution.py:270
  0.5 0.0 collective-permute-start.2
  0.5 3.1 %collective-permute-start = (bf16[512,128]{1,0:T(8,128)(2,1)}, bf16[512,128]{1,0:T(8,128)(2,1)S(1)}, u32[]{:S(2)}, u32[]{:S(2)}) collective-permute-start(bf16[512,128]{1,0:T(8,128)(2,1)} %bitcast.5), channel_id=1, source_target_pairs={{0,4},{1,5},{2,6},{3,7},{4,0},{5,1},{6,2},{7,3},{8,12},{9,13},{10,... | collective-permute-start | bytes 393224 | tf_op jit(solution)/shard_map/ppermute | solution.py:270
  3.6 1.5 %collective-permute-start.4 = (bf16[1024,128]{1,0:T(8,128)(2,1)}, bf16[1024,128]{1,0:T(8,128)(2,1)S(1)}, u32[]{:S(2)}, u32[]{:S(2)}) collective-permute-start(bf16[1024,128]{1,0:T(8,128)(2,1)} %refs_3_.1), channel_id=1, source_target_pairs={{0,2},{1,3},{2,0},{3,1},{4,6},{5,7},{6,4},{7,5},{8,10},{9,11},{10,... | collective-permute-start | bytes 786440 | tf_op jit(solution)/shard_map/ppermute | solution.py:270
  5.1 0.5 %collective-permute-start.5 = (bf16[1024,128]{1,0:T(8,128)(2,1)}, bf16[1024,128]{1,0:T(8,128)(2,1)S(1)}, u32[]{:S(2)}, u32[]{:S(2)}) collective-permute-start(bf16[1024,128]{1,0:T(8,128)(2,1)} %refs_4_.1), channel_id=1, source_target_pairs={{0,2},{1,3},{2,0},{3,1},{4,6},{5,7},{6,4},{7,5},{8,10},{9,11},{10,... | collective-permute-start | bytes 786440 | tf_op jit(solution)/shard_map/ppermute | solution.py:270
  5.6 1.8 %collective-permute-done.refs_1_ = bf16[512,128]{1,0:T(8,128)(2,1)S(1)} collective-permute-done((bf16[512,128]{1,0:T(8,128)(2,1)}, bf16[512,128]{1,0:T(8,128)(2,1)S(1)}, u32[]{:S(2)}, u32[]{:S(2)}) %collective-permute-start) | collective-permute-done | bytes 131104 | tf_op jit(solution)/shard_map/ppermute | solution.py:270
  7.4 2.8 %collective-permute-start.3 = (bf16[512,128]{1,0:T(8,128)(2,1)}, bf16[512,128]{1,0:T(8,128)(2,1)S(1)}, u32[]{:S(2)}, u32[]{:S(2)}) collective-permute-start(bf16[512,128]{1,0:T(8,128)(2,1)} %bitcast.6), channel_id=1, source_target_pairs={{0,8},{1,9},{2,10},{3,11},{4,12},{5,13},{6,14},{7,15},{8,0},{9,1},... | collective-permute-start | bytes 393224 | tf_op jit(solution)/shard_map/ppermute | solution.py:270
  10.8 0.0 copy-start.1
  10.9 0.7 %copy-done.1 = s32[512]{0:T(512)S(1)} copy-done((s32[512]{0:T(512)S(1)}, s32[512]{0:T(512)}, u32[]{:S(2)}) %copy-start.1) | copy-done | bytes 2072
  11.5 2.1 %shard_map.55 = (f32[1,512]{1,0:T(1,128)S(1)}, f32[1,512]{1,0:T(1,128)S(1)}, f32[128,512]{1,0:T(8,128)S(1)}, s32[4,512]{1,0:T(4,128)S(1)}, bf16[1024,128]{1,0:T(8,128)(2,1)S(1)}, /*index=5*/bf16[1024,128]{1,0:T(8,128)(2,1)S(1)}) custom-call(s32[4,128]{1,0:T(4,128)S(1)} %bitcast.9, s32[1,1]{1,0:T(1,128)} %bitcast.4.refs_1_, bf16[512,128]{1,0:T(8,128)(2,1)} %bitcast.7, ...), custom_call_target="tpu_custom_call" | custom-call | tf_op jit(solution)/shard_map/pallas_call | solution.py:334
  13.6 0.0 collective-permute-done.1.refs_4_.refs_2_
  13.7 0.0 collective-permute-done.2.refs_5_.refs_3_
  13.7 1.5 %shard_map.56 = (f32[1,512]{1,0:T(1,128)S(1)}, f32[1,512]{1,0:T(1,128)S(1)}, f32[128,512]{1,0:T(8,128)S(1)}) custom-call(s32[4,512]{1,0:T(4,128)S(1)} %get-tuple-element.129.refs_0_.limits_ref, bf16[512,128]{1,0:T(8,128)(2,1)S(1)} %collective-permute-done.refs_1_, bf16[1024,128]{1,0:T(8,128)(2,1)S(1)} %get-tuple-element.78.refs_2_, ...), custom_call_target="tpu_custom_call" | custom-call | tf_op jit(solution)/shard_map/pallas_call | solution.py:334
  15.2 1.0 %collective-permute-done.3.refs_1_.q_ref = bf16[512,128]{1,0:T(8,128)(2,1)S(1)} collective-permute-done((bf16[512,128]{1,0:T(8,128)(2,1)}, bf16[512,128]{1,0:T(8,128)(2,1)S(1)}, u32[]{:S(2)}, u32[]{:S(2)}) %collective-permute-start.3) | collective-permute-done | bytes 131104 | tf_op jit(solution)/shard_map/ppermute | solution.py:270
  16.2 0.0 collective-permute-done.4.refs_0_.refs_2_.refs_6_.refs_4_
  16.2 1.5 %shard_map.57 = (f32[1,512]{1,0:T(1,128)S(1)}, f32[1,512]{1,0:T(1,128)S(1)}, f32[128,512]{1,0:T(8,128)S(1)}) custom-call(s32[4,512]{1,0:T(4,128)S(1)} %get-tuple-element.129.refs_0_.limits_ref, bf16[512,128]{1,0:T(8,128)(2,1)S(1)} %collective-permute-done.3.refs_1_.q_ref, bf16[1024,128]{1,0:T(8,128)(2,1)S(1)} %get-tuple-element.78.refs_2_, ...), custom_call_target="tpu_custom_call" | custom-call | tf_op jit(solution)/shard_map/pallas_call | solution.py:334
  17.7 0.1 collective-permute-start.6
  17.8 0.8 %shard_map.58 = (bf16[1024,512]{1,0:T(8,128)(2,1)S(1)}, f32[1,512]{1,0:T(1,128)S(1)}) custom-call(s32[4,512]{1,0:T(4,128)S(1)} %get-tuple-element.129.refs_0_.limits_ref, bf16[512,128]{1,0:T(8,128)(2,1)S(1)} %collective-permute-done.3.refs_1_.q_ref, bf16[1024,128]{1,0:T(8,128)(2,1)S(1)} %collective-permute-done.4.refs_0_.refs_2_.refs_6_.refs_4_), custom_call_target="tpu_custom_call" | custom-call | tf_op jit(solution)/shard_map/pallas_call | solution.py:382
  18.6 0.0 collective-permute-done.5.refs_0_.refs_3_.refs_7_.refs_5_
  18.6 0.5 %collective-permute-start.7 = (bf16[1024,128]{1,0:T(8,128)(2,1)S(1)}, bf16[1024,128]{1,0:T(8,128)(2,1)S(1)}, u32[]{:S(2)}, u32[]{:S(2)}) collective-permute-start(bf16[1024,128]{1,0:T(8,128)(2,1)S(1)} %collective-permute-done.5.refs_0_.refs_3_.refs_7_.refs_5_), channel_id=1, source_target_pairs={{0,1},{1,0},{2,3},{3,2},{4,5},{5,4},{6,7},{7,6},{8,9},{9,8},{10,11... | collective-permute-start | bytes 786440 | tf_op jit(solution)/shard_map/ppermute | solution.py:270
  19.1 0.4 shard_map.59
  19.5 0.0 collective-permute-done.6.refs_0_.refs_4_.refs_8_.refs_6_
  19.5 0.8 %shard_map.60 = (bf16[1024,512]{1,0:T(8,128)(2,1)S(1)}, f32[1,512]{1,0:T(1,128)S(1)}) custom-call(s32[4,512]{1,0:T(4,128)S(1)} %get-tuple-element.129.refs_0_.limits_ref, bf16[512,128]{1,0:T(8,128)(2,1)S(1)} %collective-permute-done.3.refs_1_.q_ref, bf16[1024,128]{1,0:T(8,128)(2,1)S(1)} %collective-permute-done.6.refs_0_.refs_4_.refs_8_.refs_6_), custom_call_target="tpu_custom_call" | custom-call | tf_op jit(solution)/shard_map/pallas_call | solution.py:382
  20.3 0.0 collective-permute-done.7.refs_0_.refs_5_.refs_9_.refs_7_
  20.3 0.5 %shard_map.61 = bf16[136,512]{1,0:T(8,128)(2,1)S(1)} custom-call(bf16[1024,128]{1,0:T(8,128)(2,1)S(1)} %collective-permute-done.7.refs_0_.refs_5_.refs_9_.refs_7_, bf16[1024,512]{1,0:T(8,128)(2,1)S(1)} %get-tuple-element.110.refs_1_, f32[1,512]{1,0:T(1,128)S(1)} %get-tuple-element.111.refs_2_, f32[1,512]{1,0:T(1,128)S(1)} %get-tuple-element.112.refs_3_, ...), custom_call_target="tpu_custom_call" | custom-call | tf_op jit(solution)/shard_map/pallas_call | solution.py:398
  20.8 0.7 %collective-permute-start.9 = (bf16[136,512]{1,0:T(8,128)(2,1)S(1)}, bf16[136,512]{1,0:T(8,128)(2,1)S(1)}, u32[]{:S(2)}, u32[]{:S(2)}) collective-permute-start(bf16[136,512]{1,0:T(8,128)(2,1)S(1)} %shard_map.61), channel_id=1, source_target_pairs={{0,4},{1,5},{2,6},{3,7},{4,0},{5,1},{6,2},{7,3},{8,12},{9,13},{10,... | collective-permute-start | bytes 417800 | tf_op jit(solution)/shard_map/ppermute | solution.py:270
  21.5 1.4 %collective-permute-start.8 = (bf16[512,128]{1,0:T(8,128)(2,1)S(1)}, bf16[512,128]{1,0:T(8,128)(2,1)S(1)}, u32[]{:S(2)}, u32[]{:S(2)}) collective-permute-start(bf16[512,128]{1,0:T(8,128)(2,1)S(1)} %collective-permute-done.3.refs_1_.q_ref), channel_id=1, source_target_pairs={{0,4},{1,5},{2,6},{3,7},{4,0},{5,1},{6,2},{7,3},{8,12},{9,13},{10,... | collective-permute-start | bytes 393224 | tf_op jit(solution)/shard_map/ppermute | solution.py:270
  22.9 1.6 %shard_map.62 = bf16[136,512]{1,0:T(8,128)(2,1)S(1)} custom-call(s32[4,512]{1,0:T(4,128)S(1)} %get-tuple-element.129.refs_0_.limits_ref, bf16[512,128]{1,0:T(8,128)(2,1)S(1)} %collective-permute-done.refs_1_, bf16[1024,128]{1,0:T(8,128)(2,1)S(1)} %collective-permute-done.4.refs_0_.refs_2_.refs_6_.refs_4_, ...), custom_call_target="tpu_custom_call" | custom-call | tf_op jit(solution)/shard_map/pallas_call | solution.py:334
  24.5 5.1 %collective-permute-done.8.refs_1_ = bf16[512,128]{1,0:T(8,128)(2,1)S(1)} collective-permute-done((bf16[512,128]{1,0:T(8,128)(2,1)S(1)}, bf16[512,128]{1,0:T(8,128)(2,1)S(1)}, u32[]{:S(2)}, u32[]{:S(2)}) %collective-permute-start.8) | collective-permute-done | bytes 131104 | tf_op jit(solution)/shard_map/ppermute | solution.py:270
  29.6 2.8 %shard_map.63 = (f32[128,512]{1,0:T(8,128)S(1)}, f32[1,512]{1,0:T(1,128)S(1)}) custom-call(s32[4,512]{1,0:T(4,128)S(1)} %get-tuple-element.129.refs_0_.limits_ref, bf16[512,128]{1,0:T(8,128)(2,1)S(1)} %collective-permute-done.8.refs_1_, bf16[1024,128]{1,0:T(8,128)(2,1)S(1)} %get-tuple-element.78.refs_2_, bf16[1024,128]{1,0:T(8,128)(2,1)S(1)} %get-tuple-element.79.refs_3_, ...), custom_call_target="tpu_custom_call" | custom-call | tf_op jit(solution)/shard_map/pallas_call | solution.py:334
  32.5 0.0 copy-start
  32.5 0.7 %collective-permute-start.10 = (bf16[136,512]{1,0:T(8,128)(2,1)S(1)}, bf16[136,512]{1,0:T(8,128)(2,1)S(1)}, u32[]{:S(2)}, u32[]{:S(2)}) collective-permute-start(bf16[136,512]{1,0:T(8,128)(2,1)S(1)} %shard_map.62), channel_id=1, source_target_pairs={{0,4},{1,5},{2,6},{3,7},{4,0},{5,1},{6,2},{7,3},{8,12},{9,13},{10,... | collective-permute-start | bytes 417800 | tf_op jit(solution)/shard_map/ppermute | solution.py:270
  33.2 0.0 collective-permute-done.9.part_ref
  33.2 0.3 shard_map.64
  33.5 3.1 %collective-permute-start.11 = (bf16[136,512]{1,0:T(8,128)(2,1)S(1)}, bf16[136,512]{1,0:T(8,128)(2,1)S(1)}, u32[]{:S(2)}, u32[]{:S(2)}) collective-permute-start(bf16[136,512]{1,0:T(8,128)(2,1)S(1)} %shard_map.64), channel_id=1, source_target_pairs={{0,12},{1,13},{2,14},{3,15},{4,8},{5,9},{6,10},{7,11},{8,4},{9,5},... | collective-permute-start | bytes 417800 | tf_op jit(solution)/shard_map/ppermute | solution.py:270
  36.6 0.0 copy-done
  36.6 2.2 %shard_map.65 = (f32[128,512]{1,0:T(8,128)S(1)}, f32[1,512]{1,0:T(1,128)S(1)}) custom-call(s32[4,512]{1,0:T(4,128)S(1)} %get-tuple-element.129.refs_0_.limits_ref, bf16[512,128]{1,0:T(8,128)(2,1)S(1)} %bitcast.8, bf16[1024,128]{1,0:T(8,128)(2,1)S(1)} %collective-permute-done.1.refs_4_.refs_2_, bf16[1024,128]{1,0:T(8,128)(2,1)S(1)} %collective-permute-done.2.refs_5_.refs_3_, ...), custom_call_target="tpu_custom_call" | custom-call | tf_op jit(solution)/shard_map/pallas_call | solution.py:334
  38.8 0.0 collective-permute-done.10.part_ref
  38.8 0.1 shard_map.66
  38.9 3.8 %collective-permute-done.11.refs_2_ = bf16[136,512]{1,0:T(8,128)(2,1)S(1)} collective-permute-done((bf16[136,512]{1,0:T(8,128)(2,1)S(1)}, bf16[136,512]{1,0:T(8,128)(2,1)S(1)}, u32[]{:S(2)}, u32[]{:S(2)}) %collective-permute-start.11) | collective-permute-done | bytes 139296 | tf_op jit(solution)/shard_map/ppermute | solution.py:270
  42.7 0.8 %merge.1 = bf16[512,128]{1,0:T(8,128)(2,1)} custom-call(f32[128,512]{1,0:T(8,128)S(1)} %get-tuple-element.138.refs_0_, f32[1,512]{1,0:T(1,128)S(1)} %get-tuple-element.139.refs_1_, bf16[136,512]{1,0:T(8,128)(2,1)S(1)} %collective-permute-done.11.refs_2_), custom_call_target="tpu_custom_call" | custom-call | tf_op jit(solution)/shard_map/merge/pallas_call | solution.py:458
Async XLA Ops:
  0.0 13.7 %collective-permute-start.1 = (bf16[1024,128]{1,0:T(8,128)(2,1)}, bf16[1024,128]{1,0:T(8,128)(2,1)S(1)}, u32[]{:S(2)}, u32[]{:S(2)}) collective-permute-start(bf16[1024,128]{1,0:T(8,128)(2,1)} %refs_3_.1), channel_id=1, source_target_pairs={{0,1},{1,0},{2,3},{3,2},{4,5},{5,4},{6,7},{7,6},{8,9},{9,8},{10,11... | collective-permute-start | bytes 786440 | tf_op jit(solution)/shard_map/ppermute | solution.py:270
  0.5 13.2 %collective-permute-start.2 = (bf16[1024,128]{1,0:T(8,128)(2,1)}, bf16[1024,128]{1,0:T(8,128)(2,1)S(1)}, u32[]{:S(2)}, u32[]{:S(2)}) collective-permute-start(bf16[1024,128]{1,0:T(8,128)(2,1)} %refs_4_.1), channel_id=1, source_target_pairs={{0,1},{1,0},{2,3},{3,2},{4,5},{5,4},{6,7},{7,6},{8,9},{9,8},{10,11... | collective-permute-start | bytes 786440 | tf_op jit(solution)/shard_map/ppermute | solution.py:270
  0.5 6.9 %collective-permute-start = (bf16[512,128]{1,0:T(8,128)(2,1)}, bf16[512,128]{1,0:T(8,128)(2,1)S(1)}, u32[]{:S(2)}, u32[]{:S(2)}) collective-permute-start(bf16[512,128]{1,0:T(8,128)(2,1)} %bitcast.5), channel_id=1, source_target_pairs={{0,4},{1,5},{2,6},{3,7},{4,0},{5,1},{6,2},{7,3},{8,12},{9,13},{10,... | collective-permute-start | bytes 393224 | tf_op jit(solution)/shard_map/ppermute | solution.py:270
  3.6 12.6 %collective-permute-start.4 = (bf16[1024,128]{1,0:T(8,128)(2,1)}, bf16[1024,128]{1,0:T(8,128)(2,1)S(1)}, u32[]{:S(2)}, u32[]{:S(2)}) collective-permute-start(bf16[1024,128]{1,0:T(8,128)(2,1)} %refs_3_.1), channel_id=1, source_target_pairs={{0,2},{1,3},{2,0},{3,1},{4,6},{5,7},{6,4},{7,5},{8,10},{9,11},{10,... | collective-permute-start | bytes 786440 | tf_op jit(solution)/shard_map/ppermute | solution.py:270
  5.1 13.5 %collective-permute-start.5 = (bf16[1024,128]{1,0:T(8,128)(2,1)}, bf16[1024,128]{1,0:T(8,128)(2,1)S(1)}, u32[]{:S(2)}, u32[]{:S(2)}) collective-permute-start(bf16[1024,128]{1,0:T(8,128)(2,1)} %refs_4_.1), channel_id=1, source_target_pairs={{0,2},{1,3},{2,0},{3,1},{4,6},{5,7},{6,4},{7,5},{8,10},{9,11},{10,... | collective-permute-start | bytes 786440 | tf_op jit(solution)/shard_map/ppermute | solution.py:270
  7.4 8.7 %collective-permute-start.3 = (bf16[512,128]{1,0:T(8,128)(2,1)}, bf16[512,128]{1,0:T(8,128)(2,1)S(1)}, u32[]{:S(2)}, u32[]{:S(2)}) collective-permute-start(bf16[512,128]{1,0:T(8,128)(2,1)} %bitcast.6), channel_id=1, source_target_pairs={{0,8},{1,9},{2,10},{3,11},{4,12},{5,13},{6,14},{7,15},{8,0},{9,1},... | collective-permute-start | bytes 393224 | tf_op jit(solution)/shard_map/ppermute | solution.py:270
  10.8 0.7 %copy-start.1 = (s32[512]{0:T(512)S(1)}, s32[512]{0:T(512)}, u32[]{:S(2)}) copy-start(s32[512]{0:T(512)} %param.9) | copy-start | bytes 6148
  17.7 1.8 %collective-permute-start.6 = (bf16[1024,128]{1,0:T(8,128)(2,1)S(1)}, bf16[1024,128]{1,0:T(8,128)(2,1)S(1)}, u32[]{:S(2)}, u32[]{:S(2)}) collective-permute-start(bf16[1024,128]{1,0:T(8,128)(2,1)S(1)} %collective-permute-done.4.refs_0_.refs_2_.refs_6_.refs_4_), channel_id=1, source_target_pairs={{0,1},{1,0},{2,3},{3,2},{4,5},{5,4},{6,7},{7,6},{8,9},{9,8},{10,11... | collective-permute-start | bytes 786440 | tf_op jit(solution)/shard_map/ppermute | solution.py:270
  18.6 1.7 %collective-permute-start.7 = (bf16[1024,128]{1,0:T(8,128)(2,1)S(1)}, bf16[1024,128]{1,0:T(8,128)(2,1)S(1)}, u32[]{:S(2)}, u32[]{:S(2)}) collective-permute-start(bf16[1024,128]{1,0:T(8,128)(2,1)S(1)} %collective-permute-done.5.refs_0_.refs_3_.refs_7_.refs_5_), channel_id=1, source_target_pairs={{0,1},{1,0},{2,3},{3,2},{4,5},{5,4},{6,7},{7,6},{8,9},{9,8},{10,11... | collective-permute-start | bytes 786440 | tf_op jit(solution)/shard_map/ppermute | solution.py:270
  20.8 12.4 %collective-permute-start.9 = (bf16[136,512]{1,0:T(8,128)(2,1)S(1)}, bf16[136,512]{1,0:T(8,128)(2,1)S(1)}, u32[]{:S(2)}, u32[]{:S(2)}) collective-permute-start(bf16[136,512]{1,0:T(8,128)(2,1)S(1)} %shard_map.61), channel_id=1, source_target_pairs={{0,4},{1,5},{2,6},{3,7},{4,0},{5,1},{6,2},{7,3},{8,12},{9,13},{10,... | collective-permute-start | bytes 417800 | tf_op jit(solution)/shard_map/ppermute | solution.py:270
  21.5 8.1 %collective-permute-start.8 = (bf16[512,128]{1,0:T(8,128)(2,1)S(1)}, bf16[512,128]{1,0:T(8,128)(2,1)S(1)}, u32[]{:S(2)}, u32[]{:S(2)}) collective-permute-start(bf16[512,128]{1,0:T(8,128)(2,1)S(1)} %collective-permute-done.3.refs_1_.q_ref), channel_id=1, source_target_pairs={{0,4},{1,5},{2,6},{3,7},{4,0},{5,1},{6,2},{7,3},{8,12},{9,13},{10,... | collective-permute-start | bytes 393224 | tf_op jit(solution)/shard_map/ppermute | solution.py:270
  32.5 4.1 %copy-start = (bf16[32,16,128]{2,1,0:T(8,128)(2,1)S(1)}, bf16[32,16,128]{2,1,0:T(8,128)(2,1)}, u32[]{:S(2)}) copy-start(bf16[32,16,128]{2,1,0:T(8,128)(2,1)} %param.5) | copy-start | bytes 393220
  32.5 6.3 %collective-permute-start.10 = (bf16[136,512]{1,0:T(8,128)(2,1)S(1)}, bf16[136,512]{1,0:T(8,128)(2,1)S(1)}, u32[]{:S(2)}, u32[]{:S(2)}) collective-permute-start(bf16[136,512]{1,0:T(8,128)(2,1)S(1)} %shard_map.62), channel_id=1, source_target_pairs={{0,4},{1,5},{2,6},{3,7},{4,0},{5,1},{6,2},{7,3},{8,12},{9,13},{10,... | collective-permute-start | bytes 417800 | tf_op jit(solution)/shard_map/ppermute | solution.py:270
  33.5 9.2 %collective-permute-start.11 = (bf16[136,512]{1,0:T(8,128)(2,1)S(1)}, bf16[136,512]{1,0:T(8,128)(2,1)S(1)}, u32[]{:S(2)}, u32[]{:S(2)}) collective-permute-start(bf16[136,512]{1,0:T(8,128)(2,1)S(1)} %shard_map.64), channel_id=1, source_target_pairs={{0,12},{1,13},{2,14},{3,15},{4,8},{5,9},{6,10},{7,11},{8,4},{9,5},... | collective-permute-start | bytes 417800 | tf_op jit(solution)/shard_map/ppermute | solution.py:270

commit v10 on v9

--- a/solution.py
+++ b/solution.py
@@ -175,25 +175,21 @@
         limits_ref[k : k + 1, :] = wide[2 * k : 2 * k + 1] * 256 + wide[2 * k + 1 : 2 * k + 2] + span_ref[...]
 
 
-def attend_kernel(scale, index, blocks, has_state, plan, setup, *refs):
+def setup_kernel(own_tokens, head_count, offsets_ref, span_ref, *refs):
+    sources, limits_ref, targets, arrived = refs[:3], refs[3], refs[4:7], refs[7]
+    copies = [pltpu.make_async_copy(*pair, arrived.at[at]) for at, pair in enumerate(zip(sources, targets))]
+    for copy in copies:
+        copy.start()
+    spread_limits(lax.axis_index("ctx"), own_tokens, head_count, offsets_ref, span_ref, limits_ref)
+    for copy in copies:
+        copy.wait()
+
+
+def attend_kernel(scale, index, blocks, has_state, plan, *refs):
     me = lax.axis_index("ctx")
     refs = list(refs)
-    if setup:
-        offsets_ref, span_ref, q_hbm, k_hbm, v_hbm = refs[:5]
-        arrived, q_ref = refs.pop(), refs.pop()
-        scratch = [refs.pop() for _ in range(3)][::-1]
-        v_ref, k_ref, limits_ref = refs.pop(), refs.pop(), refs.pop()
-        pairs = ((q_hbm, q_ref), (k_hbm, k_ref), (v_hbm, v_ref))
-        copies = [pltpu.make_async_copy(*pair, arrived.at[at]) for at, pair in enumerate(pairs)]
-        for copy in copies:
-            copy.start()
-        spread_limits(me, *setup, offsets_ref, span_ref, limits_ref)
-        for copy in copies:
-            copy.wait()
-        refs = [limits_ref, q_ref, k_ref, v_ref] + refs[5:]
-    else:
-        scratch = [refs.pop() for _ in range(3)][::-1]
-        limits_ref, q_ref = refs[:2]
+    scratch = [refs.pop() for _ in range(3)][::-1]
+    limits_ref, q_ref = refs[:2]
     keys = refs[2 : 2 + 2 * len(blocks) : 2]
     values = refs[3 : 3 + 2 * len(blocks) : 2]
     rest = list(refs[2 + 2 * len(blocks) :])
@@ -317,37 +313,22 @@
     states = [None] * len(stages)
 
     def attend(index, blocks, plan=None, shapes=state_shapes):
-        setup = None
-        if chain[0] is None:
-            setup = (own_tokens, head_count)
-            shapes = shapes + [jax.ShapeDtypeStruct((len(stages), stage_rows), jnp.int32)]
-            shapes += [jax.ShapeDtypeStruct(array.shape, array.dtype) for array in pairs[0]]
-            own = [pltpu.with_memory_space_constraint(array, pltpu.HBM) for array in (query, *pairs[0])]
-            operands = [positions.reshape(-1, 128), span_offset.reshape(1, 1)] + own
-            specs = [vmem] * 2 + [pl.BlockSpec(memory_space=pltpu.HBM)] * 3
-            extra = [pltpu.VMEM(query.shape, query.dtype), pltpu.SemaphoreType.DMA((3,))]
-            operands += [array for b in blocks[1:] for array in pairs[b]]
-        else:
-            operands = [chain[0], stage_query[index]] + [array for b in blocks for array in pairs[b]]
-            operands += list(states[index] or ())
-            specs, extra = [], []
+        operands = [chain[0], stage_query[index]] + [array for b in blocks for array in pairs[b]]
+        operands += list(states[index] or ())
         results = pl.pallas_call(
             functools.partial(
-                attend_kernel, scale, index, blocks, states[index] is not None, plan, setup
+                attend_kernel, scale, index, blocks, states[index] is not None, plan
             ),
-            in_specs=specs + [vmem] * (len(operands) - len(specs)),
+            in_specs=[vmem] * len(operands),
             out_specs=[vmem] * len(shapes),
             out_shape=shapes,
             scratch_shapes=[
                 pltpu.VMEM((2, shard_keys, tile), jnp.float32),
                 pltpu.VMEM((2, shard_keys, tile), jnp.bfloat16),
                 pltpu.VMEM((len(blocks), head_width + extra_rows, shard_keys), jnp.bfloat16),
-            ]
-            + extra,
+            ],
             compiler_params=params,
         )(*operands)
-        if setup:
-            chain[0], pairs[0], results = results[-3], list(results[-2:]), results[:-3]
         chain[0], results = lax.optimization_barrier((chain[0], results))
         if plan is None:
             states[index] = results
@@ -365,36 +346,48 @@
     for index in range(len(stages) - 1):
         gather(index)
         ready(index)
-    attend(0, [0])
+    if fused_setup:
+        own = [pltpu.with_memory_space_constraint(array, pltpu.HBM) for array in (query, *pairs[0])]
+        chain[0], stage_query[0], *pairs[0] = pl.pallas_call(
+            functools.partial(setup_kernel, own_tokens, head_count),
+            in_specs=[vmem] * 2 + [pl.BlockSpec(memory_space=pltpu.HBM)] * 3,
+            out_specs=[vmem] * 4,
+            out_shape=[jax.ShapeDtypeStruct((len(stages), stage_rows), jnp.int32)]
+            + [jax.ShapeDtypeStruct(array.shape, array.dtype) for array in own],
+            scratch_shapes=[pltpu.SemaphoreType.DMA((3,))],
+            compiler_params=params,
+            name="setup",
+        )(positions.reshape(-1, 128), span_offset.reshape(1, 1), *own)
     for index in range(1, last - 1):
         attend(index, [0, 1])
-    source = stages[last][0] ^ (stages[last][0] & -stages[last][0])
-    (got[source],) = hold(got[source])
-    gather(last)
-    ready(last)
-    far_pair[0], = hold(far_pair[0])
-    across_keys = swap(far_pair[0], 1)
-    attend(last - 1, [0, 1])
-    ahead = stage_query[last - 1]
     block = jax.ShapeDtypeStruct((shard_keys, stage_rows), jnp.bfloat16)
 
-    def weigh(block_index, keys):
+    def weigh(index, block_index, keys):
         results = pl.pallas_call(
-            functools.partial(weigh_kernel, scale, last - 1, [block_index]),
+            functools.partial(weigh_kernel, scale, index, [block_index]),
             in_specs=[vmem] * 3,
             out_specs=[vmem] * 2,
             out_shape=[block, stat],
             scratch_shapes=[pltpu.VMEM((2, shard_keys, tile), jnp.float32)],
             compiler_params=params,
-        )(chain[0], ahead, keys)
+        )(chain[0], stage_query[index], keys)
         return hold(*results)
 
-    far_weights = weigh(2, far_pair[0])
+    far_pair[0], = hold(far_pair[0])
+    across_keys = swap(far_pair[0], 1)
+    if outer == 4:
+        first_weights = weigh(1, 2, far_pair[0])
+    source = stages[last][0] ^ (stages[last][0] & -stages[last][0])
+    (got[source],) = hold(got[source])
+    gather(last)
+    ready(last)
+    attend(last - 1, [0, 1])
+    far_weights = weigh(last - 1, 2, far_pair[0])
     far_pair[1], = hold(far_pair[1])
     across_values = swap(far_pair[1], 1)
     pairs += [far_pair, [across_keys, across_values]]
 
-    def finish(values, weights, top, plan, shapes):
+    def finish(index, values, weights, top, plan, shapes):
         results = pl.pallas_call(
             functools.partial(finish_kernel, 1, plan),
             in_specs=[vmem] * 6,
@@ -402,14 +395,14 @@
             out_shape=shapes,
             scratch_shapes=[pltpu.VMEM((1, head_width + extra_rows, shard_keys), jnp.bfloat16)],
             compiler_params=params,
-        )(values, weights, top, *states[last - 1])
+        )(values, weights, top, *states[index])
         return hold(*results)
 
-    states[last - 1] = finish(far_pair[1], *far_weights, None, state_shapes)
-    across_weights = weigh(3, across_keys)
+    states[last - 1] = finish(last - 1, far_pair[1], *far_weights, None, state_shapes)
+    across_weights = weigh(last - 1, 3, across_keys)
     (across_values,) = hold(across_values)
     pairs[3] = [across_keys, across_values]
-    (packed,) = finish(across_values, *across_weights, whole_plan, [packed_shape(stage_rows)])
+    (packed,) = finish(last - 1, across_values, *across_weights, whole_plan, [packed_shape(stage_rows)])
     own_plan = [(at, "float", 0, at * tile, tile) for at in tiles]
     parts = []
 
@@ -432,7 +425,8 @@
 
     if outer == 4:
         handed = swap(packed, inner)
-        (packed,) = attend(1, [2, 3], whole_plan, coded)
+        states[1] = finish(1, far_pair[1], *first_weights, None, state_shapes)
+        (packed,) = attend(1, [3], whole_plan, coded)
         parts.append(swap(packed, inner))
         value, level = attend(3, [0, 1, 2, 3], own_plan, float_shapes(stage_rows))
         (handed,) = hold(handed)
@@ -445,13 +439,13 @@
         for index in range(last - 2, 0, -1):
             send(index, attend(index, [2, 3], whole_plan, coded)[0])
     if per_stage == 1:
-        own = attend(0, [1, 2, 3], own_plan, float_shapes(rows))
+        own = attend(0, [0, 1, 2, 3], own_plan, float_shapes(rows))
         if outer == 4:
             own = fold("float", *own, parts.pop(0), float_shapes(rows))
     else:
         own_plan = [(0, "float", 1, 0, rows)]
         packed, *own = attend(
-            0, [1, 2, 3], whole_plan + own_plan, [packed_shape(stage_rows)] + float_shapes(rows)
+            0, [0, 1, 2, 3], whole_plan + own_plan, [packed_shape(stage_rows)] + float_shapes(rows)
         )
         send(0, packed)
     groups = [(slice(0, rows), [(at, 0) for at in range(len(parts))])]

time: 43.7 us -> 44 us (level)
  waiting for transfers between devices: 11.7 us -> 12.3 us
  starting transfers between devices: 14.8 us -> 14.3 us
    pallas_call x6 -> x5, Pallas kernels: 11.9 us -> 9.78 us  [attend(): pl.pallas_call(functools.partial(attend_kernel, scale, index, blocks, sta...]
    pallas_call x2 -> x4, Pallas kernels: 1.54 us -> 3.49 us  [the longest x3 2.32 us: weigh(): pl.pallas_call(functools.partial(weigh_kernel, scale, index, [block_index...]
    ppermute x12, waiting for transfers between devices: 11.7 us -> 12.3 us  [swap(): return lax.ppermute(array, 'ctx', [(i, i ^ step) for i in range(size)])]
    ppermute x12, starting transfers between devices: 14.8 us -> 14.3 us  [swap(): return lax.ppermute(array, 'ctx', [(i, i ^ step) for i in range(size)])]
    pallas_call x2 -> x3, Pallas kernels: 0.86 us -> 1.21 us  [finish(): pl.pallas_call(functools.partial(finish_kernel, 1, plan), in_specs=[vmem]...]
  transfers between devices with their start and end apart: 12 -> 12, of which waited for: 4 -> 5; matrix products, arithmetic and copies ran while one was open for 0% -> 0% of each run, Pallas kernels for 32% -> 33%
where the time goes in v10:
time: 44 us; the launch traced here: 43.8 us
  Pallas kernels  15.7 us (36%)
  starting transfers between devices  14.3 us (32%)
  waiting for transfers between devices  12.3 us (28%)
  between operations  0.83 us (2%)
  local copies, waits for them, and re-layouts  0.67 us (2%)
    ppermute x12, starting transfers between devices, swap(): return lax.ppermute(array, 'ctx', [(i, i ^ step) for i in range(size)])  14.3 us
    ppermute x12, waiting for transfers between devices, swap(): return lax.ppermute(array, 'ctx', [(i, i ^ step) for i in range(size)])  12.3 us
    pallas_call x5, Pallas kernels, attend(): pl.pallas_call(functools.partial(attend_kernel, scale, index, blocks, sta...  9.78 us
    pallas_call x3, Pallas kernels, weigh(): pl.pallas_call(functools.partial(weigh_kernel, scale, index, [block_index...  2.32 us
    pallas_call x3, Pallas kernels, finish(): pl.pallas_call(functools.partial(finish_kernel, 1, plan), in_specs=[vmem]...  1.21 us
    pallas_call x1, Pallas kernels, local(): pl.pallas_call(functools.partial(setup_kernel, own_tokens, head_count), i...  1.17 us
  transfers between devices with their start and end apart: 12, of which 5 were waited for; matrix products, arithmetic and copies ran while one was open for 0% of the time, Pallas kernels for 33%

profile of v10, /device:TPU:0, one launch (start us, length us, event | category | flops | bytes accessed | tf_op | source)
XLA Modules:
  0.0 43.8 jit_solution(15596241170089600594)
XLA Ops:
  0.0 0.5 %collective-permute-start.1 = (bf16[1024,128]{1,0:T(8,128)(2,1)}, bf16[1024,128]{1,0:T(8,128)(2,1)S(1)}, u32[]{:S(2)}, u32[]{:S(2)}) collective-permute-start(bf16[1024,128]{1,0:T(8,128)(2,1)} %refs_1_.1), channel_id=1, source_target_pairs={{0,1},{1,0},{2,3},{3,2},{4,5},{5,4},{6,7},{7,6},{8,9},{9,8},{10,11... | collective-permute-start | bytes 786440 | tf_op jit(solution)/shard_map/ppermute | solution.py:266
  0.5 0.0 collective-permute-start.2
  0.5 3.0 %collective-permute-start.3 = (bf16[1024,128]{1,0:T(8,128)(2,1)}, bf16[1024,128]{1,0:T(8,128)(2,1)S(1)}, u32[]{:S(2)}, u32[]{:S(2)}) collective-permute-start(bf16[1024,128]{1,0:T(8,128)(2,1)} %refs_1_.1), channel_id=1, source_target_pairs={{0,2},{1,3},{2,0},{3,1},{4,6},{5,7},{6,4},{7,5},{8,10},{9,11},{10,... | collective-permute-start | bytes 786440 | tf_op jit(solution)/shard_map/ppermute | solution.py:266
  3.5 1.6 %collective-permute-start = (bf16[512,128]{1,0:T(8,128)(2,1)}, bf16[512,128]{1,0:T(8,128)(2,1)S(1)}, u32[]{:S(2)}, u32[]{:S(2)}) collective-permute-start(bf16[512,128]{1,0:T(8,128)(2,1)} %bitcast.6), channel_id=1, source_target_pairs={{0,4},{1,5},{2,6},{3,7},{4,0},{5,1},{6,2},{7,3},{8,12},{9,13},{10,... | collective-permute-start | bytes 393224 | tf_op jit(solution)/shard_map/ppermute | solution.py:266
  5.1 0.5 %collective-permute-start.5 = (bf16[1024,128]{1,0:T(8,128)(2,1)}, bf16[1024,128]{1,0:T(8,128)(2,1)S(1)}, u32[]{:S(2)}, u32[]{:S(2)}) collective-permute-start(bf16[1024,128]{1,0:T(8,128)(2,1)} %refs_2_.1), channel_id=1, source_target_pairs={{0,2},{1,3},{2,0},{3,1},{4,6},{5,7},{6,4},{7,5},{8,10},{9,11},{10,... | collective-permute-start | bytes 786440 | tf_op jit(solution)/shard_map/ppermute | solution.py:266
  5.6 3.3 %collective-permute-done.refs_1_.q_ref = bf16[512,128]{1,0:T(8,128)(2,1)S(1)} collective-permute-done((bf16[512,128]{1,0:T(8,128)(2,1)}, bf16[512,128]{1,0:T(8,128)(2,1)S(1)}, u32[]{:S(2)}, u32[]{:S(2)}) %collective-permute-start) | collective-permute-done | bytes 131104 | tf_op jit(solution)/shard_map/ppermute | solution.py:266
  8.8 2.6 %collective-permute-start.4 = (bf16[512,128]{1,0:T(8,128)(2,1)}, bf16[512,128]{1,0:T(8,128)(2,1)S(1)}, u32[]{:S(2)}, u32[]{:S(2)}) collective-permute-start(bf16[512,128]{1,0:T(8,128)(2,1)} %bitcast.7), channel_id=1, source_target_pairs={{0,8},{1,9},{2,10},{3,11},{4,12},{5,13},{6,14},{7,15},{8,0},{9,1},... | collective-permute-start | bytes 393224 | tf_op jit(solution)/shard_map/ppermute | solution.py:266
  12.1 0.0 copy-start
  12.1 0.7 %copy-done = s32[512]{0:T(512)S(1)} copy-done((s32[512]{0:T(512)S(1)}, s32[512]{0:T(512)}, u32[]{:S(2)}) %copy-start) | copy-done | bytes 2072
  12.8 1.2 %setup.1 = (s32[4,512]{1,0:T(4,128)S(1)}, bf16[512,128]{1,0:T(8,128)(2,1)S(1)}, bf16[1024,128]{1,0:T(8,128)(2,1)S(1)}, bf16[1024,128]{1,0:T(8,128)(2,1)S(1)}) custom-call(s32[4,128]{1,0:T(4,128)S(1)} %bitcast.5, s32[1,1]{1,0:T(1,128)} %bitcast.4.span_ref, bf16[512,128]{1,0:T(8,128)(2,1)} %bitcast.8, bf16[1024,128]{1,0:T(8,128)(2,1)} %refs_1_.1, ...), custom_call_target="tpu_custom_call" | custom-call | tf_op jit(solution)/shard_map/setup/pallas_call | solution.py:351
  13.9 0.0 collective-permute-done.1.refs_4_
  14.0 0.0 collective-permute-done.2.refs_5_
  14.0 1.5 %shard_map.55 = (f32[1,512]{1,0:T(1,128)S(1)}, f32[1,512]{1,0:T(1,128)S(1)}, f32[128,512]{1,0:T(8,128)S(1)}) custom-call(s32[4,512]{1,0:T(4,128)S(1)} %get-tuple-element.143.refs_0_.limits_ref, bf16[512,128]{1,0:T(8,128)(2,1)S(1)} %collective-permute-done.refs_1_.q_ref, bf16[1024,128]{1,0:T(8,128)(2,1)S(1)} %get-tuple-element.80.refs_2_, ...), custom_call_target="tpu_custom_call" | custom-call | tf_op jit(solution)/shard_map/pallas_call | solution.py:318
  15.5 0.0 collective-permute-done.3.refs_0_.refs_6_
  15.5 0.1 collective-permute-start.6
  15.6 0.8 %shard_map.56 = (bf16[1024,512]{1,0:T(8,128)(2,1)S(1)}, f32[1,512]{1,0:T(1,128)S(1)}) custom-call(s32[4,512]{1,0:T(4,128)S(1)} %get-tuple-element.143.refs_0_.limits_ref, bf16[512,128]{1,0:T(8,128)(2,1)S(1)} %collective-permute-done.refs_1_.q_ref, bf16[1024,128]{1,0:T(8,128)(2,1)S(1)} %collective-permute-done.3.refs_0_.refs_6_), custom_call_target="tpu_custom_call" | custom-call | tf_op jit(solution)/shard_map/pallas_call | solution.py:366
  16.4 0.7 %collective-permute-done.4.refs_1_.q_ref = bf16[512,128]{1,0:T(8,128)(2,1)S(1)} collective-permute-done((bf16[512,128]{1,0:T(8,128)(2,1)}, bf16[512,128]{1,0:T(8,128)(2,1)S(1)}, u32[]{:S(2)}, u32[]{:S(2)}) %collective-permute-start.4) | collective-permute-done | bytes 131104 | tf_op jit(solution)/shard_map/ppermute | solution.py:266
  17.0 1.5 %shard_map.57 = (f32[1,512]{1,0:T(1,128)S(1)}, f32[1,512]{1,0:T(1,128)S(1)}, f32[128,512]{1,0:T(8,128)S(1)}) custom-call(s32[4,512]{1,0:T(4,128)S(1)} %get-tuple-element.143.refs_0_.limits_ref, bf16[512,128]{1,0:T(8,128)(2,1)S(1)} %collective-permute-done.4.refs_1_.q_ref, bf16[1024,128]{1,0:T(8,128)(2,1)S(1)} %get-tuple-element.80.refs_2_, ...), custom_call_target="tpu_custom_call" | custom-call | tf_op jit(solution)/shard_map/pallas_call | solution.py:318
  18.6 0.8 %shard_map.58 = (bf16[1024,512]{1,0:T(8,128)(2,1)S(1)}, f32[1,512]{1,0:T(1,128)S(1)}) custom-call(s32[4,512]{1,0:T(4,128)S(1)} %get-tuple-element.143.refs_0_.limits_ref, bf16[512,128]{1,0:T(8,128)(2,1)S(1)} %collective-permute-done.4.refs_1_.q_ref, bf16[1024,128]{1,0:T(8,128)(2,1)S(1)} %collective-permute-done.3.refs_0_.refs_6_), custom_call_target="tpu_custom_call" | custom-call | tf_op jit(solution)/shard_map/pallas_call | solution.py:366
  19.4 0.0 collective-permute-done.5.refs_0_.refs_7_
  19.4 0.1 collective-permute-start.7
  19.4 0.4 shard_map.59
  19.8 0.0 collective-permute-done.6.refs_0_.refs_2_.refs_8_
  19.8 0.8 %shard_map.60 = (bf16[1024,512]{1,0:T(8,128)(2,1)S(1)}, f32[1,512]{1,0:T(1,128)S(1)}) custom-call(s32[4,512]{1,0:T(4,128)S(1)} %get-tuple-element.143.refs_0_.limits_ref, bf16[512,128]{1,0:T(8,128)(2,1)S(1)} %collective-permute-done.4.refs_1_.q_ref, bf16[1024,128]{1,0:T(8,128)(2,1)S(1)} %collective-permute-done.6.refs_0_.refs_2_.refs_8_), custom_call_target="tpu_custom_call" | custom-call | tf_op jit(solution)/shard_map/pallas_call | solution.py:366
  20.6 0.4 collective-permute-done.7.refs_0_.refs_3_.refs_9_
  21.0 0.5 %shard_map.61 = bf16[136,512]{1,0:T(8,128)(2,1)S(1)} custom-call(bf16[1024,128]{1,0:T(8,128)(2,1)S(1)} %collective-permute-done.7.refs_0_.refs_3_.refs_9_, bf16[1024,512]{1,0:T(8,128)(2,1)S(1)} %get-tuple-element.115.refs_1_, f32[1,512]{1,0:T(1,128)S(1)} %get-tuple-element.116.refs_2_, f32[1,512]{1,0:T(1,128)S(1)} %get-tuple-element.117.refs_3_, ...), custom_call_target="tpu_custom_call" | custom-call | tf_op jit(solution)/shard_map/pallas_call | solution.py:391
  21.5 1.1 %collective-permute-start.9 = (bf16[136,512]{1,0:T(8,128)(2,1)S(1)}, bf16[136,512]{1,0:T(8,128)(2,1)S(1)}, u32[]{:S(2)}, u32[]{:S(2)}) collective-permute-start(bf16[136,512]{1,0:T(8,128)(2,1)S(1)} %shard_map.61), channel_id=1, source_target_pairs={{0,4},{1,5},{2,6},{3,7},{4,0},{5,1},{6,2},{7,3},{8,12},{9,13},{10,... | collective-permute-start | bytes 417800 | tf_op jit(solution)/shard_map/ppermute | solution.py:266
  22.6 1.0 %collective-permute-start.8 = (bf16[512,128]{1,0:T(8,128)(2,1)S(1)}, bf16[512,128]{1,0:T(8,128)(2,1)S(1)}, u32[]{:S(2)}, u32[]{:S(2)}) collective-permute-start(bf16[512,128]{1,0:T(8,128)(2,1)S(1)} %collective-permute-done.4.refs_1_.q_ref), channel_id=1, source_target_pairs={{0,4},{1,5},{2,6},{3,7},{4,0},{5,1},{6,2},{7,3},{8,12},{9,13},{10,... | collective-permute-start | bytes 393224 | tf_op jit(solution)/shard_map/ppermute | solution.py:266
  23.6 0.4 shard_map.62
  23.9 1.0 %shard_map.63 = bf16[136,512]{1,0:T(8,128)(2,1)S(1)} custom-call(s32[4,512]{1,0:T(4,128)S(1)} %get-tuple-element.143.refs_0_.limits_ref, bf16[512,128]{1,0:T(8,128)(2,1)S(1)} %collective-permute-done.refs_1_.q_ref, bf16[1024,128]{1,0:T(8,128)(2,1)S(1)} %collective-permute-done.6.refs_0_.refs_2_.refs_8_, ...), custom_call_target="tpu_custom_call" | custom-call | tf_op jit(solution)/shard_map/pallas_call | solution.py:318
  24.9 5.1 %collective-permute-done.8.refs_1_ = bf16[512,128]{1,0:T(8,128)(2,1)S(1)} collective-permute-done((bf16[512,128]{1,0:T(8,128)(2,1)S(1)}, bf16[512,128]{1,0:T(8,128)(2,1)S(1)}, u32[]{:S(2)}, u32[]{:S(2)}) %collective-permute-start.8) | collective-permute-done | bytes 131104 | tf_op jit(solution)/shard_map/ppermute | solution.py:266
  30.1 2.9 %shard_map.64 = (f32[128,512]{1,0:T(8,128)S(1)}, f32[1,512]{1,0:T(1,128)S(1)}) custom-call(s32[4,512]{1,0:T(4,128)S(1)} %get-tuple-element.143.refs_0_.limits_ref, bf16[512,128]{1,0:T(8,128)(2,1)S(1)} %collective-permute-done.8.refs_1_, bf16[1024,128]{1,0:T(8,128)(2,1)S(1)} %get-tuple-element.80.refs_2_, bf16[1024,128]{1,0:T(8,128)(2,1)S(1)} %get-tuple-element.81.refs_3_, ...), custom_call_target="tpu_custom_call" | custom-call | tf_op jit(solution)/shard_map/pallas_call | solution.py:318
  32.9 1.3 %collective-permute-start.10 = (bf16[136,512]{1,0:T(8,128)(2,1)S(1)}, bf16[136,512]{1,0:T(8,128)(2,1)S(1)}, u32[]{:S(2)}, u32[]{:S(2)}) collective-permute-start(bf16[136,512]{1,0:T(8,128)(2,1)S(1)} %shard_map.63), channel_id=1, source_target_pairs={{0,4},{1,5},{2,6},{3,7},{4,0},{5,1},{6,2},{7,3},{8,12},{9,13},{10,... | collective-permute-start | bytes 417800 | tf_op jit(solution)/shard_map/ppermute | solution.py:266
  34.2 0.0 collective-permute-done.9.part_ref
  34.2 0.3 shard_map.65
  34.5 2.6 %collective-permute-start.11 = (bf16[136,512]{1,0:T(8,128)(2,1)S(1)}, bf16[136,512]{1,0:T(8,128)(2,1)S(1)}, u32[]{:S(2)}, u32[]{:S(2)}) collective-permute-start(bf16[136,512]{1,0:T(8,128)(2,1)S(1)} %shard_map.65), channel_id=1, source_target_pairs={{0,12},{1,13},{2,14},{3,15},{4,8},{5,9},{6,10},{7,11},{8,4},{9,5},... | collective-permute-start | bytes 417800 | tf_op jit(solution)/shard_map/ppermute | solution.py:266
  37.1 2.8 %shard_map.66 = (f32[128,512]{1,0:T(8,128)S(1)}, f32[1,512]{1,0:T(1,128)S(1)}) custom-call(s32[4,512]{1,0:T(4,128)S(1)} %get-tuple-element.143.refs_0_.limits_ref, bf16[512,128]{1,0:T(8,128)(2,1)S(1)} %get-tuple-element.144.refs_1_, bf16[1024,128]{1,0:T(8,128)(2,1)S(1)} %get-tuple-element.80.refs_2_, bf16[1024,128]{1,0:T(8,128)(2,1)S(1)} %get-tuple-element.81.refs_3_, ...), custom_call_target="tpu_custom_call" | custom-call | tf_op jit(solution)/shard_map/pallas_call | solution.py:318
  39.9 0.0 collective-permute-done.10.part_ref
  39.9 0.1 shard_map.67
  40.0 2.9 %collective-permute-done.11.refs_2_ = bf16[136,512]{1,0:T(8,128)(2,1)S(1)} collective-permute-done((bf16[136,512]{1,0:T(8,128)(2,1)S(1)}, bf16[136,512]{1,0:T(8,128)(2,1)S(1)}, u32[]{:S(2)}, u32[]{:S(2)}) %collective-permute-start.11) | collective-permute-done | bytes 139296 | tf_op jit(solution)/shard_map/ppermute | solution.py:266
  42.9 0.8 %merge.1 = bf16[512,128]{1,0:T(8,128)(2,1)} custom-call(f32[128,512]{1,0:T(8,128)S(1)} %get-tuple-element.150.refs_0_, f32[1,512]{1,0:T(1,128)S(1)} %get-tuple-element.151.refs_1_, bf16[136,512]{1,0:T(8,128)(2,1)S(1)} %collective-permute-done.11.refs_2_), custom_call_target="tpu_custom_call" | custom-call | tf_op jit(solution)/shard_map/merge/pallas_call | solution.py:452
Async XLA Ops:
  0.0 13.9 %collective-permute-start.1 = (bf16[1024,128]{1,0:T(8,128)(2,1)}, bf16[1024,128]{1,0:T(8,128)(2,1)S(1)}, u32[]{:S(2)}, u32[]{:S(2)}) collective-permute-start(bf16[1024,128]{1,0:T(8,128)(2,1)} %refs_1_.1), channel_id=1, source_target_pairs={{0,1},{1,0},{2,3},{3,2},{4,5},{5,4},{6,7},{7,6},{8,9},{9,8},{10,11... | collective-permute-start | bytes 786440 | tf_op jit(solution)/shard_map/ppermute | solution.py:266
  0.5 13.5 %collective-permute-start.2 = (bf16[1024,128]{1,0:T(8,128)(2,1)}, bf16[1024,128]{1,0:T(8,128)(2,1)S(1)}, u32[]{:S(2)}, u32[]{:S(2)}) collective-permute-start(bf16[1024,128]{1,0:T(8,128)(2,1)} %refs_2_.1), channel_id=1, source_target_pairs={{0,1},{1,0},{2,3},{3,2},{4,5},{5,4},{6,7},{7,6},{8,9},{9,8},{10,11... | collective-permute-start | bytes 786440 | tf_op jit(solution)/shard_map/ppermute | solution.py:266
  0.5 15.0 %collective-permute-start.3 = (bf16[1024,128]{1,0:T(8,128)(2,1)}, bf16[1024,128]{1,0:T(8,128)(2,1)S(1)}, u32[]{:S(2)}, u32[]{:S(2)}) collective-permute-start(bf16[1024,128]{1,0:T(8,128)(2,1)} %refs_1_.1), channel_id=1, source_target_pairs={{0,2},{1,3},{2,0},{3,1},{4,6},{5,7},{6,4},{7,5},{8,10},{9,11},{10,... | collective-permute-start | bytes 786440 | tf_op jit(solution)/shard_map/ppermute | solution.py:266
  3.5 5.3 %collective-permute-start = (bf16[512,128]{1,0:T(8,128)(2,1)}, bf16[512,128]{1,0:T(8,128)(2,1)S(1)}, u32[]{:S(2)}, u32[]{:S(2)}) collective-permute-start(bf16[512,128]{1,0:T(8,128)(2,1)} %bitcast.6), channel_id=1, source_target_pairs={{0,4},{1,5},{2,6},{3,7},{4,0},{5,1},{6,2},{7,3},{8,12},{9,13},{10,... | collective-permute-start | bytes 393224 | tf_op jit(solution)/shard_map/ppermute | solution.py:266
  5.1 14.3 %collective-permute-start.5 = (bf16[1024,128]{1,0:T(8,128)(2,1)}, bf16[1024,128]{1,0:T(8,128)(2,1)S(1)}, u32[]{:S(2)}, u32[]{:S(2)}) collective-permute-start(bf16[1024,128]{1,0:T(8,128)(2,1)} %refs_2_.1), channel_id=1, source_target_pairs={{0,2},{1,3},{2,0},{3,1},{4,6},{5,7},{6,4},{7,5},{8,10},{9,11},{10,... | collective-permute-start | bytes 786440 | tf_op jit(solution)/shard_map/ppermute | solution.py:266
  8.8 8.2 %collective-permute-start.4 = (bf16[512,128]{1,0:T(8,128)(2,1)}, bf16[512,128]{1,0:T(8,128)(2,1)S(1)}, u32[]{:S(2)}, u32[]{:S(2)}) collective-permute-start(bf16[512,128]{1,0:T(8,128)(2,1)} %bitcast.7), channel_id=1, source_target_pairs={{0,8},{1,9},{2,10},{3,11},{4,12},{5,13},{6,14},{7,15},{8,0},{9,1},... | collective-permute-start | bytes 393224 | tf_op jit(solution)/shard_map/ppermute | solution.py:266
  12.1 0.7 %copy-start = (s32[512]{0:T(512)S(1)}, s32[512]{0:T(512)}, u32[]{:S(2)}) copy-start(s32[512]{0:T(512)} %param.9) | copy-start | bytes 6148
  15.5 4.3 %collective-permute-start.6 = (bf16[1024,128]{1,0:T(8,128)(2,1)S(1)}, bf16[1024,128]{1,0:T(8,128)(2,1)S(1)}, u32[]{:S(2)}, u32[]{:S(2)}) collective-permute-start(bf16[1024,128]{1,0:T(8,128)(2,1)S(1)} %collective-permute-done.3.refs_0_.refs_6_), channel_id=1, source_target_pairs={{0,1},{1,0},{2,3},{3,2},{4,5},{5,4},{6,7},{7,6},{8,9},{9,8},{10,11... | collective-permute-start | bytes 786440 | tf_op jit(solution)/shard_map/ppermute | solution.py:266
  19.4 1.6 %collective-permute-start.7 = (bf16[1024,128]{1,0:T(8,128)(2,1)S(1)}, bf16[1024,128]{1,0:T(8,128)(2,1)S(1)}, u32[]{:S(2)}, u32[]{:S(2)}) collective-permute-start(bf16[1024,128]{1,0:T(8,128)(2,1)S(1)} %collective-permute-done.5.refs_0_.refs_7_), channel_id=1, source_target_pairs={{0,1},{1,0},{2,3},{3,2},{4,5},{5,4},{6,7},{7,6},{8,9},{9,8},{10,11... | collective-permute-start | bytes 786440 | tf_op jit(solution)/shard_map/ppermute | solution.py:266
  21.5 12.8 %collective-permute-start.9 = (bf16[136,512]{1,0:T(8,128)(2,1)S(1)}, bf16[136,512]{1,0:T(8,128)(2,1)S(1)}, u32[]{:S(2)}, u32[]{:S(2)}) collective-permute-start(bf16[136,512]{1,0:T(8,128)(2,1)S(1)} %shard_map.61), channel_id=1, source_target_pairs={{0,4},{1,5},{2,6},{3,7},{4,0},{5,1},{6,2},{7,3},{8,12},{9,13},{10,... | collective-permute-start | bytes 417800 | tf_op jit(solution)/shard_map/ppermute | solution.py:266
  22.6 7.5 %collective-permute-start.8 = (bf16[512,128]{1,0:T(8,128)(2,1)S(1)}, bf16[512,128]{1,0:T(8,128)(2,1)S(1)}, u32[]{:S(2)}, u32[]{:S(2)}) collective-permute-start(bf16[512,128]{1,0:T(8,128)(2,1)S(1)} %collective-permute-done.4.refs_1_.q_ref), channel_id=1, source_target_pairs={{0,4},{1,5},{2,6},{3,7},{4,0},{5,1},{6,2},{7,3},{8,12},{9,13},{10,... | collective-permute-start | bytes 393224 | tf_op jit(solution)/shard_map/ppermute | solution.py:266
  32.9 7.0 %collective-permute-start.10 = (bf16[136,512]{1,0:T(8,128)(2,1)S(1)}, bf16[136,512]{1,0:T(8,128)(2,1)S(1)}, u32[]{:S(2)}, u32[]{:S(2)}) collective-permute-start(bf16[136,512]{1,0:T(8,128)(2,1)S(1)} %shard_map.63), channel_id=1, source_target_pairs={{0,4},{1,5},{2,6},{3,7},{4,0},{5,1},{6,2},{7,3},{8,12},{9,13},{10,... | collective-permute-start | bytes 417800 | tf_op jit(solution)/shard_map/ppermute | solution.py:266
  34.5 8.4 %collective-permute-start.11 = (bf16[136,512]{1,0:T(8,128)(2,1)S(1)}, bf16[136,512]{1,0:T(8,128)(2,1)S(1)}, u32[]{:S(2)}, u32[]{:S(2)}) collective-permute-start(bf16[136,512]{1,0:T(8,128)(2,1)S(1)} %shard_map.65), channel_id=1, source_target_pairs={{0,12},{1,13},{2,14},{3,15},{4,8},{5,9},{6,10},{7,11},{8,4},{9,5},... | collective-permute-start | bytes 417800 | tf_op jit(solution)/shard_map/ppermute | solution.py:266

commit v11 on v10

--- a/solution.py
+++ b/solution.py
@@ -375,8 +375,6 @@
 
     far_pair[0], = hold(far_pair[0])
     across_keys = swap(far_pair[0], 1)
-    if outer == 4:
-        first_weights = weigh(1, 2, far_pair[0])
     source = stages[last][0] ^ (stages[last][0] & -stages[last][0])
     (got[source],) = hold(got[source])
     gather(last)
@@ -425,8 +423,7 @@
 
     if outer == 4:
         handed = swap(packed, inner)
-        states[1] = finish(1, far_pair[1], *first_weights, None, state_shapes)
-        (packed,) = attend(1, [3], whole_plan, coded)
+        (packed,) = attend(1, [2, 3], whole_plan, coded)
         parts.append(swap(packed, inner))
         value, level = attend(3, [0, 1, 2, 3], own_plan, float_shapes(stage_rows))
         (handed,) = hold(handed)

time: 44 us -> 44.6 us (1.014)
  waiting for transfers between devices: 12.3 us -> 13 us
  Pallas kernels: 15.7 us -> 15.1 us
  starting transfers between devices: 14.3 us -> 14.8 us
    pallas_call x3 -> x2, Pallas kernels: 2.32 us -> 1.52 us  [weigh(): pl.pallas_call(functools.partial(weigh_kernel, scale, index, [block_index...]
    ppermute x12, waiting for transfers between devices: 12.3 us -> 13 us  [swap(): return lax.ppermute(array, 'ctx', [(i, i ^ step) for i in range(size)])]
    pallas_call x5, Pallas kernels: 9.78 us -> 10.4 us  [attend(): pl.pallas_call(functools.partial(attend_kernel, scale, index, blocks, sta...]
    ppermute x12, starting transfers between devices: 14.3 us -> 14.8 us  [swap(): return lax.ppermute(array, 'ctx', [(i, i ^ step) for i in range(size)])]
    pallas_call x3 -> x2, Pallas kernels: 1.21 us -> 0.86 us  [finish(): pl.pallas_call(functools.partial(finish_kernel, 1, plan), in_specs=[vmem]...]
  transfers between devices with their start and end apart: 12 -> 12, of which waited for: 5 -> 4; matrix products, arithmetic and copies ran while one was open for 0% -> 0% of each run, Pallas kernels for 33% -> 31%
where the time goes in v11:
time: 44.6 us; the launch traced here: 44.5 us
  Pallas kernels  15.1 us (34%)
  starting transfers between devices  14.8 us (33%)
  waiting for transfers between devices  13 us (29%)
  between operations  0.81 us (2%)
  local copies, waits for them, and re-layouts  0.67 us (2%)
    ppermute x12, starting transfers between devices, swap(): return lax.ppermute(array, 'ctx', [(i, i ^ step) for i in range(size)])  14.8 us
    ppermute x12, waiting for transfers between devices, swap(): return lax.ppermute(array, 'ctx', [(i, i ^ step) for i in range(size)])  13 us
    pallas_call x5, Pallas kernels, attend(): pl.pallas_call(functools.partial(attend_kernel, scale, index, blocks, sta...  10.4 us
    pallas_call x2, Pallas kernels, weigh(): pl.pallas_call(functools.partial(weigh_kernel, scale, index, [block_index...  1.52 us
    pallas_call x1, Pallas kernels, local(): pl.pallas_call(functools.partial(setup_kernel, own_tokens, head_count), i...  1.17 us
  transfers between devices with their start and end apart: 12, of which 4 were waited for; matrix products, arithmetic and copies ran while one was open for 0% of the time, Pallas kernels for 31%

profile of v11, /device:TPU:0, one launch (start us, length us, event | category | flops | bytes accessed | tf_op | source)
XLA Modules:
  0.0 44.5 jit_solution(198577010051531465)
XLA Ops:
  0.0 0.5 %collective-permute-start.1 = (bf16[1024,128]{1,0:T(8,128)(2,1)}, bf16[1024,128]{1,0:T(8,128)(2,1)S(1)}, u32[]{:S(2)}, u32[]{:S(2)}) collective-permute-start(bf16[1024,128]{1,0:T(8,128)(2,1)} %refs_1_.1), channel_id=1, source_target_pairs={{0,1},{1,0},{2,3},{3,2},{4,5},{5,4},{6,7},{7,6},{8,9},{9,8},{10,11... | collective-permute-start | bytes 786440 | tf_op jit(solution)/shard_map/ppermute | solution.py:266
  0.5 0.0 collective-permute-start.2
  0.5 3.0 %collective-permute-start.3 = (bf16[1024,128]{1,0:T(8,128)(2,1)}, bf16[1024,128]{1,0:T(8,128)(2,1)S(1)}, u32[]{:S(2)}, u32[]{:S(2)}) collective-permute-start(bf16[1024,128]{1,0:T(8,128)(2,1)} %refs_1_.1), channel_id=1, source_target_pairs={{0,2},{1,3},{2,0},{3,1},{4,6},{5,7},{6,4},{7,5},{8,10},{9,11},{10,... | collective-permute-start | bytes 786440 | tf_op jit(solution)/shard_map/ppermute | solution.py:266
  3.5 1.6 %collective-permute-start = (bf16[512,128]{1,0:T(8,128)(2,1)}, bf16[512,128]{1,0:T(8,128)(2,1)S(1)}, u32[]{:S(2)}, u32[]{:S(2)}) collective-permute-start(bf16[512,128]{1,0:T(8,128)(2,1)} %bitcast.6), channel_id=1, source_target_pairs={{0,4},{1,5},{2,6},{3,7},{4,0},{5,1},{6,2},{7,3},{8,12},{9,13},{10,... | collective-permute-start | bytes 393224 | tf_op jit(solution)/shard_map/ppermute | solution.py:266
  5.1 0.5 %collective-permute-start.5 = (bf16[1024,128]{1,0:T(8,128)(2,1)}, bf16[1024,128]{1,0:T(8,128)(2,1)S(1)}, u32[]{:S(2)}, u32[]{:S(2)}) collective-permute-start(bf16[1024,128]{1,0:T(8,128)(2,1)} %refs_2_.1), channel_id=1, source_target_pairs={{0,2},{1,3},{2,0},{3,1},{4,6},{5,7},{6,4},{7,5},{8,10},{9,11},{10,... | collective-permute-start | bytes 786440 | tf_op jit(solution)/shard_map/ppermute | solution.py:266
  5.6 3.3 %collective-permute-done.refs_1_ = bf16[512,128]{1,0:T(8,128)(2,1)S(1)} collective-permute-done((bf16[512,128]{1,0:T(8,128)(2,1)}, bf16[512,128]{1,0:T(8,128)(2,1)S(1)}, u32[]{:S(2)}, u32[]{:S(2)}) %collective-permute-start) | collective-permute-done | bytes 131104 | tf_op jit(solution)/shard_map/ppermute | solution.py:266
  8.8 2.6 %collective-permute-start.4 = (bf16[512,128]{1,0:T(8,128)(2,1)}, bf16[512,128]{1,0:T(8,128)(2,1)S(1)}, u32[]{:S(2)}, u32[]{:S(2)}) collective-permute-start(bf16[512,128]{1,0:T(8,128)(2,1)} %bitcast.7), channel_id=1, source_target_pairs={{0,8},{1,9},{2,10},{3,11},{4,12},{5,13},{6,14},{7,15},{8,0},{9,1},... | collective-permute-start | bytes 393224 | tf_op jit(solution)/shard_map/ppermute | solution.py:266
  12.1 0.0 copy-start
  12.1 0.7 %copy-done = s32[512]{0:T(512)S(1)} copy-done((s32[512]{0:T(512)S(1)}, s32[512]{0:T(512)}, u32[]{:S(2)}) %copy-start) | copy-done | bytes 2072
  12.8 1.2 %setup.1 = (s32[4,512]{1,0:T(4,128)S(1)}, bf16[512,128]{1,0:T(8,128)(2,1)S(1)}, bf16[1024,128]{1,0:T(8,128)(2,1)S(1)}, bf16[1024,128]{1,0:T(8,128)(2,1)S(1)}) custom-call(s32[4,128]{1,0:T(4,128)S(1)} %bitcast.5, s32[1,1]{1,0:T(1,128)} %bitcast.4.span_ref, bf16[512,128]{1,0:T(8,128)(2,1)} %bitcast.8, bf16[1024,128]{1,0:T(8,128)(2,1)} %refs_1_.1, ...), custom_call_target="tpu_custom_call" | custom-call | tf_op jit(solution)/shard_map/setup/pallas_call | solution.py:351
  13.9 0.0 collective-permute-done.1.refs_4_
  14.0 0.0 collective-permute-done.2.refs_5_
  14.0 1.5 %shard_map.55 = (f32[1,512]{1,0:T(1,128)S(1)}, f32[1,512]{1,0:T(1,128)S(1)}, f32[128,512]{1,0:T(8,128)S(1)}) custom-call(s32[4,512]{1,0:T(4,128)S(1)} %get-tuple-element.119.refs_0_.limits_ref, bf16[512,128]{1,0:T(8,128)(2,1)S(1)} %collective-permute-done.refs_1_, bf16[1024,128]{1,0:T(8,128)(2,1)S(1)} %get-tuple-element.68.refs_2_, ...), custom_call_target="tpu_custom_call" | custom-call | tf_op jit(solution)/shard_map/pallas_call | solution.py:318
  15.5 0.0 collective-permute-done.3.refs_0_.refs_2_.refs_6_
  15.5 1.5 %collective-permute-done.4.refs_1_.q_ref = bf16[512,128]{1,0:T(8,128)(2,1)S(1)} collective-permute-done((bf16[512,128]{1,0:T(8,128)(2,1)}, bf16[512,128]{1,0:T(8,128)(2,1)S(1)}, u32[]{:S(2)}, u32[]{:S(2)}) %collective-permute-start.4) | collective-permute-done | bytes 131104 | tf_op jit(solution)/shard_map/ppermute | solution.py:266
  17.0 1.5 %shard_map.56 = (f32[1,512]{1,0:T(1,128)S(1)}, f32[1,512]{1,0:T(1,128)S(1)}, f32[128,512]{1,0:T(8,128)S(1)}) custom-call(s32[4,512]{1,0:T(4,128)S(1)} %get-tuple-element.119.refs_0_.limits_ref, bf16[512,128]{1,0:T(8,128)(2,1)S(1)} %collective-permute-done.4.refs_1_.q_ref, bf16[1024,128]{1,0:T(8,128)(2,1)S(1)} %get-tuple-element.68.refs_2_, ...), custom_call_target="tpu_custom_call" | custom-call | tf_op jit(solution)/shard_map/pallas_call | solution.py:318
  18.6 0.1 collective-permute-start.6
  18.6 0.8 %shard_map.57 = (bf16[1024,512]{1,0:T(8,128)(2,1)S(1)}, f32[1,512]{1,0:T(1,128)S(1)}) custom-call(s32[4,512]{1,0:T(4,128)S(1)} %get-tuple-element.119.refs_0_.limits_ref, bf16[512,128]{1,0:T(8,128)(2,1)S(1)} %collective-permute-done.4.refs_1_.q_ref, bf16[1024,128]{1,0:T(8,128)(2,1)S(1)} %collective-permute-done.3.refs_0_.refs_2_.refs_6_), custom_call_target="tpu_custom_call" | custom-call | tf_op jit(solution)/shard_map/pallas_call | solution.py:366
  19.4 0.0 collective-permute-done.5.refs_0_.refs_3_.refs_7_
  19.4 0.6 %collective-permute-start.7 = (bf16[1024,128]{1,0:T(8,128)(2,1)S(1)}, bf16[1024,128]{1,0:T(8,128)(2,1)S(1)}, u32[]{:S(2)}, u32[]{:S(2)}) collective-permute-start(bf16[1024,128]{1,0:T(8,128)(2,1)S(1)} %collective-permute-done.5.refs_0_.refs_3_.refs_7_), channel_id=1, source_target_pairs={{0,1},{1,0},{2,3},{3,2},{4,5},{5,4},{6,7},{7,6},{8,9},{9,8},{10,11... | collective-permute-start | bytes 786440 | tf_op jit(solution)/shard_map/ppermute | solution.py:266
  20.0 0.4 shard_map.58
  20.4 0.0 collective-permute-done.6.refs_0_.refs_4_.refs_8_
  20.4 0.8 %shard_map.59 = (bf16[1024,512]{1,0:T(8,128)(2,1)S(1)}, f32[1,512]{1,0:T(1,128)S(1)}) custom-call(s32[4,512]{1,0:T(4,128)S(1)} %get-tuple-element.119.refs_0_.limits_ref, bf16[512,128]{1,0:T(8,128)(2,1)S(1)} %collective-permute-done.4.refs_1_.q_ref, bf16[1024,128]{1,0:T(8,128)(2,1)S(1)} %collective-permute-done.6.refs_0_.refs_4_.refs_8_), custom_call_target="tpu_custom_call" | custom-call | tf_op jit(solution)/shard_map/pallas_call | solution.py:366
  21.1 0.0 collective-permute-done.7.refs_0_.refs_5_.refs_9_
  21.1 0.5 %shard_map.60 = bf16[136,512]{1,0:T(8,128)(2,1)S(1)} custom-call(bf16[1024,128]{1,0:T(8,128)(2,1)S(1)} %collective-permute-done.7.refs_0_.refs_5_.refs_9_, bf16[1024,512]{1,0:T(8,128)(2,1)S(1)} %get-tuple-element.100.refs_1_, f32[1,512]{1,0:T(1,128)S(1)} %get-tuple-element.101.refs_2_, f32[1,512]{1,0:T(1,128)S(1)} %get-tuple-element.102.refs_3_, ...), custom_call_target="tpu_custom_call" | custom-call | tf_op jit(solution)/shard_map/pallas_call | solution.py:389
  21.6 0.8 %collective-permute-start.9 = (bf16[136,512]{1,0:T(8,128)(2,1)S(1)}, bf16[136,512]{1,0:T(8,128)(2,1)S(1)}, u32[]{:S(2)}, u32[]{:S(2)}) collective-permute-start(bf16[136,512]{1,0:T(8,128)(2,1)S(1)} %shard_map.60), channel_id=1, source_target_pairs={{0,4},{1,5},{2,6},{3,7},{4,0},{5,1},{6,2},{7,3},{8,12},{9,13},{10,... | collective-permute-start | bytes 417800 | tf_op jit(solution)/shard_map/ppermute | solution.py:266
  22.5 1.2 %collective-permute-start.8 = (bf16[512,128]{1,0:T(8,128)(2,1)S(1)}, bf16[512,128]{1,0:T(8,128)(2,1)S(1)}, u32[]{:S(2)}, u32[]{:S(2)}) collective-permute-start(bf16[512,128]{1,0:T(8,128)(2,1)S(1)} %collective-permute-done.4.refs_1_.q_ref), channel_id=1, source_target_pairs={{0,4},{1,5},{2,6},{3,7},{4,0},{5,1},{6,2},{7,3},{8,12},{9,13},{10,... | collective-permute-start | bytes 393224 | tf_op jit(solution)/shard_map/ppermute | solution.py:266
  23.7 1.6 %shard_map.61 = bf16[136,512]{1,0:T(8,128)(2,1)S(1)} custom-call(s32[4,512]{1,0:T(4,128)S(1)} %get-tuple-element.119.refs_0_.limits_ref, bf16[512,128]{1,0:T(8,128)(2,1)S(1)} %collective-permute-done.refs_1_, bf16[1024,128]{1,0:T(8,128)(2,1)S(1)} %collective-permute-done.3.refs_0_.refs_2_.refs_6_, ...), custom_call_target="tpu_custom_call" | custom-call | tf_op jit(solution)/shard_map/pallas_call | solution.py:318
  25.4 5.1 %collective-permute-done.8.refs_1_ = bf16[512,128]{1,0:T(8,128)(2,1)S(1)} collective-permute-done((bf16[512,128]{1,0:T(8,128)(2,1)S(1)}, bf16[512,128]{1,0:T(8,128)(2,1)S(1)}, u32[]{:S(2)}, u32[]{:S(2)}) %collective-permute-start.8) | collective-permute-done | bytes 131104 | tf_op jit(solution)/shard_map/ppermute | solution.py:266
  30.5 2.8 %shard_map.62 = (f32[128,512]{1,0:T(8,128)S(1)}, f32[1,512]{1,0:T(1,128)S(1)}) custom-call(s32[4,512]{1,0:T(4,128)S(1)} %get-tuple-element.119.refs_0_.limits_ref, bf16[512,128]{1,0:T(8,128)(2,1)S(1)} %collective-permute-done.8.refs_1_, bf16[1024,128]{1,0:T(8,128)(2,1)S(1)} %get-tuple-element.68.refs_2_, bf16[1024,128]{1,0:T(8,128)(2,1)S(1)} %get-tuple-element.69.refs_3_, ...), custom_call_target="tpu_custom_call" | custom-call | tf_op jit(solution)/shard_map/pallas_call | solution.py:318
  33.3 0.8 %collective-permute-start.10 = (bf16[136,512]{1,0:T(8,128)(2,1)S(1)}, bf16[136,512]{1,0:T(8,128)(2,1)S(1)}, u32[]{:S(2)}, u32[]{:S(2)}) collective-permute-start(bf16[136,512]{1,0:T(8,128)(2,1)S(1)} %shard_map.61), channel_id=1, source_target_pairs={{0,4},{1,5},{2,6},{3,7},{4,0},{5,1},{6,2},{7,3},{8,12},{9,13},{10,... | collective-permute-start | bytes 417800 | tf_op jit(solution)/shard_map/ppermute | solution.py:266
  34.2 0.0 collective-permute-done.9.part_ref
  34.2 0.3 shard_map.63
  34.4 3.1 %collective-permute-start.11 = (bf16[136,512]{1,0:T(8,128)(2,1)S(1)}, bf16[136,512]{1,0:T(8,128)(2,1)S(1)}, u32[]{:S(2)}, u32[]{:S(2)}) collective-permute-start(bf16[136,512]{1,0:T(8,128)(2,1)S(1)} %shard_map.63), channel_id=1, source_target_pairs={{0,12},{1,13},{2,14},{3,15},{4,8},{5,9},{6,10},{7,11},{8,4},{9,5},... | collective-permute-start | bytes 417800 | tf_op jit(solution)/shard_map/ppermute | solution.py:266
  37.5 2.8 %shard_map.64 = (f32[128,512]{1,0:T(8,128)S(1)}, f32[1,512]{1,0:T(1,128)S(1)}) custom-call(s32[4,512]{1,0:T(4,128)S(1)} %get-tuple-element.119.refs_0_.limits_ref, bf16[512,128]{1,0:T(8,128)(2,1)S(1)} %get-tuple-element.120.refs_1_, bf16[1024,128]{1,0:T(8,128)(2,1)S(1)} %get-tuple-element.68.refs_2_, bf16[1024,128]{1,0:T(8,128)(2,1)S(1)} %get-tuple-element.69.refs_3_, ...), custom_call_target="tpu_custom_call" | custom-call | tf_op jit(solution)/shard_map/pallas_call | solution.py:318
  40.4 0.0 collective-permute-done.10.part_ref
  40.4 0.1 shard_map.65
  40.5 3.1 %collective-permute-done.11.refs_2_ = bf16[136,512]{1,0:T(8,128)(2,1)S(1)} collective-permute-done((bf16[136,512]{1,0:T(8,128)(2,1)S(1)}, bf16[136,512]{1,0:T(8,128)(2,1)S(1)}, u32[]{:S(2)}, u32[]{:S(2)}) %collective-permute-start.11) | collective-permute-done | bytes 139296 | tf_op jit(solution)/shard_map/ppermute | solution.py:266
  43.6 0.8 %merge.1 = bf16[512,128]{1,0:T(8,128)(2,1)} custom-call(f32[128,512]{1,0:T(8,128)S(1)} %get-tuple-element.126.refs_0_, f32[1,512]{1,0:T(1,128)S(1)} %get-tuple-element.127.refs_1_, bf16[136,512]{1,0:T(8,128)(2,1)S(1)} %collective-permute-done.11.refs_2_), custom_call_target="tpu_custom_call" | custom-call | tf_op jit(solution)/shard_map/merge/pallas_call | solution.py:449
Async XLA Ops:
  0.0 13.9 %collective-permute-start.1 = (bf16[1024,128]{1,0:T(8,128)(2,1)}, bf16[1024,128]{1,0:T(8,128)(2,1)S(1)}, u32[]{:S(2)}, u32[]{:S(2)}) collective-permute-start(bf16[1024,128]{1,0:T(8,128)(2,1)} %refs_1_.1), channel_id=1, source_target_pairs={{0,1},{1,0},{2,3},{3,2},{4,5},{5,4},{6,7},{7,6},{8,9},{9,8},{10,11... | collective-permute-start | bytes 786440 | tf_op jit(solution)/shard_map/ppermute | solution.py:266
  0.5 13.5 %collective-permute-start.2 = (bf16[1024,128]{1,0:T(8,128)(2,1)}, bf16[1024,128]{1,0:T(8,128)(2,1)S(1)}, u32[]{:S(2)}, u32[]{:S(2)}) collective-permute-start(bf16[1024,128]{1,0:T(8,128)(2,1)} %refs_2_.1), channel_id=1, source_target_pairs={{0,1},{1,0},{2,3},{3,2},{4,5},{5,4},{6,7},{7,6},{8,9},{9,8},{10,11... | collective-permute-start | bytes 786440 | tf_op jit(solution)/shard_map/ppermute | solution.py:266
  0.5 15.0 %collective-permute-start.3 = (bf16[1024,128]{1,0:T(8,128)(2,1)}, bf16[1024,128]{1,0:T(8,128)(2,1)S(1)}, u32[]{:S(2)}, u32[]{:S(2)}) collective-permute-start(bf16[1024,128]{1,0:T(8,128)(2,1)} %refs_1_.1), channel_id=1, source_target_pairs={{0,2},{1,3},{2,0},{3,1},{4,6},{5,7},{6,4},{7,5},{8,10},{9,11},{10,... | collective-permute-start | bytes 786440 | tf_op jit(solution)/shard_map/ppermute | solution.py:266
  3.5 5.3 %collective-permute-start = (bf16[512,128]{1,0:T(8,128)(2,1)}, bf16[512,128]{1,0:T(8,128)(2,1)S(1)}, u32[]{:S(2)}, u32[]{:S(2)}) collective-permute-start(bf16[512,128]{1,0:T(8,128)(2,1)} %bitcast.6), channel_id=1, source_target_pairs={{0,4},{1,5},{2,6},{3,7},{4,0},{5,1},{6,2},{7,3},{8,12},{9,13},{10,... | collective-permute-start | bytes 393224 | tf_op jit(solution)/shard_map/ppermute | solution.py:266
  5.1 14.3 %collective-permute-start.5 = (bf16[1024,128]{1,0:T(8,128)(2,1)}, bf16[1024,128]{1,0:T(8,128)(2,1)S(1)}, u32[]{:S(2)}, u32[]{:S(2)}) collective-permute-start(bf16[1024,128]{1,0:T(8,128)(2,1)} %refs_2_.1), channel_id=1, source_target_pairs={{0,2},{1,3},{2,0},{3,1},{4,6},{5,7},{6,4},{7,5},{8,10},{9,11},{10,... | collective-permute-start | bytes 786440 | tf_op jit(solution)/shard_map/ppermute | solution.py:266
  8.8 8.2 %collective-permute-start.4 = (bf16[512,128]{1,0:T(8,128)(2,1)}, bf16[512,128]{1,0:T(8,128)(2,1)S(1)}, u32[]{:S(2)}, u32[]{:S(2)}) collective-permute-start(bf16[512,128]{1,0:T(8,128)(2,1)} %bitcast.7), channel_id=1, source_target_pairs={{0,8},{1,9},{2,10},{3,11},{4,12},{5,13},{6,14},{7,15},{8,0},{9,1},... | collective-permute-start | bytes 393224 | tf_op jit(solution)/shard_map/ppermute | solution.py:266
  12.1 0.7 %copy-start = (s32[512]{0:T(512)S(1)}, s32[512]{0:T(512)}, u32[]{:S(2)}) copy-start(s32[512]{0:T(512)} %param.9) | copy-start | bytes 6148
  18.6 1.8 %collective-permute-start.6 = (bf16[1024,128]{1,0:T(8,128)(2,1)S(1)}, bf16[1024,128]{1,0:T(8,128)(2,1)S(1)}, u32[]{:S(2)}, u32[]{:S(2)}) collective-permute-start(bf16[1024,128]{1,0:T(8,128)(2,1)S(1)} %collective-permute-done.3.refs_0_.refs_2_.refs_6_), channel_id=1, source_target_pairs={{0,1},{1,0},{2,3},{3,2},{4,5},{5,4},{6,7},{7,6},{8,9},{9,8},{10,11... | collective-permute-start | bytes 786440 | tf_op jit(solution)/shard_map/ppermute | solution.py:266
  19.4 1.7 %collective-permute-start.7 = (bf16[1024,128]{1,0:T(8,128)(2,1)S(1)}, bf16[1024,128]{1,0:T(8,128)(2,1)S(1)}, u32[]{:S(2)}, u32[]{:S(2)}) collective-permute-start(bf16[1024,128]{1,0:T(8,128)(2,1)S(1)} %collective-permute-done.5.refs_0_.refs_3_.refs_7_), channel_id=1, source_target_pairs={{0,1},{1,0},{2,3},{3,2},{4,5},{5,4},{6,7},{7,6},{8,9},{9,8},{10,11... | collective-permute-start | bytes 786440 | tf_op jit(solution)/shard_map/ppermute | solution.py:266
  21.6 12.5 %collective-permute-start.9 = (bf16[136,512]{1,0:T(8,128)(2,1)S(1)}, bf16[136,512]{1,0:T(8,128)(2,1)S(1)}, u32[]{:S(2)}, u32[]{:S(2)}) collective-permute-start(bf16[136,512]{1,0:T(8,128)(2,1)S(1)} %shard_map.60), channel_id=1, source_target_pairs={{0,4},{1,5},{2,6},{3,7},{4,0},{5,1},{6,2},{7,3},{8,12},{9,13},{10,... | collective-permute-start | bytes 417800 | tf_op jit(solution)/shard_map/ppermute | solution.py:266
  22.5 8.0 %collective-permute-start.8 = (bf16[512,128]{1,0:T(8,128)(2,1)S(1)}, bf16[512,128]{1,0:T(8,128)(2,1)S(1)}, u32[]{:S(2)}, u32[]{:S(2)}) collective-permute-start(bf16[512,128]{1,0:T(8,128)(2,1)S(1)} %collective-permute-done.4.refs_1_.q_ref), channel_id=1, source_target_pairs={{0,4},{1,5},{2,6},{3,7},{4,0},{5,1},{6,2},{7,3},{8,12},{9,13},{10,... | collective-permute-start | bytes 393224 | tf_op jit(solution)/shard_map/ppermute | solution.py:266
  33.3 7.0 %collective-permute-start.10 = (bf16[136,512]{1,0:T(8,128)(2,1)S(1)}, bf16[136,512]{1,0:T(8,128)(2,1)S(1)}, u32[]{:S(2)}, u32[]{:S(2)}) collective-permute-start(bf16[136,512]{1,0:T(8,128)(2,1)S(1)} %shard_map.61), channel_id=1, source_target_pairs={{0,4},{1,5},{2,6},{3,7},{4,0},{5,1},{6,2},{7,3},{8,12},{9,13},{10,... | collective-permute-start | bytes 417800 | tf_op jit(solution)/shard_map/ppermute | solution.py:266
  34.4 9.2 %collective-permute-start.11 = (bf16[136,512]{1,0:T(8,128)(2,1)S(1)}, bf16[136,512]{1,0:T(8,128)(2,1)S(1)}, u32[]{:S(2)}, u32[]{:S(2)}) collective-permute-start(bf16[136,512]{1,0:T(8,128)(2,1)S(1)} %shard_map.63), channel_id=1, source_target_pairs={{0,12},{1,13},{2,14},{3,15},{4,8},{5,9},{6,10},{7,11},{8,4},{9,5},... | collective-permute-start | bytes 417800 | tf_op jit(solution)/shard_map/ppermute | solution.py:266
